TPU v7x, 32 devices: a whole 2x2x4 slice. The times are simulated.
32 devices in a mesh: cols: 8 (over z, x), sec: 4 (over y, core).
Axes of the slice: x: 2, y: 2, z: 4, core: 2. Of those that a mesh axis runs over, the one named last changes fastest.
Arguments:
- trial: float32 [16, 16, 96, 512], P('cols', None, None, 'sec'), may hold values from -6 to 6
- orbitals: float32 [8, 16, 96, 512], P('cols', None, None, 'sec'), may hold values from -6 to 6
- potential: float32 [16, 96, 512], P(None, None, 'sec'), may hold values from -4 to 4
- owner: int32 [2], replicated, may hold values from 0 to 7
Outputs:
- response: float32 [16, 16, 96, 512], P('cols', None, None, 'sec')
All inputs are finite; a program needn't handle non-finite values.
Results may differ from a plain program's by a relative error of at most 0.00002.
Values sent between devices are 32-bit elements; how exact they have to be, the bound alone decides.
No kernel may reach another device: no remote copies, remote signals or barrier semaphores. Data moves between devices by JAX's collectives and lax.ppermute only.
A program may use at most 64 MiB of HBM per device.

v0:
```python
import jax
import jax.numpy as jnp
from jax import lax
from jax.sharding import PartitionSpec as P

ROUNDS = 2


grid_step = 0.5
spectrum_mid = 16.0
spectrum_half = 20.0
occupation = 2.0
weight_zero = 0.4
weight_one = -0.5
weight_two = 0.3
weight_three = -0.25


def broadcast(block, axis, holder):
    block = jnp.where(lax.axis_index(axis) == holder, block, jnp.zeros_like(block))
    return lax.psum(block, axis)


def with_halo(shard, sides, width):
    for axis, dim in sides:
        devices, length = (lax.axis_size(axis), shard.shape[dim])
        up = [(i, (i + 1) % devices) for i in range(devices)]
        down = [(j, i) for i, j in up]
        last = lax.slice_in_dim(shard, length - width, length, axis=dim)
        leading = lax.slice_in_dim(shard, 0, width, axis=dim)
        before = lax.ppermute(last, axis, up)
        after = lax.ppermute(leading, axis, down)
        shard = jnp.concatenate([before, shard, after], axis=dim)
    return shard


def apply_scaled(extended, potential):
    center = extended[..., 2:-2]
    diag_coef = -30.0 / 12.0
    near_coef = 16.0 / 12.0
    far_coef = -1.0 / 12.0
    along_x = (
        diag_coef * center
        + near_coef * (extended[..., 3:-1] + extended[..., 1:-3])
        + far_coef * (extended[..., 4:] + extended[..., :-4])
    )
    leading = center.ndim - 3
    padded = jnp.pad(center, [(0, 0)] * leading + [(2, 2), (2, 2), (0, 0)])
    along_y = (
        diag_coef * center
        + near_coef * (padded[..., 3:-1, 2:-2, :] + padded[..., 1:-3, 2:-2, :])
        + far_coef * (padded[..., 4:, 2:-2, :] + padded[..., :-4, 2:-2, :])
    )
    along_z = (
        diag_coef * center
        + near_coef * (padded[..., 2:-2, 3:-1, :] + padded[..., 2:-2, 1:-3, :])
        + far_coef * (padded[..., 2:-2, 4:, :] + padded[..., 2:-2, :-4, :])
    )
    kinetic = -0.5 * (along_x + along_y + along_z) / (grid_step * grid_step)
    return (kinetic + potential * center - spectrum_mid * center) / spectrum_half


def fetch_orbital(orbitals, root):
    local = orbitals[0]
    return broadcast(local, "cols", root)


def body(trial, orbitals, potential, owner):
    total = jnp.zeros_like(trial)
    wide_potential = with_halo(potential, (("sec", 2),), 6)
    for turn in range(ROUNDS):
        orbital = fetch_orbital(orbitals, owner[turn])
        first = orbital[None] * trial
        first_wide = with_halo(first, (("sec", 3),), 6)
        second_wide = apply_scaled(first_wide, wide_potential[..., 2:-2])
        third_wide = (
            2.0 * apply_scaled(second_wide, wide_potential[..., 4:-4]) - first_wide[..., 4:-4]
        )
        fourth = 2.0 * apply_scaled(third_wide, wide_potential[..., 6:-6]) - second_wide[..., 4:-4]
        filtered = (
            weight_zero * first_wide[..., 6:-6]
            + weight_one * second_wide[..., 4:-4]
            + weight_two * third_wide[..., 2:-2]
            + weight_three * fourth
        )
        total = total + occupation * orbital[None] * filtered
    return total


def solution(mesh):
    placed = (P("cols", None, None, "sec"), P("cols", None, None, "sec"), P(None, None, "sec"), P())
    return jax.shard_map(
        body, mesh=mesh, in_specs=placed, out_specs=P("cols", None, None, "sec"), check_vma=False
    )
```

profile of v0, /device:TPU:0, one launch (start us, length us, event | category | flops | bytes accessed | tf_op | source)
XLA Modules:
  0.0 193.6 jit_solution(1553654587848540653)
XLA Ops:
  6.5 0.0 all-reduce.9.cloned.1.call-start
  6.5 1.3 fusion.146
  9.2 2.5 %select_bitcast_fusion = (f32[16,96,128]{2,1,0:T(8,128)}, f32[16,96,128]{2,1,0:T(8,128)}) fusion(f32[1,16,96,128]{3,2,1,0:T(8,128)} %param.5, pred[]{:T(512)S(6)} %eq.7, pred[]{:T(512)S(6)} %eq.6), kind=kLoop, calls=%fused_computation.208 | loop fusion | flops 393216 | bytes 2359298 | tf_op jit(solution)/shard_map/jit(_where)/select_n | solution.py:20
  11.7 0.0 all-reduce.9.cloned.1.call-update
  11.7 0.0 copy-done.16
  11.7 0.5 copy.8
  12.2 0.5 collective-permute-start.2
  12.7 2.0 %collective-permute-start.3 = (f32[16,96,6]{1,0,2:T(8,128)S(1)}, f32[16,96,6]{1,0,2:T(8,128)S(1)}, u32[]{:S(2)}, u32[]{:S(2)}) collective-permute-start(f32[16,96,6]{1,0,2:T(8,128)S(1)} %get-tuple-element.18), channel_id=1, source_target_pairs={{1,0},{2,1},{3,2},{0,3},{5,4},{6,5},{7,6},{4,7},{9,8},{10,9},{11,1... | collective-permute-start | bytes 110600 | tf_op jit(solution)/shard_map/ppermute | solution.py:32
  14.8 2.1 %copy.7 = f32[2,16,96,128]{2,1,3,0:T(8,128)S(1)} copy(f32[2,16,96,128]{3,2,1,0:T(8,128)} %param.4) | data formatting | bytes 3145728 | tf_op args[0]
  16.9 0.0 collective-permute-done.2
  16.9 1.2 copy.10
  18.1 0.0 collective-permute-done.3
  18.1 1.2 copy.11
  19.3 2.5 %pad_maximum_fusion.2 = f32[16,96,140]{2,1,0:T(8,128)S(1)} fusion(f32[16,96,6]{2,1,0:T(8,128)} %copy.11, f32[16,96,128]{2,1,0:T(8,128)} %param.6, f32[16,96,6]{2,1,0:T(8,128)} %copy.10), kind=kLoop, calls=%fused_computation.205 | loop fusion | flops 430080 | bytes 1720320 | tf_op jit(solution)/shard_map/concatenate | solution.py:33
  21.8 1.6 slice.383
  23.4 1.7 slice.390
  25.1 3.1 %copy.12 = f32[16,96,136]{1,0,2:T(8,128)} copy(f32[16,96,136]{2,1,0:T(8,128)} %slice.383) | data formatting | bytes 1671168 | tf_op jit(solution)/shard_map/slice | solution.py:75
  28.2 3.1 %copy.13 = f32[16,96,132]{1,0,2:T(8,128)} copy(f32[16,96,132]{2,1,0:T(8,128)} %slice.390) | data formatting | bytes 1622016 | tf_op jit(solution)/shard_map/slice | solution.py:77
  31.3 72.6 %all-reduce.9.cloned.1.call-done = (f32[16,96,128]{2,1,0:T(8,128)}, f32[16,96,128]{2,1,0:T(8,128)}) async-done(((f32[16,96,128]{2,1,0:T(8,128)}, f32[16,96,128]{2,1,0:T(8,128)}), (f32[16,96,128]{2,1,0:T(8,128)}, f32[16,96,128]{2,1,0:T(8,128)})) %all-reduce.9.cloned.1.call-update) | async-done | bytes 1572880 | tf_op jit(solution)/shard_map/psum | solution.py:21
  103.9 2.5 %copy.16 = f32[16,96,128]{1,0,2:T(8,128)} copy(f32[16,96,128]{2,1,0:T(8,128)} %get-tuple-element.6) | data formatting | bytes 1572864 | tf_op jit(solution)/shard_map/psum | solution.py:21
  106.4 2.5 %copy.6 = f32[16,96,128]{1,0,2:T(8,128)} copy(f32[16,96,128]{2,1,0:T(8,128)} %get-tuple-element.5) | data formatting | bytes 1572864 | tf_op jit(solution)/shard_map/psum | solution.py:21
  108.9 2.8 %broadcast_multiply_fusion.2 = (f32[16,96,128]{2,1,0:T(8,128)}, f32[16,96,128]{2,1,0:T(8,128)}) fusion(f32[16,96,128]{2,1,0:T(8,128)} %get-tuple-element.6, f32[16,96,128]{2,1,0:T(8,128)} %get-tuple-element.5), kind=kLoop, calls=%fused_computation.210 | loop fusion | flops 393216 | bytes 3145728 | tf_op jit(solution)/shard_map/mul | solution.py:86
  111.7 0.0 copy-done.13
  111.7 0.0 copy-done.14
  111.7 0.4 broadcast_multiply_fusion
  112.1 0.0 copy-start.9
  112.1 0.0 copy-start.11
  112.1 0.0 copy-start.15
  112.1 0.1 collective-permute-start
  112.2 1.7 collective-permute-start.1
  114.0 0.1 copy-done.11
  114.0 0.0 collective-permute-start.4
  114.0 1.7 collective-permute-start.5
  115.8 2.5 %copy.15 = f32[16,96,128]{1,0,2:T(8,128)} copy(f32[16,96,128]{2,1,0:T(8,128)} %get-tuple-element.23) | data formatting | bytes 1572864 | tf_op jit(solution)/shard_map/mul | solution.py:86
  118.3 1.4 copy.5
  119.7 0.0 collective-permute-done
  119.7 0.6 copy-done.17
  120.3 0.0 collective-permute-done.1
  120.3 1.8 pad_maximum_fusion
  122.2 1.4 copy-done
  123.5 0.0 collective-permute-done.4
  123.5 0.0 collective-permute-done.5
  123.5 1.0 copy-done.10
  124.6 1.2 pad_maximum_fusion.1
  125.8 0.0 slice-start
  125.9 0.1 slice.399
  126.0 1.2 copy-done.3
  127.3 1.2 slice-done
  128.4 0.3 copy-done.12
  128.7 6.5 %fusion.27 = (f32[2,16,96,136]{2,1,3,0:T(8,128)S(1)}, f32[2,16,96,136]{2,1,3,0:T(8,128)S(1)}) fusion(f32[2,16,96,136]{2,1,3,0:T(8,128)S(1)} %slice.399, f32[2,16,96,140]{2,1,3,0:T(8,128)S(1)} %pad_maximum_fusion.1, f32[16,96,136]{1,0,2:T(8,128)S(1)} %copy-done.12, f32[2,16,96,136]{2,1,3,0:T(8,128)S(1)} %slice-done, f32[2,16,96,140]{2,1,3,0:T(8,128)S(1)} %copy-done.1), kind=kLoop, calls=%fused_computation.77 | loop fusion | flops 22560768 | bytes 20889600 | tf_op jit(solution)/shard_map/div | solution.py:60
  135.2 0.0 copy-start.6
  135.2 0.0 copy-start.4
  135.2 1.8 slice.385
  137.0 0.3 copy-done.6
  137.3 0.6 copy-done.4
  138.0 1.5 slice.405
  139.4 0.9 copy-done.2
  140.4 25.0 %fusion.73 = (f32[2,16,96,132]{2,1,3,0:T(8,128)}, f32[2,16,96,132]{2,1,3,0:T(8,128)}) fusion(f32[2,16,96,132]{2,1,3,0:T(8,128)} %slice.405, f32[2,16,96,140]{2,1,3,0:T(8,128)} %copy-done.3, f32[2,16,96,136]{2,1,3,0:T(8,128)} %copy-done.4, f32[16,96,132]{1,0,2:T(8,128)} %copy.13, f32[2,16,96,140]{2,1,3,0:T(8,128)S(1)} %copy-done.2, ...), kind=kLoop, calls=%fused_computation.127 | loop fusion | flops 22708224 | bytes 23519232 | tf_op jit(solution)/shard_map/sub | solution.py:77
  165.4 1.9 slice.392
  167.3 0.3 copy-done.8
  167.6 1.5 slice.411
  169.1 0.6 copy-done.5
  169.7 15.2 %fusion.104 = f32[2,16,96,128]{2,1,3,0:T(8,128)S(1)} fusion(f32[2,16,96,128]{2,1,3,0:T(8,128)S(1)} %slice.392, f32[2,16,96,128]{2,1,3,0:T(8,128)} %slice.411, f32[2,16,96,132]{2,1,3,0:T(8,128)S(1)} %copy-done.8, f32[2,16,96,132]{2,1,3,0:T(8,128)} %get-tuple-element.16, f32[2,16,96,136]{2,1,3,0:T(8,128)S(1)} %copy-done.5, f32[2,16,96,128]{2,1,3,0:T(8,128)} %copy-done.9, ...), kind=kLoop, calls=%fused_computation.162 | loop fusion | flops 28704768 | bytes 25952256 | tf_op jit(solution)/shard_map/add | solution.py:86
  184.9 1.8 copy.18
  (20 shorter events, 0.1 us)
Async XLA Ops:
  6.5 5.1 %copy-start.16 = (f32[16,96,128]{2,1,0:T(8,128)S(1)}, f32[16,96,128]{2,1,0:T(8,128)}, u32[]{:S(2)}) copy-start(f32[16,96,128]{2,1,0:T(8,128)} %param.6) | copy-start | bytes 2359300
  6.5 97.4 %all-reduce.9.cloned.1.call-start = ((), (), s32[]{:S(2)}) async-start(), calls=%async_computation | async-start | bytes 3145728 | tf_op jit(solution)/shard_map/psum | solution.py:21
  12.2 4.7 %collective-permute-start.2 = (f32[16,96,6]{1,0,2:T(8,128)S(1)}, f32[16,96,6]{1,0,2:T(8,128)S(1)}, u32[]{:S(2)}, u32[]{:S(2)}) collective-permute-start(f32[16,96,6]{1,0,2:T(8,128)S(1)} %get-tuple-element.17), channel_id=1, source_target_pairs={{0,1},{1,2},{2,3},{3,0},{4,5},{5,6},{6,7},{7,4},{8,9},{9,10},{10,1... | collective-permute-start | bytes 110600 | tf_op jit(solution)/shard_map/ppermute | solution.py:31
  12.7 5.4 %collective-permute-start.3 = (f32[16,96,6]{1,0,2:T(8,128)S(1)}, f32[16,96,6]{1,0,2:T(8,128)S(1)}, u32[]{:S(2)}, u32[]{:S(2)}) collective-permute-start(f32[16,96,6]{1,0,2:T(8,128)S(1)} %get-tuple-element.18), channel_id=1, source_target_pairs={{1,0},{2,1},{3,2},{0,3},{5,4},{6,5},{7,6},{4,7},{9,8},{10,9},{11,1... | collective-permute-start | bytes 110600 | tf_op jit(solution)/shard_map/ppermute | solution.py:32
  108.9 2.8 %copy-start.13 = (f32[16,96,128]{1,0,2:T(8,128)S(1)}, f32[16,96,128]{1,0,2:T(8,128)}, u32[]{:S(2)}) copy-start(f32[16,96,128]{1,0,2:T(8,128)} %copy.16) | copy-start | bytes 2359300
  108.9 2.8 %copy-start.14 = (f32[16,96,128]{1,0,2:T(8,128)S(1)}, f32[16,96,128]{1,0,2:T(8,128)}, u32[]{:S(2)}) copy-start(f32[16,96,128]{1,0,2:T(8,128)} %copy.6) | copy-start | bytes 2359300
  112.1 1.9 copy-start.9
  112.1 1.9 copy-start.11
  112.1 6.2 %copy-start.15 = (f32[16,96,128]{2,1,0:T(8,128)S(1)}, f32[16,96,128]{2,1,0:T(8,128)}, u32[]{:S(2)}) copy-start(f32[16,96,128]{2,1,0:T(8,128)} %get-tuple-element.24) | copy-start | bytes 2359300
  112.1 7.5 %collective-permute-start = (f32[2,16,96,6]{2,1,3,0:T(8,128)S(1)}, f32[2,16,96,6]{2,1,3,0:T(8,128)S(1)}, u32[]{:S(2)}, u32[]{:S(2)}) collective-permute-start(f32[2,16,96,6]{2,1,3,0:T(8,128)S(1)} %get-tuple-element.11), channel_id=1, source_target_pairs={{0,1},{1,2},{2,3},{3,0},{4,5},{5,6},{6,7},{7,4},{8,9},{9,10},{10,1... | collective-permute-start | bytes 221192 | tf_op jit(solution)/shard_map/ppermute | solution.py:31
  112.2 8.1 %collective-permute-start.1 = (f32[2,16,96,6]{2,1,3,0:T(8,128)S(1)}, f32[2,16,96,6]{2,1,3,0:T(8,128)}, u32[]{:S(2)}, u32[]{:S(2)}) collective-permute-start(f32[2,16,96,6]{2,1,3,0:T(8,128)S(1)} %get-tuple-element.12), channel_id=1, source_target_pairs={{1,0},{2,1},{3,2},{0,3},{5,4},{6,5},{7,6},{4,7},{9,8},{10,9},{11,1... | collective-permute-start | bytes 221192 | tf_op jit(solution)/shard_map/ppermute | solution.py:32
  114.0 9.5 %collective-permute-start.4 = (f32[2,16,96,6]{2,1,3,0:T(8,128)S(1)}, f32[2,16,96,6]{2,1,3,0:T(8,128)}, u32[]{:S(2)}, u32[]{:S(2)}) collective-permute-start(f32[2,16,96,6]{2,1,3,0:T(8,128)S(1)} %get-tuple-element.7), channel_id=1, source_target_pairs={{0,1},{1,2},{2,3},{3,0},{4,5},{5,6},{6,7},{7,4},{8,9},{9,10},{10,1... | collective-permute-start | bytes 221192 | tf_op jit(solution)/shard_map/ppermute | solution.py:31
  114.0 9.5 %collective-permute-start.5 = (f32[2,16,96,6]{2,1,3,0:T(8,128)S(1)}, f32[2,16,96,6]{2,1,3,0:T(8,128)}, u32[]{:S(2)}, u32[]{:S(2)}) collective-permute-start(f32[2,16,96,6]{2,1,3,0:T(8,128)S(1)} %get-tuple-element.8), channel_id=1, source_target_pairs={{1,0},{2,1},{3,2},{0,3},{5,4},{6,5},{7,6},{4,7},{9,8},{10,9},{11,1... | collective-permute-start | bytes 221192 | tf_op jit(solution)/shard_map/ppermute | solution.py:32
  119.7 0.6 copy-start.17
  122.1 1.4 copy-start
  122.2 2.4 %copy-start.10 = (f32[2,16,96,128]{2,1,3,0:T(8,128)S(1)}, f32[2,16,96,128]{2,1,3,0:T(8,128)}, u32[]{:S(2)}) copy-start(f32[2,16,96,128]{2,1,3,0:T(8,128)} %copy-done.9) | copy-start | bytes 4718596
  124.6 2.7 %copy-start.1 = (f32[2,16,96,140]{2,1,3,0:T(8,128)S(1)}, f32[2,16,96,140]{2,1,3,0:T(8,128)}, u32[]{:S(2)}) copy-start(f32[2,16,96,140]{2,1,3,0:T(8,128)} %copy-done) | copy-start | bytes 5160964
  125.8 1.4 copy-start.3
  125.8 2.6 %slice-start = ((f32[2,16,96,140]{2,1,3,0:T(8,128)}), f32[2,16,96,136]{2,1,3,0:T(8,128)S(1)}, s32[]{:S(2)}) async-start(f32[2,16,96,140]{2,1,3,0:T(8,128)} %copy-done), calls=%async_computation.1 | async-start | bytes 4456448 | tf_op jit(solution)/shard_map/slice | solution.py:38
  125.8 2.9 %copy-start.12 = (f32[16,96,136]{1,0,2:T(8,128)S(1)}, f32[16,96,136]{1,0,2:T(8,128)}, u32[]{:S(2)}) copy-start(f32[16,96,136]{1,0,2:T(8,128)} %copy.12) | copy-start | bytes 2506756
  135.2 2.1 %copy-start.6 = (f32[2,16,96,136]{2,1,3,0:T(8,128)}, f32[2,16,96,136]{2,1,3,0:T(8,128)S(1)}, u32[]{:S(2)}) copy-start(f32[2,16,96,136]{2,1,3,0:T(8,128)S(1)} %get-tuple-element.14) | copy-start | bytes 5013508
  135.2 2.7 %copy-start.4 = (f32[2,16,96,136]{2,1,3,0:T(8,128)}, f32[2,16,96,136]{2,1,3,0:T(8,128)S(1)}, u32[]{:S(2)}) copy-start(f32[2,16,96,136]{2,1,3,0:T(8,128)S(1)} %get-tuple-element.13) | copy-start | bytes 5013508
  138.0 2.4 %copy-start.2 = (f32[2,16,96,140]{2,1,3,0:T(8,128)S(1)}, f32[2,16,96,140]{2,1,3,0:T(8,128)}, u32[]{:S(2)}) copy-start(f32[2,16,96,140]{2,1,3,0:T(8,128)} %copy-done) | copy-start | bytes 5160964
  165.4 2.2 %copy-start.8 = (f32[2,16,96,132]{2,1,3,0:T(8,128)S(1)}, f32[2,16,96,132]{2,1,3,0:T(8,128)}, u32[]{:S(2)}) copy-start(f32[2,16,96,132]{2,1,3,0:T(8,128)} %get-tuple-element.15) | copy-start | bytes 4866052
  165.4 3.7 %copy-start.7 = (f32[2,16,96,136]{2,1,3,0:T(8,128)S(1)}, f32[2,16,96,136]{2,1,3,0:T(8,128)}, u32[]{:S(2)}) copy-start(f32[2,16,96,136]{2,1,3,0:T(8,128)} %copy-done.6) | copy-start | bytes 5013508
  167.3 2.4 %copy-start.5 = (f32[2,16,96,136]{2,1,3,0:T(8,128)S(1)}, f32[2,16,96,136]{2,1,3,0:T(8,128)}, u32[]{:S(2)}) copy-start(f32[2,16,96,136]{2,1,3,0:T(8,128)} %copy-done.4) | copy-start | bytes 5013508
Sparse Core Ops, SparseCore 0:
  11.8 92.0 all-reduce.8
where the time goes:
time: 194 us
  waiting for transfers between devices  72.7 us (37%)
  other arithmetic  57.8 us (30%)
  local copies, waits for them, and re-layouts  42 us (22%)
  between operations  15 us (8%)
  starting transfers between devices  6.09 us (3%)
    psum x1, waiting for transfers between devices, broadcast(): return lax.psum(block, axis)  72.6 us
    sub x1, other arithmetic, body(): 2.0 * apply_scaled(second_wide, wide_potential[..., 4:-4])  25 us
    add x1, other arithmetic, body(): total = total + occupation * orbital[None] * filtered  15.2 us
    unnamed x38, local copies, waits for them, and re-layouts  10.1 us
    div x1, other arithmetic, apply_scaled(): (kinetic + potential * center - spectrum_mid * center) / spectrum_half  6.51 us
    concatenate x3, other arithmetic, with_halo(): shard = jnp.concatenate([before, shard, after], axis=dim)  5.53 us
    ppermute x3, starting transfers between devices, with_halo(): after = lax.ppermute(leading, axis, down)  5.48 us
    psum x2, local copies, waits for them, and re-layouts, broadcast(): return lax.psum(block, axis)  5 us
  transfers between devices with their start and end apart: 7, of which 1 were waited for; matrix products, arithmetic and copies ran while one was open for 12% of the time, Pallas kernels for 0%

commit v1 on v0

v1 whole, which is shorter than its diff:
```python
import functools

import jax
import jax.numpy as jnp
from jax import lax
from jax.experimental import pallas as pl
from jax.experimental.pallas import tpu as pltpu
from jax.sharding import PartitionSpec as P

SCALE = 120.0
ALPHA = 0.6 * SCALE
BETA = 0.25 * SCALE**2
GAMMA = 0.1 * SCALE**3
FINAL = -2.0 / SCALE**3
HALO = 6
ZP = 8
CHUNK = 32


def lanes(rows):
    return lax.broadcasted_iota(jnp.int32, (rows, 128), 1)


def between(lane, low, high):
    return (lane >= low) & (lane < high)


def pack_edges(plane, ny, lane, first):
    tile = jnp.zeros_like(plane(0))
    for y in range(ny):
        source = 0 if first else 128 - HALO
        moved = pltpu.roll(plane(y), (8 * y - source) % 128, 1)
        tile = jnp.where(between(lane, 8 * y, 8 * y + HALO), moved, tile)
    return tile


def halo_plane(left, right, low, high, lane, y):
    inner = lane % 64
    tile = jnp.where(inner < 6, pltpu.roll(left, (-8 * y) % 128, 1), 0.0)
    tile = jnp.where(between(inner, 22, 28), pltpu.roll(right, (22 - 8 * y) % 128, 1), tile)
    tile = jnp.where(between(lane, 6, 12), pltpu.roll(low, 6, 1), tile)
    tile = jnp.where(between(lane, 16, 22), pltpu.roll(low, 22, 1), tile)
    tile = jnp.where(between(lane, 70, 76), pltpu.roll(high, 70, 1), tile)
    tile = jnp.where(between(lane, 80, 86), pltpu.roll(high, 86, 1), tile)
    return tile


def pack_kernel(trial, potential, last, first):
    columns, ny, nz, _ = trial.shape
    lane = lanes(nz)
    for out, leading in ((last, False), (first, True)):
        for c in range(columns):
            out[c] = pack_edges(lambda y: trial[c, y], ny, lane, leading)
        out[columns] = pack_edges(lambda y: potential[y], ny, lane, leading)


def prepare_kernel(trial, potential, left, right, trial_halo, scaled, scaled_halo):
    columns, ny, nz, _ = trial.shape
    lane = lanes(nz)
    half = ny // 2
    for y in range(half):
        tile = jnp.zeros((nz, 128), jnp.float32)
        for c in range(columns):
            part = halo_plane(left[c], right[c], trial[c, y], trial[c, y + half], lane, y)
            tile = tile + (pltpu.roll(part, 32 * c, 1) if c else part)
        trial_halo[y] = tile
        part = halo_plane(left[columns], right[columns], potential[y], potential[y + half], lane, y)
        scaled_halo[y] = 6.0 * (part + pltpu.roll(part, 32, 1)) - 8.0
    for y in range(ny):
        scaled[y] = 6.0 * potential[y] - 8.0


def gather_kernel(count, rows, where, *refs):
    blocks, (whole, last, first) = refs[:count], refs[count:]
    nz = last.shape[0]
    ny = whole.shape[0] // nz
    for k in range(count):
        whole[pl.ds(pl.multiple_of(where[k] * rows, 8), rows), :] = blocks[k][...]
    lane = lanes(nz)
    last[...] = pack_edges(lambda y: whole[y * nz : (y + 1) * nz], ny, lane, False)
    first[...] = pack_edges(lambda y: whole[y * nz : (y + 1) * nz], ny, lane, True)


def clear_borders(ref, ny, nz):
    for c in range(ref.shape[0]):
        for y in (0, 1, ny + 2, ny + 3):
            ref[c, y] = jnp.zeros_like(ref[c, y])

        @pl.loop(2, ny + 2)
        def _(y):
            ref[c, y, 0:ZP] = jnp.zeros((ZP, 128), jnp.float32)
            ref[c, y, ZP + nz : 2 * ZP + nz] = jnp.zeros((ZP, 128), jnp.float32)


def neighbours(ref, c, y, at, rows):
    near = (ref[c, y - 1, pl.ds(at, rows)] + ref[c, y + 1, pl.ds(at, rows)]) + (
        ref[c, y, pl.ds(at - 1, rows)] + ref[c, y, pl.ds(at + 1, rows)]
    )
    far = (ref[c, y - 2, pl.ds(at, rows)] + ref[c, y + 2, pl.ds(at, rows)]) + (
        ref[c, y, pl.ds(at - 2, rows)] + ref[c, y, pl.ds(at + 2, rows)]
    )
    return near, far


def wrap_halo(ref, half, nz, lane):
    inside = pl.ds(ZP, nz)
    for k in range(2):
        ref[0, half + 2 + k, inside] = jnp.where(lane < 64, pltpu.roll(ref[0, 2 + k, inside], 64, 1), 0.0)
        ref[0, k, inside] = jnp.where(lane >= 64, pltpu.roll(ref[0, half + k, inside], 64, 1), 0.0)


def round_kernel(adds, psi, left, right, trial, trial_halo, scaled, scaled_halo, *refs):
    if adds:
        total, out, w, u, v, ends, w_halo, u_halo, v_halo = refs
    else:
        out, w, u, v, ends, w_halo, u_halo, v_halo = refs
    columns, ny, nz, _ = trial.shape
    half = ny // 2
    full = lanes(nz)
    lane = lanes(CHUNK)
    for ref in (w, u, v):
        clear_borders(ref, ny, nz)
    for ref in (w_halo, u_halo, v_halo):
        clear_borders(ref, half, nz)

    for y in range(half):
        part = halo_plane(left[...], right[...], psi[y], psi[y + half], full, y)
        w_halo[0, y + 2, pl.ds(ZP, nz)] = (part + pltpu.roll(part, 32, 1)) * trial_halo[y]
    wrap_halo(w_halo, half, nz, full)

    @pl.loop(0, ny)
    def _(y):
        for c in range(columns):
            w[c, y + 2, pl.ds(ZP, nz)] = psi[y] * trial[c, y]

    def along(f):
        pair = f + pltpu.roll(f, 2, 1)
        return pltpu.roll(pair, 127, 1), pair + pltpu.roll(pair, 126, 1)

    def halo_stage(source, target, shift, weight):
        @pl.loop(0, half)
        def _(y):
            for z in range(0, nz, CHUNK):
                at = ZP + z
                f = source[0, y + 2, pl.ds(at, CHUNK)]
                near, far = neighbours(source, 0, y + 2, at, CHUNK)
                one, two = along(f)
                value = (far + two) - 16.0 * (near + one) + (scaled_halo[y, pl.ds(z, CHUNK)] - shift) * f
                if weight:
                    value = value - weight * w_halo[0, y + 2, pl.ds(at, CHUNK)]
                target[0, y + 2, pl.ds(at, CHUNK)] = value

        wrap_halo(target, half, nz, full)

    def mend(source):
        inner = lane % 32

        @pl.loop(0, half)
        def _(y):
            for z in range(0, nz, CHUNK):
                f = source[0, y + 2, pl.ds(ZP + z, CHUNK)]
                gap = f - pltpu.roll(f, 112, 1)
                gap = jnp.where(between(inner, 4, 6), gap, jnp.where(between(inner, 6, 8), -gap, 0.0))
                far = jnp.where(inner < 6, pltpu.roll(gap, 126, 1), pltpu.roll(gap, 2, 1))
                near = jnp.where(inner == 5, pltpu.roll(gap, 127, 1), pltpu.roll(gap, 1, 1))
                both = far - jnp.where(between(inner, 5, 7), 16.0 * near, 0.0)
                for h in range(2):
                    for c in range(columns):
                        moved = pltpu.roll(both, (122 - 64 * h - 32 * c) % 128, 1)
                        ends[c, y + h * half, pl.ds(z, CHUNK)] = jnp.where((lane < 2) | (lane >= 126), moved, 0.0)

    def stage(source, shift, weight, store):
        @pl.loop(0, ny)
        def _(y):
            for z in range(0, nz, CHUNK):
                at = ZP + z
                diagonal = scaled[y, pl.ds(z, CHUNK)] - shift if shift else scaled[y, pl.ds(z, CHUNK)]
                for c in range(columns):
                    f = source[c, y + 2, pl.ds(at, CHUNK)]
                    near, far = neighbours(source, c, y + 2, at, CHUNK)
                    one, two = along(f)
                    value = (far + two) - 16.0 * (near + one) + diagonal * f + ends[c, y, pl.ds(z, CHUNK)]
                    if weight:
                        value = value - weight * w[c, y + 2, pl.ds(at, CHUNK)]
                    store(c, y, z, value)

    def into(target):
        def store(c, y, z, value):
            target[c, y + 2, pl.ds(ZP + z, CHUNK)] = value

        return store

    def finish(c, y, z, value):
        term = (FINAL * psi[y, pl.ds(z, CHUNK)]) * value
        if adds:
            term = term + total[c, y, pl.ds(z, CHUNK)]
        out[c, y, pl.ds(z, CHUNK)] = term

    halo_stage(w_halo, u_halo, ALPHA, None)
    halo_stage(u_halo, v_halo, 0.0, BETA)
    mend(w_halo)
    stage(w, ALPHA, None, into(u))
    mend(u_halo)
    stage(u, 0.0, BETA, into(v))
    mend(v_halo)
    stage(v, 0.0, GAMMA, finish)


def vmem(count):
    return [pl.BlockSpec(memory_space=pltpu.VMEM)] * count


def params(mib):
    return pltpu.CompilerParams(vmem_limit_bytes=mib << 20)


def f32(*shape):
    return jax.ShapeDtypeStruct(shape, jnp.float32)


def ring_of(n):
    return [*range(0, n, 2), *range(n - 1 - n % 2, 0, -2)]


def body(trial, orbitals, potential, owner):
    columns, ny, nz, nx = trial.shape
    n, parts = lax.axis_size("cols"), lax.axis_size("sec")
    rounds = owner.shape[0]
    rows = ny * nz // n
    sec_up = [(i, (i + 1) % parts) for i in range(parts)]
    sec_down = [(j, i) for i, j in sec_up]

    last, first = pl.pallas_call(
        pack_kernel,
        out_shape=[f32(columns + 1, nz, nx)] * 2,
        in_specs=vmem(2),
        out_specs=vmem(2),
        compiler_params=params(8),
        name="pack",
    )(trial, potential)
    left = lax.ppermute(last, "sec", sec_up)
    right = lax.ppermute(first, "sec", sec_down)

    mine = lax.all_to_all(orbitals.reshape(n, rows, nx), "cols", 0, 0)
    ring = ring_of(n)
    order = jnp.array(ring, jnp.int32)
    spot = jnp.array([ring.index(i) for i in range(n)], jnp.int32)[lax.axis_index("cols")]
    clockwise = [(ring[i], ring[(i + 1) % n]) for i in range(n)]
    counter = [(j, i) for i, j in clockwise]

    own = [lax.dynamic_index_in_dim(mine, owner[r], 0, False) for r in range(rounds)]
    ahead, behind = list(own), list(own)
    blocks = [[own[r]] for r in range(rounds)]
    places = [spot]
    for step in range(1, n // 2 + 1):
        for r in range(rounds):
            ahead[r] = lax.ppermute(ahead[r], "cols", clockwise)
            blocks[r].append(ahead[r])
            if 2 * step < n:
                behind[r] = lax.ppermute(behind[r], "cols", counter)
                blocks[r].append(behind[r])
        places.append((spot - step) % n)
        if 2 * step < n:
            places.append((spot + step) % n)
    where = order[jnp.stack(places)]

    trial_halo, scaled, scaled_halo = pl.pallas_call(
        prepare_kernel,
        out_shape=[f32(ny // 2, nz, nx), f32(ny, nz, nx), f32(ny // 2, nz, nx)],
        in_specs=vmem(4),
        out_specs=vmem(3),
        compiler_params=params(10),
        name="prepare",
    )(trial, potential, left, right)

    total = None
    sections = []
    for r in range(rounds):
        psi, psi_last, psi_first = pl.pallas_call(
            functools.partial(gather_kernel, n, rows),
            out_shape=[f32(ny * nz, nx), f32(nz, nx), f32(nz, nx)],
            in_specs=[pl.BlockSpec(memory_space=pltpu.SMEM)] + vmem(n),
            out_specs=vmem(3),
            compiler_params=params(6),
            name="gather",
        )(where, *blocks[r])
        psi_left = lax.ppermute(psi_last, "sec", sec_up)
        psi_right = lax.ppermute(psi_first, "sec", sec_down)
        sections.append((psi.reshape(ny, nz, nx), psi_left, psi_right))
    for r in range(rounds):
        given = [*sections[r], trial, trial_halo, scaled, scaled_halo] + ([total] if r else [])
        planes = [pltpu.VMEM((columns, ny + 4, nz + 2 * ZP, nx), jnp.float32)] * 3
        planes.append(pltpu.VMEM((columns, ny, nz, nx), jnp.float32))
        halos = [pltpu.VMEM((1, ny // 2 + 4, nz + 2 * ZP, nx), jnp.float32)] * 3
        total = pl.pallas_call(
            functools.partial(round_kernel, r > 0),
            out_shape=f32(columns, ny, nz, nx),
            in_specs=vmem(len(given)),
            out_specs=pl.BlockSpec(memory_space=pltpu.VMEM),
            scratch_shapes=planes + halos,
            compiler_params=params(24),
            name="round",
        )(*given)
    return total


def solution(mesh):
    placed = (P("cols", None, None, "sec"), P("cols", None, None, "sec"), P(None, None, "sec"), P())
    return jax.shard_map(
        body, mesh=mesh, in_specs=placed, out_specs=P("cols", None, None, "sec"), check_vma=False
    )
```

time: 194 us -> 116 us (0.60)
  other arithmetic: 57.8 us -> 0.01 us
  Pallas kernels: 0 us -> 52.1 us
  waiting for transfers between devices: 72.7 us -> 22.5 us
  local copies, waits for them, and re-layouts: 42 us -> 6.06 us
  starting transfers between devices: 6.09 us -> 26.1 us
  between operations: 15 us -> 8.92 us
    psum x1 -> x0, waiting for transfers between devices: 72.6 us -> none  [broadcast(): return lax.psum(block, axis)]
    pallas_call x0 -> x6, Pallas kernels: none -> 52.1 us  [the longest x2 44.3 us: body(): pl.pallas_call(functools.partial(round_kernel, r > 0), out_shape=f32(colu...]
    sub x1 -> x0, other arithmetic: 25 us -> none  [body(): 2.0 * apply_scaled(second_wide, wide_potential[..., 4:-4])]
    slice x15 -> x1, local copies, waits for them, and re-layouts: 18.8 us -> 0.65 us  [body(): owner[r]]
    all_to_all x0 -> x1, waiting for transfers between devices: none -> 15.5 us  [body(): mine = lax.all_to_all(orbitals.reshape(n, rows, nx), 'cols', 0, 0)]
    add x1 -> x0, other arithmetic: 15.2 us -> none  [body(): total = total + occupation * orbital[None] * filtered]
    ppermute x6 -> x20, starting transfers between devices: 6.09 us -> 18.7 us  [the longest x6 8.12 us: body(): behind[r] = lax.ppermute(behind[r], 'cols', counter)]
    all_to_all x0 -> x1, starting transfers between devices: none -> 7.41 us  [body(): mine = lax.all_to_all(orbitals.reshape(n, rows, nx), 'cols', 0, 0)]
  transfers between devices with their start and end apart: 7 -> 21, of which waited for: 1 -> 7; matrix products, arithmetic and copies ran while one was open for 12% -> 2% of each run, Pallas kernels for 0% -> 25%
where the time goes in v1:
time: 116 us
  Pallas kernels  52.1 us (45%)
  starting transfers between devices  26.1 us (22%)
  waiting for transfers between devices  22.5 us (19%)
  between operations  8.92 us (8%)
  local copies, waits for them, and re-layouts  6.06 us (5%)
    pallas_call x2, Pallas kernels, body(): pl.pallas_call(functools.partial(round_kernel, r > 0), out_shape=f32(colu...  44.3 us
    all_to_all x1, waiting for transfers between devices, body(): mine = lax.all_to_all(orbitals.reshape(n, rows, nx), 'cols', 0, 0)  15.5 us
    ppermute x6, starting transfers between devices, body(): behind[r] = lax.ppermute(behind[r], 'cols', counter)  8.12 us
    all_to_all x1, starting transfers between devices, body(): mine = lax.all_to_all(orbitals.reshape(n, rows, nx), 'cols', 0, 0)  7.41 us
    ppermute x8, starting transfers between devices, body(): ahead[r] = lax.ppermute(ahead[r], 'cols', clockwise)  5.83 us
    ppermute x8, waiting for transfers between devices, body(): ahead[r] = lax.ppermute(ahead[r], 'cols', clockwise)  3.82 us
    ppermute x2, starting transfers between devices, body(): psi_right = lax.ppermute(psi_first, 'sec', sec_down)  3.45 us
    unnamed x18, local copies, waits for them, and re-layouts  3.34 us
  transfers between devices with their start and end apart: 21, of which 7 were waited for; matrix products, arithmetic and copies ran while one was open for 2% of the time, Pallas kernels for 25%

profile of v1, /device:TPU:0, one launch (start us, length us, event | category | flops | bytes accessed | tf_op | source)
XLA Modules:
  0.0 115.7 jit_solution(9576679575675138755)
XLA Ops:
  0.0 0.0 copy-start.7
  0.0 7.4 %all-to-all-start = ((f32[8,192,128]{2,1,0:T(8,128)}), f32[8,192,128]{2,1,0:T(8,128)S(1)}, u32[]{:S(2)}, u32[]{:S(2)}) async-start(f32[8,192,128]{2,1,0:T(8,128)} %bitcast.28), calls=%async_computation | async-start | bytes 1572864 | tf_op jit(solution)/shard_map/all_to_all | solution.py:244
  7.4 0.0 copy-done.7
  7.4 0.0 copy-start.8
  7.4 0.0 copy-start.6
  7.4 0.6 fusion.1
  12.1 15.5 %all-to-all-done = f32[8,192,128]{2,1,0:T(8,128)S(1)} async-done(((f32[8,192,128]{2,1,0:T(8,128)}), f32[8,192,128]{2,1,0:T(8,128)S(1)}, u32[]{:S(2)}, u32[]{:S(2)}) %all-to-all-start) | async-done | bytes 786464 | tf_op jit(solution)/shard_map/all_to_all | solution.py:244
  27.6 1.4 %collective-permute-start.12 = (f32[192,128]{1,0:T(8,128)S(1)}, f32[192,128]{1,0:T(8,128)S(1)}, u32[]{:S(2)}, u32[]{:S(2)}) collective-permute-start(f32[192,128]{1,0:T(8,128)S(1)} %get-tuple-element.27.refs_0_), channel_id=1, source_target_pairs={{8,0},{16,8},{24,16},{28,24},{20,28},{12,20},{4,12},{0,4},{9,1},{1... | collective-permute-start | bytes 294920 | tf_op jit(solution)/shard_map/ppermute | solution.py:260
  29.1 0.6 collective-permute-start.11
  29.7 0.3 collective-permute-start
  30.0 1.7 %collective-permute-start.1 = (f32[192,128]{1,0:T(8,128)S(1)}, f32[192,128]{1,0:T(8,128)S(1)}, u32[]{:S(2)}, u32[]{:S(2)}) collective-permute-start(f32[192,128]{1,0:T(8,128)S(1)} %get-tuple-element.28.refs_0_), channel_id=1, source_target_pairs={{8,0},{16,8},{24,16},{28,24},{20,28},{12,20},{4,12},{0,4},{9,1},{1... | collective-permute-start | bytes 294920 | tf_op jit(solution)/shard_map/ppermute | solution.py:260
  31.7 1.3 %collective-permute-done.12.refs_2_ = f32[192,128]{1,0:T(8,128)S(1)} collective-permute-done((f32[192,128]{1,0:T(8,128)S(1)}, f32[192,128]{1,0:T(8,128)S(1)}, u32[]{:S(2)}, u32[]{:S(2)}) %collective-permute-start.12) | collective-permute-done | bytes 98336 | tf_op jit(solution)/shard_map/ppermute | solution.py:260
  33.0 1.5 %collective-permute-start.14 = (f32[192,128]{1,0:T(8,128)S(1)}, f32[192,128]{1,0:T(8,128)S(1)}, u32[]{:S(2)}, u32[]{:S(2)}) collective-permute-start(f32[192,128]{1,0:T(8,128)S(1)} %collective-permute-done.12.refs_2_), channel_id=1, source_target_pairs={{8,0},{16,8},{24,16},{28,24},{20,28},{12,20},{4,12},{0,4},{9,1},{1... | collective-permute-start | bytes 294920 | tf_op jit(solution)/shard_map/ppermute | solution.py:260
  34.5 0.0 collective-permute-done.11.refs_1_
  34.5 0.5 collective-permute-start.13
  35.0 0.2 collective-permute-done.refs_1_
  35.2 1.0 collective-permute-start.2
  36.2 0.0 copy-done
  36.2 1.1 copy-done.1
  37.3 1.7 %pack.1 = (f32[3,96,128]{2,1,0:T(8,128)}, f32[3,96,128]{2,1,0:T(8,128)S(1)}) custom-call(f32[2,16,96,128]{3,2,1,0:T(8,128)S(1)} %copy-done, f32[16,96,128]{2,1,0:T(8,128)S(1)} %copy-done.1), custom_call_target="tpu_custom_call" | custom-call | tf_op jit(solution)/shard_map/pack/pallas_call | solution.py:233
  39.1 0.7 copy-done.5
  39.7 0.0 collective-permute-start.9
  39.7 0.0 copy-done.8
  39.7 0.6 dynamic_slice.10
  45.2 0.8 stack.34
  45.9 0.0 collective-permute-done.1.refs_2_
  46.0 1.1 collective-permute-start.3
  47.0 0.0 collective-permute-done.14.refs_4_
  47.0 1.3 %collective-permute-start.16 = (f32[192,128]{1,0:T(8,128)S(1)}, f32[192,128]{1,0:T(8,128)S(1)}, u32[]{:S(2)}, u32[]{:S(2)}) collective-permute-start(f32[192,128]{1,0:T(8,128)S(1)} %collective-permute-done.14.refs_4_), channel_id=1, source_target_pairs={{8,0},{16,8},{24,16},{28,24},{20,28},{12,20},{4,12},{0,4},{9,1},{1... | collective-permute-start | bytes 294920 | tf_op jit(solution)/shard_map/ppermute | solution.py:260
  48.4 0.0 collective-permute-done.13.refs_3_
  48.4 0.7 collective-permute-start.15
  49.1 0.0 collective-permute-done.2.refs_3_
  49.1 1.0 collective-permute-start.4
  50.1 1.0 collective-permute-done.3.refs_4_
  51.1 1.2 %collective-permute-start.10 = (f32[3,96,128]{2,1,0:T(8,128)}, f32[3,96,128]{2,1,0:T(8,128)S(1)}, u32[]{:S(2)}, u32[]{:S(2)}) collective-permute-start(f32[3,96,128]{2,1,0:T(8,128)} %copy-done.5), channel_id=1, source_target_pairs={{1,0},{2,1},{3,2},{0,3},{5,4},{6,5},{7,6},{4,7},{9,8},{10,9},{11,1... | collective-permute-start | bytes 442376 | tf_op jit(solution)/shard_map/ppermute | solution.py:242
  52.3 0.8 collective-permute-done.16.refs_6_
  53.1 0.6 copy-done.3
  53.7 1.0 collective-permute-start.5
  54.8 0.0 collective-permute-done.15.refs_5_
  54.8 1.0 collective-permute-start.17
  55.8 0.4 collective-permute-done.4.refs_5_
  56.1 0.7 collective-permute-start.6
  56.9 0.0 copy-done.6
  56.9 0.6 gather_fusion
  57.5 3.3 %collective-permute-done.17.refs_7_ = f32[192,128]{1,0:T(8,128)} collective-permute-done((f32[192,128]{1,0:T(8,128)}, f32[192,128]{1,0:T(8,128)}, u32[]{:S(2)}, u32[]{:S(2)}) %collective-permute-start.17) | collective-permute-done | bytes 98336 | tf_op jit(solution)/shard_map/ppermute | solution.py:257
  60.8 0.9 copy-done.4
  61.7 1.5 %gather.9 = (f32[1536,128]{1,0:T(8,128)S(1)}, f32[96,128]{1,0:T(8,128)S(1)}, f32[96,128]{1,0:T(8,128)S(1)}) custom-call(s32[8]{0:T(128)S(1)} %gather_fusion, f32[192,128]{1,0:T(8,128)S(1)} %get-tuple-element.27.refs_0_, f32[192,128]{1,0:T(8,128)S(1)} %collective-permute-done.11.refs_1_, f32[192,128]{1,0:T(8,128)S(1)} %collective-permute-done.12.refs_2_, ...), custom_call_target="tpu_custom_call" | custom-call | tf_op jit(solution)/shard_map/gather/pallas_call | solution.py:279
  63.1 0.1 collective-permute-start.18
  63.2 0.0 collective-permute-done.5.refs_6_
  63.2 1.7 %collective-permute-start.19 = (f32[96,128]{1,0:T(8,128)S(1)}, f32[96,128]{1,0:T(8,128)S(1)}, u32[]{:S(2)}, u32[]{:S(2)}) collective-permute-start(f32[96,128]{1,0:T(8,128)S(1)} %get-tuple-element.26), channel_id=1, source_target_pairs={{1,0},{2,1},{3,2},{0,3},{5,4},{6,5},{7,6},{4,7},{9,8},{10,9},{11,1... | collective-permute-start | bytes 147464 | tf_op jit(solution)/shard_map/ppermute | solution.py:288
  64.9 0.0 collective-permute-done.6.refs_7_
  64.9 1.6 %gather.8 = (f32[1536,128]{1,0:T(8,128)S(1)}, f32[96,128]{1,0:T(8,128)S(1)}, f32[96,128]{1,0:T(8,128)S(1)}) custom-call(s32[8]{0:T(128)S(1)} %gather_fusion, f32[192,128]{1,0:T(8,128)S(1)} %get-tuple-element.28.refs_0_, f32[192,128]{1,0:T(8,128)S(1)} %collective-permute-done.refs_1_, f32[192,128]{1,0:T(8,128)S(1)} %collective-permute-done.1.refs_2_, ...), custom_call_target="tpu_custom_call" | custom-call | tf_op jit(solution)/shard_map/gather/pallas_call | solution.py:279
  66.5 0.1 collective-permute-start.7
  66.6 0.0 collective-permute-done.9.left
  66.6 1.7 %collective-permute-start.8 = (f32[96,128]{1,0:T(8,128)S(1)}, f32[96,128]{1,0:T(8,128)S(1)}, u32[]{:S(2)}, u32[]{:S(2)}) collective-permute-start(f32[96,128]{1,0:T(8,128)S(1)} %get-tuple-element.18), channel_id=1, source_target_pairs={{1,0},{2,1},{3,2},{0,3},{5,4},{6,5},{7,6},{4,7},{9,8},{10,9},{11,1... | collective-permute-start | bytes 147464 | tf_op jit(solution)/shard_map/ppermute | solution.py:288
  68.3 0.0 collective-permute-done.10.right
  68.3 0.0 copy-done.2
  68.3 3.0 %prepare.1 = (f32[8,96,128]{2,1,0:T(8,128)S(1)}, f32[16,96,128]{2,1,0:T(8,128)S(1)}, f32[8,96,128]{2,1,0:T(8,128)S(1)}) custom-call(f32[2,16,96,128]{3,2,1,0:T(8,128)S(1)} %copy-done, f32[16,96,128]{2,1,0:T(8,128)S(1)} %copy-done.2, f32[3,96,128]{2,1,0:T(8,128)S(1)} %collective-permute-done.9.left, f32[3,96,128]{2,1,0:T(8,128)S(1)} %collective-permute-done.10.right), custom_call_target="tpu_custom_call" | custom-call | tf_op jit(solution)/shard_map/prepare/pallas_call | solution.py:267
  71.3 0.0 collective-permute-done.18.left
  71.3 0.0 collective-permute-done.19.right
  71.3 21.5 %round.2.refs_0_ = f32[2,16,96,128]{3,2,1,0:T(8,128)S(1)} custom-call(f32[16,96,128]{2,1,0:T(8,128)S(1)} %bitcast.27, f32[96,128]{1,0:T(8,128)S(1)} %collective-permute-done.18.left, f32[96,128]{1,0:T(8,128)S(1)} %collective-permute-done.19.right, f32[2,16,96,128]{3,2,1,0:T(8,128)S(1)} %copy-done, f32[8,96,128]{2,1,0:T(8,128)S(1)} %get-tuple-element.21.trial_halo, ...), custom_call_target="tpu_custom_call" | custom-call | tf_op jit(solution)/shard_map/round/pallas_call | solution.py:295
  92.9 0.0 collective-permute-done.7.left
  92.9 0.0 collective-permute-done.8.right
  92.9 22.8 %round.3 = f32[2,16,96,128]{3,2,1,0:T(8,128)} custom-call(f32[16,96,128]{2,1,0:T(8,128)S(1)} %bitcast.26, f32[96,128]{1,0:T(8,128)S(1)} %collective-permute-done.7.left, f32[96,128]{1,0:T(8,128)S(1)} %collective-permute-done.8.right, f32[2,16,96,128]{3,2,1,0:T(8,128)S(1)} %copy-done, f32[8,96,128]{2,1,0:T(8,128)S(1)} %get-tuple-element.21.trial_halo, ...), custom_call_target="tpu_custom_call" | custom-call | tf_op jit(solution)/shard_map/round/pallas_call | solution.py:295
  (9 shorter events, 0.0 us)
Async XLA Ops:
  0.0 7.4 %copy-start.7 = (s32[2]{0:T(128)S(1)}, s32[2]{0:T(128)}, u32[]{:S(2)}) copy-start(s32[2]{0:T(128)} %param.9) | copy-start | bytes 28
  0.0 36.2 %copy-start = (f32[2,16,96,128]{3,2,1,0:T(8,128)S(1)}, f32[2,16,96,128]{3,2,1,0:T(8,128)}, u32[]{:S(2)}) copy-start(f32[2,16,96,128]{3,2,1,0:T(8,128)} %trial.7) | copy-start | bytes 4718596
  0.0 27.6 %all-to-all-start = ((f32[8,192,128]{2,1,0:T(8,128)}), f32[8,192,128]{2,1,0:T(8,128)S(1)}, u32[]{:S(2)}, u32[]{:S(2)}) async-start(f32[8,192,128]{2,1,0:T(8,128)} %bitcast.28), calls=%async_computation | async-start | bytes 1572864 | tf_op jit(solution)/shard_map/all_to_all | solution.py:244
  7.4 32.3 %copy-start.8 = (s32[8]{0:T(128)S(1)}, s32[8]{0:T(128)}, u32[]{:S(2)}) copy-start(s32[8]{0:T(128)} %constant.79.clone) | copy-start | bytes 100
  7.4 49.4 %copy-start.6 = (s32[8]{0:T(128)S(1)}, s32[8]{0:T(128)}, u32[]{:S(2)}) copy-start(s32[8]{0:T(128)} %constant.78.clone) | copy-start | bytes 100
  27.6 5.4 %collective-permute-start.12 = (f32[192,128]{1,0:T(8,128)S(1)}, f32[192,128]{1,0:T(8,128)S(1)}, u32[]{:S(2)}, u32[]{:S(2)}) collective-permute-start(f32[192,128]{1,0:T(8,128)S(1)} %get-tuple-element.27.refs_0_), channel_id=1, source_target_pairs={{8,0},{16,8},{24,16},{28,24},{20,28},{12,20},{4,12},{0,4},{9,1},{1... | collective-permute-start | bytes 294920 | tf_op jit(solution)/shard_map/ppermute | solution.py:260
  29.1 5.4 %collective-permute-start.11 = (f32[192,128]{1,0:T(8,128)S(1)}, f32[192,128]{1,0:T(8,128)S(1)}, u32[]{:S(2)}, u32[]{:S(2)}) collective-permute-start(f32[192,128]{1,0:T(8,128)S(1)} %get-tuple-element.27.refs_0_), channel_id=1, source_target_pairs={{0,8},{8,16},{16,24},{24,28},{28,20},{20,12},{12,4},{4,0},{1,9},{9... | collective-permute-start | bytes 294920 | tf_op jit(solution)/shard_map/ppermute | solution.py:257
  29.7 5.5 %collective-permute-start = (f32[192,128]{1,0:T(8,128)S(1)}, f32[192,128]{1,0:T(8,128)S(1)}, u32[]{:S(2)}, u32[]{:S(2)}) collective-permute-start(f32[192,128]{1,0:T(8,128)S(1)} %get-tuple-element.28.refs_0_), channel_id=1, source_target_pairs={{0,8},{8,16},{16,24},{24,28},{28,20},{20,12},{12,4},{4,0},{1,9},{9... | collective-permute-start | bytes 294920 | tf_op jit(solution)/shard_map/ppermute | solution.py:257
  30.0 16.0 %collective-permute-start.1 = (f32[192,128]{1,0:T(8,128)S(1)}, f32[192,128]{1,0:T(8,128)S(1)}, u32[]{:S(2)}, u32[]{:S(2)}) collective-permute-start(f32[192,128]{1,0:T(8,128)S(1)} %get-tuple-element.28.refs_0_), channel_id=1, source_target_pairs={{8,0},{16,8},{24,16},{28,24},{20,28},{12,20},{4,12},{0,4},{9,1},{1... | collective-permute-start | bytes 294920 | tf_op jit(solution)/shard_map/ppermute | solution.py:260
  33.0 14.1 %collective-permute-start.14 = (f32[192,128]{1,0:T(8,128)S(1)}, f32[192,128]{1,0:T(8,128)S(1)}, u32[]{:S(2)}, u32[]{:S(2)}) collective-permute-start(f32[192,128]{1,0:T(8,128)S(1)} %collective-permute-done.12.refs_2_), channel_id=1, source_target_pairs={{8,0},{16,8},{24,16},{28,24},{20,28},{12,20},{4,12},{0,4},{9,1},{1... | collective-permute-start | bytes 294920 | tf_op jit(solution)/shard_map/ppermute | solution.py:260
  34.5 13.9 %collective-permute-start.13 = (f32[192,128]{1,0:T(8,128)S(1)}, f32[192,128]{1,0:T(8,128)S(1)}, u32[]{:S(2)}, u32[]{:S(2)}) collective-permute-start(f32[192,128]{1,0:T(8,128)S(1)} %collective-permute-done.11.refs_1_), channel_id=1, source_target_pairs={{0,8},{8,16},{16,24},{24,28},{28,20},{20,12},{12,4},{4,0},{1,9},{9... | collective-permute-start | bytes 294920 | tf_op jit(solution)/shard_map/ppermute | solution.py:257
  35.2 13.9 %collective-permute-start.2 = (f32[192,128]{1,0:T(8,128)S(1)}, f32[192,128]{1,0:T(8,128)S(1)}, u32[]{:S(2)}, u32[]{:S(2)}) collective-permute-start(f32[192,128]{1,0:T(8,128)S(1)} %collective-permute-done.refs_1_), channel_id=1, source_target_pairs={{0,8},{8,16},{16,24},{24,28},{28,20},{20,12},{12,4},{4,0},{1,9},{9... | collective-permute-start | bytes 294920 | tf_op jit(solution)/shard_map/ppermute | solution.py:257
  36.2 1.1 copy-start.1
  39.1 0.7 copy-start.5
  39.7 28.6 %copy-start.2 = (f32[16,96,128]{2,1,0:T(8,128)S(1)}, f32[16,96,128]{2,1,0:T(8,128)}, u32[]{:S(2)}) copy-start(f32[16,96,128]{2,1,0:T(8,128)} %potential.3) | copy-start | bytes 2359300
  39.7 26.9 %collective-permute-start.9 = (f32[3,96,128]{2,1,0:T(8,128)}, f32[3,96,128]{2,1,0:T(8,128)S(1)}, u32[]{:S(2)}, u32[]{:S(2)}) collective-permute-start(f32[3,96,128]{2,1,0:T(8,128)} %get-tuple-element.19), channel_id=1, source_target_pairs={{0,1},{1,2},{2,3},{3,0},{4,5},{5,6},{6,7},{7,4},{8,9},{9,10},{10,1... | collective-permute-start | bytes 442376 | tf_op jit(solution)/shard_map/ppermute | solution.py:241
  46.0 5.2 %collective-permute-start.3 = (f32[192,128]{1,0:T(8,128)S(1)}, f32[192,128]{1,0:T(8,128)}, u32[]{:S(2)}, u32[]{:S(2)}) collective-permute-start(f32[192,128]{1,0:T(8,128)S(1)} %collective-permute-done.1.refs_2_), channel_id=1, source_target_pairs={{8,0},{16,8},{24,16},{28,24},{20,28},{12,20},{4,12},{0,4},{9,1},{1... | collective-permute-start | bytes 294920 | tf_op jit(solution)/shard_map/ppermute | solution.py:260
  47.0 6.1 %collective-permute-start.16 = (f32[192,128]{1,0:T(8,128)S(1)}, f32[192,128]{1,0:T(8,128)S(1)}, u32[]{:S(2)}, u32[]{:S(2)}) collective-permute-start(f32[192,128]{1,0:T(8,128)S(1)} %collective-permute-done.14.refs_4_), channel_id=1, source_target_pairs={{8,0},{16,8},{24,16},{28,24},{20,28},{12,20},{4,12},{0,4},{9,1},{1... | collective-permute-start | bytes 294920 | tf_op jit(solution)/shard_map/ppermute | solution.py:260
  48.4 6.4 %collective-permute-start.15 = (f32[192,128]{1,0:T(8,128)S(1)}, f32[192,128]{1,0:T(8,128)}, u32[]{:S(2)}, u32[]{:S(2)}) collective-permute-start(f32[192,128]{1,0:T(8,128)S(1)} %collective-permute-done.13.refs_3_), channel_id=1, source_target_pairs={{0,8},{8,16},{16,24},{24,28},{28,20},{20,12},{12,4},{4,0},{1,9},{9... | collective-permute-start | bytes 294920 | tf_op jit(solution)/shard_map/ppermute | solution.py:257
  49.1 7.1 %collective-permute-start.4 = (f32[192,128]{1,0:T(8,128)S(1)}, f32[192,128]{1,0:T(8,128)}, u32[]{:S(2)}, u32[]{:S(2)}) collective-permute-start(f32[192,128]{1,0:T(8,128)S(1)} %collective-permute-done.2.refs_3_), channel_id=1, source_target_pairs={{0,8},{8,16},{16,24},{24,28},{28,20},{20,12},{12,4},{4,0},{1,9},{9... | collective-permute-start | bytes 294920 | tf_op jit(solution)/shard_map/ppermute | solution.py:257
  51.1 17.2 %collective-permute-start.10 = (f32[3,96,128]{2,1,0:T(8,128)}, f32[3,96,128]{2,1,0:T(8,128)S(1)}, u32[]{:S(2)}, u32[]{:S(2)}) collective-permute-start(f32[3,96,128]{2,1,0:T(8,128)} %copy-done.5), channel_id=1, source_target_pairs={{1,0},{2,1},{3,2},{0,3},{5,4},{6,5},{7,6},{4,7},{9,8},{10,9},{11,1... | collective-permute-start | bytes 442376 | tf_op jit(solution)/shard_map/ppermute | solution.py:242
  53.1 0.6 copy-start.3
  53.7 9.5 %collective-permute-start.5 = (f32[192,128]{1,0:T(8,128)}, f32[192,128]{1,0:T(8,128)}, u32[]{:S(2)}, u32[]{:S(2)}) collective-permute-start(f32[192,128]{1,0:T(8,128)} %collective-permute-done.3.refs_4_), channel_id=1, source_target_pairs={{8,0},{16,8},{24,16},{28,24},{20,28},{12,20},{4,12},{0,4},{9,1},{1... | collective-permute-start | bytes 294920 | tf_op jit(solution)/shard_map/ppermute | solution.py:260
  54.8 6.0 %collective-permute-start.17 = (f32[192,128]{1,0:T(8,128)}, f32[192,128]{1,0:T(8,128)}, u32[]{:S(2)}, u32[]{:S(2)}) collective-permute-start(f32[192,128]{1,0:T(8,128)} %collective-permute-done.15.refs_5_), channel_id=1, source_target_pairs={{0,8},{8,16},{16,24},{24,28},{28,20},{20,12},{12,4},{4,0},{1,9},{9... | collective-permute-start | bytes 294920 | tf_op jit(solution)/shard_map/ppermute | solution.py:257
  56.1 8.8 %collective-permute-start.6 = (f32[192,128]{1,0:T(8,128)}, f32[192,128]{1,0:T(8,128)}, u32[]{:S(2)}, u32[]{:S(2)}) collective-permute-start(f32[192,128]{1,0:T(8,128)} %collective-permute-done.4.refs_5_), channel_id=1, source_target_pairs={{0,8},{8,16},{16,24},{24,28},{28,20},{20,12},{12,4},{4,0},{1,9},{9... | collective-permute-start | bytes 294920 | tf_op jit(solution)/shard_map/ppermute | solution.py:257
  60.8 0.9 copy-start.4
  63.1 8.2 %collective-permute-start.18 = (f32[96,128]{1,0:T(8,128)S(1)}, f32[96,128]{1,0:T(8,128)S(1)}, u32[]{:S(2)}, u32[]{:S(2)}) collective-permute-start(f32[96,128]{1,0:T(8,128)S(1)} %get-tuple-element.25), channel_id=1, source_target_pairs={{0,1},{1,2},{2,3},{3,0},{4,5},{5,6},{6,7},{7,4},{8,9},{9,10},{10,1... | collective-permute-start | bytes 147464 | tf_op jit(solution)/shard_map/ppermute | solution.py:287
  63.2 8.1 %collective-permute-start.19 = (f32[96,128]{1,0:T(8,128)S(1)}, f32[96,128]{1,0:T(8,128)S(1)}, u32[]{:S(2)}, u32[]{:S(2)}) collective-permute-start(f32[96,128]{1,0:T(8,128)S(1)} %get-tuple-element.26), channel_id=1, source_target_pairs={{1,0},{2,1},{3,2},{0,3},{5,4},{6,5},{7,6},{4,7},{9,8},{10,9},{11,1... | collective-permute-start | bytes 147464 | tf_op jit(solution)/shard_map/ppermute | solution.py:288
  66.5 26.4 %collective-permute-start.7 = (f32[96,128]{1,0:T(8,128)S(1)}, f32[96,128]{1,0:T(8,128)S(1)}, u32[]{:S(2)}, u32[]{:S(2)}) collective-permute-start(f32[96,128]{1,0:T(8,128)S(1)} %get-tuple-element.17), channel_id=1, source_target_pairs={{0,1},{1,2},{2,3},{3,0},{4,5},{5,6},{6,7},{7,4},{8,9},{9,10},{10,1... | collective-permute-start | bytes 147464 | tf_op jit(solution)/shard_map/ppermute | solution.py:287
  66.6 26.3 %collective-permute-start.8 = (f32[96,128]{1,0:T(8,128)S(1)}, f32[96,128]{1,0:T(8,128)S(1)}, u32[]{:S(2)}, u32[]{:S(2)}) collective-permute-start(f32[96,128]{1,0:T(8,128)S(1)} %get-tuple-element.18), channel_id=1, source_target_pairs={{1,0},{2,1},{3,2},{0,3},{5,4},{6,5},{7,6},{4,7},{9,8},{10,9},{11,1... | collective-permute-start | bytes 147464 | tf_op jit(solution)/shard_map/ppermute | solution.py:288

commit v2 on v1

--- a/solution.py
+++ b/solution.py
@@ -2,6 +2,7 @@
 
 import jax
 import jax.numpy as jnp
+import numpy as np
 from jax import lax
 from jax.experimental import pallas as pl
 from jax.experimental.pallas import tpu as pltpu
@@ -65,9 +66,9 @@
             tile = tile + (pltpu.roll(part, 32 * c, 1) if c else part)
         trial_halo[y] = tile
         part = halo_plane(left[columns], right[columns], potential[y], potential[y + half], lane, y)
-        scaled_halo[y] = 6.0 * (part + pltpu.roll(part, 32, 1)) - 8.0
+        scaled_halo[y] = 6.0 * (part + pltpu.roll(part, 32, 1)) - 6.0
     for y in range(ny):
-        scaled[y] = 6.0 * potential[y] - 8.0
+        scaled[y] = 6.0 * potential[y] - 6.0
 
 
 def gather_kernel(count, rows, where, *refs):
@@ -109,65 +110,109 @@
         ref[0, k, inside] = jnp.where(lane >= 64, pltpu.roll(ref[0, half + k, inside], 64, 1), 0.0)
 
 
-def round_kernel(adds, psi, left, right, trial, trial_halo, scaled, scaled_halo, *refs):
+def bands():
+    def weight(distance):
+        return {1: -16.0, 2: 1.0}.get(abs(distance), 0.0)
+
+    block = np.array([[weight(i - j) for j in range(128)] for i in range(128)], np.float32)
+    sections = np.zeros((2, 6, 128, 2, 128), np.float32)
+    for h in range(2):
+        for c in range(2):
+            ends = np.zeros((128, 128), np.float32)
+            for i in range(HALO):
+                for j in range(128):
+                    ends[64 * h + 32 * c + i, j] = weight(i - HALO - j)
+                    ends[64 * h + 32 * c + 16 + HALO + i, j] = weight(128 + i - j)
+            for piece in range(2):
+                sections[h, 2 * piece + c, :, c] = block
+                sections[h, 4 + piece, :, c] = ends
+    halo = np.zeros((2, 128, 128), np.float32)
+    for start in range(0, 128, 16):
+        halo[:, start : start + 2 * HALO, start : start + 2 * HALO] = block[: 2 * HALO, : 2 * HALO]
+    return jnp.asarray(sections.reshape(2, 768, 256), jnp.bfloat16), jnp.asarray(halo.reshape(256, 128), jnp.bfloat16)
+
+
+def round_scratch(columns, ny, nz, nx):
+    half = ny // 2
+    return (
+        [pltpu.VMEM((columns, ny + 4, nz + 2 * ZP, nx), jnp.float32)] * 3
+        + [pltpu.VMEM((1, half + 4, nz + 2 * ZP, nx), jnp.float32)] * 3
+        + [
+            pltpu.VMEM((ny * nz, 6 * nx), jnp.bfloat16),
+            pltpu.VMEM((ny * nz, 2 * nx), jnp.float32),
+            pltpu.VMEM((half * nz, nx), jnp.float32),
+        ]
+    )
+
+
+def round_kernel(adds, psi, left, right, trial, trial_halo, scaled, scaled_halo, bands, halo_bands, *refs):
     if adds:
-        total, out, w, u, v, ends, w_halo, u_halo, v_halo = refs
-    else:
-        out, w, u, v, ends, w_halo, u_halo, v_halo = refs
+        total, *refs = refs
+    out, w, u, v, w_halo, u_halo, v_halo, pieces, sums, halo_sums = refs
     columns, ny, nz, _ = trial.shape
     half = ny // 2
     full = lanes(nz)
-    lane = lanes(CHUNK)
     for ref in (w, u, v):
         clear_borders(ref, ny, nz)
     for ref in (w_halo, u_halo, v_halo):
         clear_borders(ref, half, nz)
 
+    def split(value, row, first, second):
+        high = value.astype(jnp.bfloat16)
+        pieces[pl.ds(row, CHUNK), 128 * first : 128 * (first + 1)] = high
+        rest = (value - high.astype(jnp.float32)).astype(jnp.bfloat16)
+        pieces[pl.ds(row, CHUNK), 128 * second : 128 * (second + 1)] = rest
+
+    def row_of(y, z):
+        return pl.multiple_of(y * nz + z, CHUNK)
+
+    def put(target, c, y, z, value):
+        target[c, y + 2, pl.ds(ZP + z, CHUNK)] = value
+        split(value, row_of(y, z), c, 2 + c)
+
+    def put_halo(target, y, z, value):
+        target[0, y + 2, pl.ds(ZP + z, CHUNK)] = value
+        for h in range(2):
+            split(value, row_of(y + h * half, z), 4, 5)
+
     for y in range(half):
         part = halo_plane(left[...], right[...], psi[y], psi[y + half], full, y)
         w_halo[0, y + 2, pl.ds(ZP, nz)] = (part + pltpu.roll(part, 32, 1)) * trial_halo[y]
     wrap_halo(w_halo, half, nz, full)
 
+    @pl.loop(0, half)
+    def _(y):
+        for z in range(0, nz, CHUNK):
+            put_halo(w_halo, y, z, w_halo[0, y + 2, pl.ds(ZP + z, CHUNK)])
+
     @pl.loop(0, ny)
     def _(y):
-        for c in range(columns):
-            w[c, y + 2, pl.ds(ZP, nz)] = psi[y] * trial[c, y]
-
-    def along(f):
-        pair = f + pltpu.roll(f, 2, 1)
-        return pltpu.roll(pair, 127, 1), pair + pltpu.roll(pair, 126, 1)
+        for z in range(0, nz, CHUNK):
+            here = psi[y, pl.ds(z, CHUNK)]
+            for c in range(columns):
+                put(w, c, y, z, here * trial[c, y, pl.ds(z, CHUNK)])
+
+    def multiply():
+        for h in range(2):
+            rows = pl.ds(h * half * nz, half * nz)
+            sums[rows, :] = jnp.dot(pieces[rows, :], bands[h], preferred_element_type=jnp.float32)
 
     def halo_stage(source, target, shift, weight):
+        halo_sums[...] = jnp.dot(pieces[: half * nz, 512:], halo_bands[...], preferred_element_type=jnp.float32)
+
         @pl.loop(0, half)
         def _(y):
             for z in range(0, nz, CHUNK):
                 at = ZP + z
                 f = source[0, y + 2, pl.ds(at, CHUNK)]
                 near, far = neighbours(source, 0, y + 2, at, CHUNK)
-                one, two = along(f)
-                value = (far + two) - 16.0 * (near + one) + (scaled_halo[y, pl.ds(z, CHUNK)] - shift) * f
+                value = (far + halo_sums[pl.ds(row_of(y, z), CHUNK), :]) - 16.0 * near
+                value = value + (scaled_halo[y, pl.ds(z, CHUNK)] - shift) * f
                 if weight:
                     value = value - weight * w_halo[0, y + 2, pl.ds(at, CHUNK)]
-                target[0, y + 2, pl.ds(at, CHUNK)] = value
+                put_halo(target, y, z, value)
 
         wrap_halo(target, half, nz, full)
-
-    def mend(source):
-        inner = lane % 32
-
-        @pl.loop(0, half)
-        def _(y):
-            for z in range(0, nz, CHUNK):
-                f = source[0, y + 2, pl.ds(ZP + z, CHUNK)]
-                gap = f - pltpu.roll(f, 112, 1)
-                gap = jnp.where(between(inner, 4, 6), gap, jnp.where(between(inner, 6, 8), -gap, 0.0))
-                far = jnp.where(inner < 6, pltpu.roll(gap, 126, 1), pltpu.roll(gap, 2, 1))
-                near = jnp.where(inner == 5, pltpu.roll(gap, 127, 1), pltpu.roll(gap, 1, 1))
-                both = far - jnp.where(between(inner, 5, 7), 16.0 * near, 0.0)
-                for h in range(2):
-                    for c in range(columns):
-                        moved = pltpu.roll(both, (122 - 64 * h - 32 * c) % 128, 1)
-                        ends[c, y + h * half, pl.ds(z, CHUNK)] = jnp.where((lane < 2) | (lane >= 126), moved, 0.0)
 
     def stage(source, shift, weight, store):
         @pl.loop(0, ny)
@@ -178,17 +223,14 @@
                 for c in range(columns):
                     f = source[c, y + 2, pl.ds(at, CHUNK)]
                     near, far = neighbours(source, c, y + 2, at, CHUNK)
-                    one, two = along(f)
-                    value = (far + two) - 16.0 * (near + one) + diagonal * f + ends[c, y, pl.ds(z, CHUNK)]
+                    value = (far + sums[pl.ds(row_of(y, z), CHUNK), 128 * c : 128 * (c + 1)]) - 16.0 * near
+                    value = value + diagonal * f
                     if weight:
                         value = value - weight * w[c, y + 2, pl.ds(at, CHUNK)]
                     store(c, y, z, value)
 
     def into(target):
-        def store(c, y, z, value):
-            target[c, y + 2, pl.ds(ZP + z, CHUNK)] = value
-
-        return store
+        return lambda c, y, z, value: put(target, c, y, z, value)
 
     def finish(c, y, z, value):
         term = (FINAL * psi[y, pl.ds(z, CHUNK)]) * value
@@ -196,13 +238,13 @@
             term = term + total[c, y, pl.ds(z, CHUNK)]
         out[c, y, pl.ds(z, CHUNK)] = term
 
+    multiply()
     halo_stage(w_halo, u_halo, ALPHA, None)
+    stage(w, ALPHA, None, into(u))
+    multiply()
     halo_stage(u_halo, v_halo, 0.0, BETA)
-    mend(w_halo)
-    stage(w, ALPHA, None, into(u))
-    mend(u_halo)
     stage(u, 0.0, BETA, into(v))
-    mend(v_halo)
+    multiply()
     stage(v, 0.0, GAMMA, finish)
 
 
@@ -287,18 +329,16 @@
         psi_left = lax.ppermute(psi_last, "sec", sec_up)
         psi_right = lax.ppermute(psi_first, "sec", sec_down)
         sections.append((psi.reshape(ny, nz, nx), psi_left, psi_right))
+    matrices = bands()
     for r in range(rounds):
-        given = [*sections[r], trial, trial_halo, scaled, scaled_halo] + ([total] if r else [])
-        planes = [pltpu.VMEM((columns, ny + 4, nz + 2 * ZP, nx), jnp.float32)] * 3
-        planes.append(pltpu.VMEM((columns, ny, nz, nx), jnp.float32))
-        halos = [pltpu.VMEM((1, ny // 2 + 4, nz + 2 * ZP, nx), jnp.float32)] * 3
+        given = [*sections[r], trial, trial_halo, scaled, scaled_halo, *matrices] + ([total] if r else [])
         total = pl.pallas_call(
             functools.partial(round_kernel, r > 0),
             out_shape=f32(columns, ny, nz, nx),
             in_specs=vmem(len(given)),
             out_specs=pl.BlockSpec(memory_space=pltpu.VMEM),
-            scratch_shapes=planes + halos,
-            compiler_params=params(24),
+            scratch_shapes=round_scratch(columns, ny, nz, nx),
+            compiler_params=params(32),
             name="round",
         )(*given)
     return total

time: 116 us -> 92.1 us (0.79)
  Pallas kernels: 52.1 us -> 28.4 us
    pallas_call x2, Pallas kernels: 44.3 us -> 20.6 us  [body(): pl.pallas_call(functools.partial(round_kernel, r > 0), out_shape=f32(colu...]
    unnamed x18 -> x22, local copies, waits for them, and re-layouts: 3.34 us -> 3.34 us
  transfers between devices with their start and end apart: 21 -> 21, of which waited for: 7 -> 7; matrix products, arithmetic and copies ran while one was open for 2% -> 3% of each run, Pallas kernels for 25% -> 19%
where the time goes in v2:
time: 92.1 us; the launch traced here: 91.7 us
  Pallas kernels  28.4 us (31%)
  starting transfers between devices  26.1 us (28%)
  waiting for transfers between devices  22.9 us (25%)
  between operations  8.34 us (9%)
  local copies, waits for them, and re-layouts  5.95 us (6%)
    pallas_call x2, Pallas kernels, body(): pl.pallas_call(functools.partial(round_kernel, r > 0), out_shape=f32(colu...  20.6 us
    all_to_all x1, waiting for transfers between devices, body(): mine = lax.all_to_all(orbitals.reshape(n, rows, nx), 'cols', 0, 0)  15.9 us
    ppermute x6, starting transfers between devices, body(): behind[r] = lax.ppermute(behind[r], 'cols', counter)  8.12 us
    all_to_all x1, starting transfers between devices, body(): mine = lax.all_to_all(orbitals.reshape(n, rows, nx), 'cols', 0, 0)  7.41 us
    ppermute x8, starting transfers between devices, body(): ahead[r] = lax.ppermute(ahead[r], 'cols', clockwise)  5.83 us
    ppermute x8, waiting for transfers between devices, body(): ahead[r] = lax.ppermute(ahead[r], 'cols', clockwise)  3.82 us
    ppermute x2, starting transfers between devices, body(): psi_right = lax.ppermute(psi_first, 'sec', sec_down)  3.43 us
    unnamed x22, local copies, waits for them, and re-layouts  3.34 us
  transfers between devices with their start and end apart: 21, of which 7 were waited for; matrix products, arithmetic and copies ran while one was open for 3% of the time, Pallas kernels for 19%

profile of v2, /device:TPU:0, one launch (start us, length us, event | category | flops | bytes accessed | tf_op | source)
XLA Modules:
  0.0 91.7 jit_solution(346225809385721771)
XLA Ops:
  0.0 7.4 %all-to-all-start = ((f32[8,192,128]{2,1,0:T(8,128)}), f32[8,192,128]{2,1,0:T(8,128)S(1)}, u32[]{:S(2)}, u32[]{:S(2)}) async-start(f32[8,192,128]{2,1,0:T(8,128)} %bitcast.28), calls=%async_computation | async-start | bytes 1572864 | tf_op jit(solution)/shard_map/all_to_all | solution.py:286
  7.4 0.0 copy-done.9
  7.4 0.0 copy-start.10
  7.4 0.0 copy-start.8
  7.4 0.6 fusion.1
  11.7 15.9 %all-to-all-done = f32[8,192,128]{2,1,0:T(8,128)S(1)} async-done(((f32[8,192,128]{2,1,0:T(8,128)}), f32[8,192,128]{2,1,0:T(8,128)S(1)}, u32[]{:S(2)}, u32[]{:S(2)}) %all-to-all-start) | async-done | bytes 786464 | tf_op jit(solution)/shard_map/all_to_all | solution.py:286
  27.6 1.4 %collective-permute-start.12 = (f32[192,128]{1,0:T(8,128)S(1)}, f32[192,128]{1,0:T(8,128)S(1)}, u32[]{:S(2)}, u32[]{:S(2)}) collective-permute-start(f32[192,128]{1,0:T(8,128)S(1)} %get-tuple-element.27.refs_0_), channel_id=1, source_target_pairs={{8,0},{16,8},{24,16},{28,24},{20,28},{12,20},{4,12},{0,4},{9,1},{1... | collective-permute-start | bytes 294920 | tf_op jit(solution)/shard_map/ppermute | solution.py:302
  29.1 0.6 collective-permute-start.11
  29.7 0.3 collective-permute-start
  30.0 1.7 %collective-permute-start.1 = (f32[192,128]{1,0:T(8,128)S(1)}, f32[192,128]{1,0:T(8,128)S(1)}, u32[]{:S(2)}, u32[]{:S(2)}) collective-permute-start(f32[192,128]{1,0:T(8,128)S(1)} %get-tuple-element.28.refs_0_), channel_id=1, source_target_pairs={{8,0},{16,8},{24,16},{28,24},{20,28},{12,20},{4,12},{0,4},{9,1},{1... | collective-permute-start | bytes 294920 | tf_op jit(solution)/shard_map/ppermute | solution.py:302
  31.7 1.3 %collective-permute-done.12.refs_2_ = f32[192,128]{1,0:T(8,128)S(1)} collective-permute-done((f32[192,128]{1,0:T(8,128)S(1)}, f32[192,128]{1,0:T(8,128)S(1)}, u32[]{:S(2)}, u32[]{:S(2)}) %collective-permute-start.12) | collective-permute-done | bytes 98336 | tf_op jit(solution)/shard_map/ppermute | solution.py:302
  33.0 1.5 %collective-permute-start.14 = (f32[192,128]{1,0:T(8,128)S(1)}, f32[192,128]{1,0:T(8,128)S(1)}, u32[]{:S(2)}, u32[]{:S(2)}) collective-permute-start(f32[192,128]{1,0:T(8,128)S(1)} %collective-permute-done.12.refs_2_), channel_id=1, source_target_pairs={{8,0},{16,8},{24,16},{28,24},{20,28},{12,20},{4,12},{0,4},{9,1},{1... | collective-permute-start | bytes 294920 | tf_op jit(solution)/shard_map/ppermute | solution.py:302
  34.5 0.0 collective-permute-done.11.refs_1_
  34.5 0.5 collective-permute-start.13
  35.0 0.2 collective-permute-done.refs_1_
  35.2 1.0 %collective-permute-start.2 = (f32[192,128]{1,0:T(8,128)S(1)}, f32[192,128]{1,0:T(8,128)S(1)}, u32[]{:S(2)}, u32[]{:S(2)}) collective-permute-start(f32[192,128]{1,0:T(8,128)S(1)} %collective-permute-done.refs_1_), channel_id=1, source_target_pairs={{0,8},{8,16},{16,24},{24,28},{28,20},{20,12},{12,4},{4,0},{1,9},{9... | collective-permute-start | bytes 294920 | tf_op jit(solution)/shard_map/ppermute | solution.py:299
  36.2 0.0 copy-done
  36.2 1.1 %copy-done.1 = f32[16,96,128]{2,1,0:T(8,128)S(1)} copy-done((f32[16,96,128]{2,1,0:T(8,128)S(1)}, f32[16,96,128]{2,1,0:T(8,128)}, u32[]{:S(2)}) %copy-start.1) | copy-done | bytes 786456
  37.3 1.7 %pack.1 = (f32[3,96,128]{2,1,0:T(8,128)}, f32[3,96,128]{2,1,0:T(8,128)S(1)}) custom-call(f32[2,16,96,128]{3,2,1,0:T(8,128)S(1)} %copy-done, f32[16,96,128]{2,1,0:T(8,128)S(1)} %copy-done.1), custom_call_target="tpu_custom_call" | custom-call | tf_op jit(solution)/shard_map/pack/pallas_call | solution.py:275
  39.1 0.6 copy-done.7
  39.7 0.0 collective-permute-start.9
  39.7 0.0 copy-done.10
  39.7 0.6 dynamic_slice.10
  44.9 0.7 stack.34
  45.6 0.0 collective-permute-done.1.refs_2_
  45.6 1.1 %collective-permute-start.3 = (f32[192,128]{1,0:T(8,128)S(1)}, f32[192,128]{1,0:T(8,128)}, u32[]{:S(2)}, u32[]{:S(2)}) collective-permute-start(f32[192,128]{1,0:T(8,128)S(1)} %collective-permute-done.1.refs_2_), channel_id=1, source_target_pairs={{8,0},{16,8},{24,16},{28,24},{20,28},{12,20},{4,12},{0,4},{9,1},{1... | collective-permute-start | bytes 294920 | tf_op jit(solution)/shard_map/ppermute | solution.py:302
  46.7 0.0 collective-permute-done.14.refs_4_
  46.7 1.3 %collective-permute-start.16 = (f32[192,128]{1,0:T(8,128)S(1)}, f32[192,128]{1,0:T(8,128)S(1)}, u32[]{:S(2)}, u32[]{:S(2)}) collective-permute-start(f32[192,128]{1,0:T(8,128)S(1)} %collective-permute-done.14.refs_4_), channel_id=1, source_target_pairs={{8,0},{16,8},{24,16},{28,24},{20,28},{12,20},{4,12},{0,4},{9,1},{1... | collective-permute-start | bytes 294920 | tf_op jit(solution)/shard_map/ppermute | solution.py:302
  48.0 0.0 collective-permute-done.13.refs_3_
  48.0 0.7 collective-permute-start.15
  48.7 0.0 collective-permute-done.2.refs_3_
  48.7 1.0 %collective-permute-start.4 = (f32[192,128]{1,0:T(8,128)S(1)}, f32[192,128]{1,0:T(8,128)}, u32[]{:S(2)}, u32[]{:S(2)}) collective-permute-start(f32[192,128]{1,0:T(8,128)S(1)} %collective-permute-done.2.refs_3_), channel_id=1, source_target_pairs={{0,8},{8,16},{16,24},{24,28},{28,20},{20,12},{12,4},{4,0},{1,9},{9... | collective-permute-start | bytes 294920 | tf_op jit(solution)/shard_map/ppermute | solution.py:299
  49.7 1.0 %collective-permute-done.3.refs_4_ = f32[192,128]{1,0:T(8,128)} collective-permute-done((f32[192,128]{1,0:T(8,128)S(1)}, f32[192,128]{1,0:T(8,128)}, u32[]{:S(2)}, u32[]{:S(2)}) %collective-permute-start.3) | collective-permute-done | bytes 98336 | tf_op jit(solution)/shard_map/ppermute | solution.py:302
  50.8 1.2 %collective-permute-start.10 = (f32[3,96,128]{2,1,0:T(8,128)}, f32[3,96,128]{2,1,0:T(8,128)S(1)}, u32[]{:S(2)}, u32[]{:S(2)}) collective-permute-start(f32[3,96,128]{2,1,0:T(8,128)} %copy-done.7), channel_id=1, source_target_pairs={{1,0},{2,1},{3,2},{0,3},{5,4},{6,5},{7,6},{4,7},{9,8},{10,9},{11,1... | collective-permute-start | bytes 442376 | tf_op jit(solution)/shard_map/ppermute | solution.py:284
  52.0 0.8 collective-permute-done.16.refs_6_
  52.8 0.6 copy-done.5
  53.4 1.0 %collective-permute-start.5 = (f32[192,128]{1,0:T(8,128)}, f32[192,128]{1,0:T(8,128)}, u32[]{:S(2)}, u32[]{:S(2)}) collective-permute-start(f32[192,128]{1,0:T(8,128)} %collective-permute-done.3.refs_4_), channel_id=1, source_target_pairs={{8,0},{16,8},{24,16},{28,24},{20,28},{12,20},{4,12},{0,4},{9,1},{1... | collective-permute-start | bytes 294920 | tf_op jit(solution)/shard_map/ppermute | solution.py:302
  54.4 0.0 collective-permute-done.15.refs_5_
  54.4 1.0 %collective-permute-start.17 = (f32[192,128]{1,0:T(8,128)}, f32[192,128]{1,0:T(8,128)}, u32[]{:S(2)}, u32[]{:S(2)}) collective-permute-start(f32[192,128]{1,0:T(8,128)} %collective-permute-done.15.refs_5_), channel_id=1, source_target_pairs={{0,8},{8,16},{16,24},{24,28},{28,20},{20,12},{12,4},{4,0},{1,9},{9... | collective-permute-start | bytes 294920 | tf_op jit(solution)/shard_map/ppermute | solution.py:299
  55.4 0.4 collective-permute-done.4.refs_5_
  55.8 0.7 collective-permute-start.6
  56.5 0.0 copy-done.8
  56.5 0.6 gather_fusion
  57.2 3.3 %collective-permute-done.17.refs_7_ = f32[192,128]{1,0:T(8,128)} collective-permute-done((f32[192,128]{1,0:T(8,128)}, f32[192,128]{1,0:T(8,128)}, u32[]{:S(2)}, u32[]{:S(2)}) %collective-permute-start.17) | collective-permute-done | bytes 98336 | tf_op jit(solution)/shard_map/ppermute | solution.py:299
  60.4 0.9 copy-done.6
  61.3 1.5 %gather.9 = (f32[1536,128]{1,0:T(8,128)S(1)}, f32[96,128]{1,0:T(8,128)S(1)}, f32[96,128]{1,0:T(8,128)S(1)}) custom-call(s32[8]{0:T(128)S(1)} %gather_fusion, f32[192,128]{1,0:T(8,128)S(1)} %get-tuple-element.27.refs_0_, f32[192,128]{1,0:T(8,128)S(1)} %collective-permute-done.11.refs_1_, f32[192,128]{1,0:T(8,128)S(1)} %collective-permute-done.12.refs_2_, ...), custom_call_target="tpu_custom_call" | custom-call | tf_op jit(solution)/shard_map/gather/pallas_call | solution.py:321
  62.8 0.1 collective-permute-start.18
  62.9 0.0 collective-permute-done.5.refs_6_
  62.9 0.0 copy-start.3
  62.9 0.0 copy-start.4
  62.9 1.7 %collective-permute-start.19 = (f32[96,128]{1,0:T(8,128)S(1)}, f32[96,128]{1,0:T(8,128)S(1)}, u32[]{:S(2)}, u32[]{:S(2)}) collective-permute-start(f32[96,128]{1,0:T(8,128)S(1)} %get-tuple-element.26), channel_id=1, source_target_pairs={{1,0},{2,1},{3,2},{0,3},{5,4},{6,5},{7,6},{4,7},{9,8},{10,9},{11,1... | collective-permute-start | bytes 147464 | tf_op jit(solution)/shard_map/ppermute | solution.py:330
  64.6 0.0 collective-permute-done.6.refs_7_
  64.6 1.6 %gather.8 = (f32[1536,128]{1,0:T(8,128)S(1)}, f32[96,128]{1,0:T(8,128)S(1)}, f32[96,128]{1,0:T(8,128)S(1)}) custom-call(s32[8]{0:T(128)S(1)} %gather_fusion, f32[192,128]{1,0:T(8,128)S(1)} %get-tuple-element.28.refs_0_, f32[192,128]{1,0:T(8,128)S(1)} %collective-permute-done.refs_1_, f32[192,128]{1,0:T(8,128)S(1)} %collective-permute-done.1.refs_2_, ...), custom_call_target="tpu_custom_call" | custom-call | tf_op jit(solution)/shard_map/gather/pallas_call | solution.py:321
  66.2 0.1 collective-permute-start.7
  66.2 0.0 collective-permute-done.9.left
  66.3 1.7 %collective-permute-start.8 = (f32[96,128]{1,0:T(8,128)S(1)}, f32[96,128]{1,0:T(8,128)S(1)}, u32[]{:S(2)}, u32[]{:S(2)}) collective-permute-start(f32[96,128]{1,0:T(8,128)S(1)} %get-tuple-element.18), channel_id=1, source_target_pairs={{1,0},{2,1},{3,2},{0,3},{5,4},{6,5},{7,6},{4,7},{9,8},{10,9},{11,1... | collective-permute-start | bytes 147464 | tf_op jit(solution)/shard_map/ppermute | solution.py:330
  68.0 0.0 collective-permute-done.10.right
  68.0 3.0 %prepare.1 = (f32[8,96,128]{2,1,0:T(8,128)S(1)}, f32[16,96,128]{2,1,0:T(8,128)S(1)}, f32[8,96,128]{2,1,0:T(8,128)S(1)}) custom-call(f32[2,16,96,128]{3,2,1,0:T(8,128)S(1)} %copy-done, f32[16,96,128]{2,1,0:T(8,128)S(1)} %copy-done.2, f32[3,96,128]{2,1,0:T(8,128)S(1)} %collective-permute-done.9.left, f32[3,96,128]{2,1,0:T(8,128)S(1)} %collective-permute-done.10.right), custom_call_target="tpu_custom_call" | custom-call | tf_op jit(solution)/shard_map/prepare/pallas_call | solution.py:309
  71.0 0.0 collective-permute-done.18.left
  71.0 0.0 collective-permute-done.19.right
  71.0 9.7 %round.2.refs_0_ = f32[2,16,96,128]{3,2,1,0:T(8,128)S(1)} custom-call(f32[16,96,128]{2,1,0:T(8,128)S(1)} %bitcast.26, f32[96,128]{1,0:T(8,128)S(1)} %collective-permute-done.18.left, f32[96,128]{1,0:T(8,128)S(1)} %collective-permute-done.19.right, f32[2,16,96,128]{3,2,1,0:T(8,128)S(1)} %copy-done, f32[8,96,128]{2,1,0:T(8,128)S(1)} %get-tuple-element.21.trial_halo, ...), custom_call_target="tpu_custom_call" | custom-call | tf_op jit(solution)/shard_map/round/pallas_call | solution.py:335
  80.7 0.0 collective-permute-done.7.left
  80.7 0.0 collective-permute-done.8.right
  80.7 10.9 %round.3 = f32[2,16,96,128]{3,2,1,0:T(8,128)} custom-call(f32[16,96,128]{2,1,0:T(8,128)S(1)} %bitcast.27, f32[96,128]{1,0:T(8,128)S(1)} %collective-permute-done.7.left, f32[96,128]{1,0:T(8,128)S(1)} %collective-permute-done.8.right, f32[2,16,96,128]{3,2,1,0:T(8,128)S(1)} %copy-done, f32[8,96,128]{2,1,0:T(8,128)S(1)} %get-tuple-element.21.trial_halo, ...), custom_call_target="tpu_custom_call" | custom-call | tf_op jit(solution)/shard_map/round/pallas_call | solution.py:335
  (13 shorter events, 0.0 us)
Async XLA Ops:
  0.0 7.4 %copy-start.9 = (s32[2]{0:T(128)S(1)}, s32[2]{0:T(128)}, u32[]{:S(2)}) copy-start(s32[2]{0:T(128)} %param.11) | copy-start | bytes 28
  0.0 36.2 %copy-start = (f32[2,16,96,128]{3,2,1,0:T(8,128)S(1)}, f32[2,16,96,128]{3,2,1,0:T(8,128)}, u32[]{:S(2)}) copy-start(f32[2,16,96,128]{3,2,1,0:T(8,128)} %trial.7) | copy-start | bytes 4718596
  0.0 27.6 %all-to-all-start = ((f32[8,192,128]{2,1,0:T(8,128)}), f32[8,192,128]{2,1,0:T(8,128)S(1)}, u32[]{:S(2)}, u32[]{:S(2)}) async-start(f32[8,192,128]{2,1,0:T(8,128)} %bitcast.28), calls=%async_computation | async-start | bytes 1572864 | tf_op jit(solution)/shard_map/all_to_all | solution.py:286
  7.4 32.3 %copy-start.10 = (s32[8]{0:T(128)S(1)}, s32[8]{0:T(128)}, u32[]{:S(2)}) copy-start(s32[8]{0:T(128)} %constant.83.clone) | copy-start | bytes 100
  7.4 49.1 %copy-start.8 = (s32[8]{0:T(128)S(1)}, s32[8]{0:T(128)}, u32[]{:S(2)}) copy-start(s32[8]{0:T(128)} %constant.82.clone) | copy-start | bytes 100
  27.6 5.4 %collective-permute-start.12 = (f32[192,128]{1,0:T(8,128)S(1)}, f32[192,128]{1,0:T(8,128)S(1)}, u32[]{:S(2)}, u32[]{:S(2)}) collective-permute-start(f32[192,128]{1,0:T(8,128)S(1)} %get-tuple-element.27.refs_0_), channel_id=1, source_target_pairs={{8,0},{16,8},{24,16},{28,24},{20,28},{12,20},{4,12},{0,4},{9,1},{1... | collective-permute-start | bytes 294920 | tf_op jit(solution)/shard_map/ppermute | solution.py:302
  29.1 5.4 %collective-permute-start.11 = (f32[192,128]{1,0:T(8,128)S(1)}, f32[192,128]{1,0:T(8,128)S(1)}, u32[]{:S(2)}, u32[]{:S(2)}) collective-permute-start(f32[192,128]{1,0:T(8,128)S(1)} %get-tuple-element.27.refs_0_), channel_id=1, source_target_pairs={{0,8},{8,16},{16,24},{24,28},{28,20},{20,12},{12,4},{4,0},{1,9},{9... | collective-permute-start | bytes 294920 | tf_op jit(solution)/shard_map/ppermute | solution.py:299
  29.7 5.5 %collective-permute-start = (f32[192,128]{1,0:T(8,128)S(1)}, f32[192,128]{1,0:T(8,128)S(1)}, u32[]{:S(2)}, u32[]{:S(2)}) collective-permute-start(f32[192,128]{1,0:T(8,128)S(1)} %get-tuple-element.28.refs_0_), channel_id=1, source_target_pairs={{0,8},{8,16},{16,24},{24,28},{28,20},{20,12},{12,4},{4,0},{1,9},{9... | collective-permute-start | bytes 294920 | tf_op jit(solution)/shard_map/ppermute | solution.py:299
  30.0 15.6 %collective-permute-start.1 = (f32[192,128]{1,0:T(8,128)S(1)}, f32[192,128]{1,0:T(8,128)S(1)}, u32[]{:S(2)}, u32[]{:S(2)}) collective-permute-start(f32[192,128]{1,0:T(8,128)S(1)} %get-tuple-element.28.refs_0_), channel_id=1, source_target_pairs={{8,0},{16,8},{24,16},{28,24},{20,28},{12,20},{4,12},{0,4},{9,1},{1... | collective-permute-start | bytes 294920 | tf_op jit(solution)/shard_map/ppermute | solution.py:302
  33.0 13.7 %collective-permute-start.14 = (f32[192,128]{1,0:T(8,128)S(1)}, f32[192,128]{1,0:T(8,128)S(1)}, u32[]{:S(2)}, u32[]{:S(2)}) collective-permute-start(f32[192,128]{1,0:T(8,128)S(1)} %collective-permute-done.12.refs_2_), channel_id=1, source_target_pairs={{8,0},{16,8},{24,16},{28,24},{20,28},{12,20},{4,12},{0,4},{9,1},{1... | collective-permute-start | bytes 294920 | tf_op jit(solution)/shard_map/ppermute | solution.py:302
  34.5 13.5 %collective-permute-start.13 = (f32[192,128]{1,0:T(8,128)S(1)}, f32[192,128]{1,0:T(8,128)S(1)}, u32[]{:S(2)}, u32[]{:S(2)}) collective-permute-start(f32[192,128]{1,0:T(8,128)S(1)} %collective-permute-done.11.refs_1_), channel_id=1, source_target_pairs={{0,8},{8,16},{16,24},{24,28},{28,20},{20,12},{12,4},{4,0},{1,9},{9... | collective-permute-start | bytes 294920 | tf_op jit(solution)/shard_map/ppermute | solution.py:299
  35.2 13.5 %collective-permute-start.2 = (f32[192,128]{1,0:T(8,128)S(1)}, f32[192,128]{1,0:T(8,128)S(1)}, u32[]{:S(2)}, u32[]{:S(2)}) collective-permute-start(f32[192,128]{1,0:T(8,128)S(1)} %collective-permute-done.refs_1_), channel_id=1, source_target_pairs={{0,8},{8,16},{16,24},{24,28},{28,20},{20,12},{12,4},{4,0},{1,9},{9... | collective-permute-start | bytes 294920 | tf_op jit(solution)/shard_map/ppermute | solution.py:299
  36.2 1.1 %copy-start.1 = (f32[16,96,128]{2,1,0:T(8,128)S(1)}, f32[16,96,128]{2,1,0:T(8,128)}, u32[]{:S(2)}) copy-start(f32[16,96,128]{2,1,0:T(8,128)} %potential.3) | copy-start | bytes 2359300
  39.1 0.6 copy-start.7
  39.7 28.3 %copy-start.2 = (f32[16,96,128]{2,1,0:T(8,128)S(1)}, f32[16,96,128]{2,1,0:T(8,128)}, u32[]{:S(2)}) copy-start(f32[16,96,128]{2,1,0:T(8,128)} %potential.3) | copy-start | bytes 2359300
  39.7 26.5 %collective-permute-start.9 = (f32[3,96,128]{2,1,0:T(8,128)}, f32[3,96,128]{2,1,0:T(8,128)S(1)}, u32[]{:S(2)}, u32[]{:S(2)}) collective-permute-start(f32[3,96,128]{2,1,0:T(8,128)} %get-tuple-element.19), channel_id=1, source_target_pairs={{0,1},{1,2},{2,3},{3,0},{4,5},{5,6},{6,7},{7,4},{8,9},{9,10},{10,1... | collective-permute-start | bytes 442376 | tf_op jit(solution)/shard_map/ppermute | solution.py:283
  45.6 5.2 %collective-permute-start.3 = (f32[192,128]{1,0:T(8,128)S(1)}, f32[192,128]{1,0:T(8,128)}, u32[]{:S(2)}, u32[]{:S(2)}) collective-permute-start(f32[192,128]{1,0:T(8,128)S(1)} %collective-permute-done.1.refs_2_), channel_id=1, source_target_pairs={{8,0},{16,8},{24,16},{28,24},{20,28},{12,20},{4,12},{0,4},{9,1},{1... | collective-permute-start | bytes 294920 | tf_op jit(solution)/shard_map/ppermute | solution.py:302
  46.7 6.1 %collective-permute-start.16 = (f32[192,128]{1,0:T(8,128)S(1)}, f32[192,128]{1,0:T(8,128)S(1)}, u32[]{:S(2)}, u32[]{:S(2)}) collective-permute-start(f32[192,128]{1,0:T(8,128)S(1)} %collective-permute-done.14.refs_4_), channel_id=1, source_target_pairs={{8,0},{16,8},{24,16},{28,24},{20,28},{12,20},{4,12},{0,4},{9,1},{1... | collective-permute-start | bytes 294920 | tf_op jit(solution)/shard_map/ppermute | solution.py:302
  48.0 6.4 %collective-permute-start.15 = (f32[192,128]{1,0:T(8,128)S(1)}, f32[192,128]{1,0:T(8,128)}, u32[]{:S(2)}, u32[]{:S(2)}) collective-permute-start(f32[192,128]{1,0:T(8,128)S(1)} %collective-permute-done.13.refs_3_), channel_id=1, source_target_pairs={{0,8},{8,16},{16,24},{24,28},{28,20},{20,12},{12,4},{4,0},{1,9},{9... | collective-permute-start | bytes 294920 | tf_op jit(solution)/shard_map/ppermute | solution.py:299
  48.7 7.1 %collective-permute-start.4 = (f32[192,128]{1,0:T(8,128)S(1)}, f32[192,128]{1,0:T(8,128)}, u32[]{:S(2)}, u32[]{:S(2)}) collective-permute-start(f32[192,128]{1,0:T(8,128)S(1)} %collective-permute-done.2.refs_3_), channel_id=1, source_target_pairs={{0,8},{8,16},{16,24},{24,28},{28,20},{20,12},{12,4},{4,0},{1,9},{9... | collective-permute-start | bytes 294920 | tf_op jit(solution)/shard_map/ppermute | solution.py:299
  50.8 17.2 %collective-permute-start.10 = (f32[3,96,128]{2,1,0:T(8,128)}, f32[3,96,128]{2,1,0:T(8,128)S(1)}, u32[]{:S(2)}, u32[]{:S(2)}) collective-permute-start(f32[3,96,128]{2,1,0:T(8,128)} %copy-done.7), channel_id=1, source_target_pairs={{1,0},{2,1},{3,2},{0,3},{5,4},{6,5},{7,6},{4,7},{9,8},{10,9},{11,1... | collective-permute-start | bytes 442376 | tf_op jit(solution)/shard_map/ppermute | solution.py:284
  52.8 0.6 copy-start.5
  53.4 9.5 %collective-permute-start.5 = (f32[192,128]{1,0:T(8,128)}, f32[192,128]{1,0:T(8,128)}, u32[]{:S(2)}, u32[]{:S(2)}) collective-permute-start(f32[192,128]{1,0:T(8,128)} %collective-permute-done.3.refs_4_), channel_id=1, source_target_pairs={{8,0},{16,8},{24,16},{28,24},{20,28},{12,20},{4,12},{0,4},{9,1},{1... | collective-permute-start | bytes 294920 | tf_op jit(solution)/shard_map/ppermute | solution.py:302
  54.4 6.0 %collective-permute-start.17 = (f32[192,128]{1,0:T(8,128)}, f32[192,128]{1,0:T(8,128)}, u32[]{:S(2)}, u32[]{:S(2)}) collective-permute-start(f32[192,128]{1,0:T(8,128)} %collective-permute-done.15.refs_5_), channel_id=1, source_target_pairs={{0,8},{8,16},{16,24},{24,28},{28,20},{20,12},{12,4},{4,0},{1,9},{9... | collective-permute-start | bytes 294920 | tf_op jit(solution)/shard_map/ppermute | solution.py:299
  55.8 8.8 %collective-permute-start.6 = (f32[192,128]{1,0:T(8,128)}, f32[192,128]{1,0:T(8,128)}, u32[]{:S(2)}, u32[]{:S(2)}) collective-permute-start(f32[192,128]{1,0:T(8,128)} %collective-permute-done.4.refs_5_), channel_id=1, source_target_pairs={{0,8},{8,16},{16,24},{24,28},{28,20},{20,12},{12,4},{4,0},{1,9},{9... | collective-permute-start | bytes 294920 | tf_op jit(solution)/shard_map/ppermute | solution.py:299
  60.4 0.9 copy-start.6
  62.8 8.2 %collective-permute-start.18 = (f32[96,128]{1,0:T(8,128)S(1)}, f32[96,128]{1,0:T(8,128)S(1)}, u32[]{:S(2)}, u32[]{:S(2)}) collective-permute-start(f32[96,128]{1,0:T(8,128)S(1)} %get-tuple-element.25), channel_id=1, source_target_pairs={{0,1},{1,2},{2,3},{3,0},{4,5},{5,6},{6,7},{7,4},{8,9},{9,10},{10,1... | collective-permute-start | bytes 147464 | tf_op jit(solution)/shard_map/ppermute | solution.py:329
  62.9 8.1 %copy-start.3 = (bf16[2,768,256]{2,1,0:T(8,128)(2,1)S(1)}, bf16[2,768,256]{2,1,0:T(8,128)(2,1)}, u32[]{:S(2)}) copy-start(bf16[2,768,256]{2,1,0:T(8,128)(2,1)} %constant.84.clone.bands) | copy-start | bytes 2359300
  62.9 8.1 %copy-start.4 = (bf16[256,128]{1,0:T(8,128)(2,1)S(1)}, bf16[256,128]{1,0:T(8,128)(2,1)}, u32[]{:S(2)}) copy-start(bf16[256,128]{1,0:T(8,128)(2,1)} %constant.85.clone.halo_bands) | copy-start | bytes 196612
  62.9 8.1 %collective-permute-start.19 = (f32[96,128]{1,0:T(8,128)S(1)}, f32[96,128]{1,0:T(8,128)S(1)}, u32[]{:S(2)}, u32[]{:S(2)}) collective-permute-start(f32[96,128]{1,0:T(8,128)S(1)} %get-tuple-element.26), channel_id=1, source_target_pairs={{1,0},{2,1},{3,2},{0,3},{5,4},{6,5},{7,6},{4,7},{9,8},{10,9},{11,1... | collective-permute-start | bytes 147464 | tf_op jit(solution)/shard_map/ppermute | solution.py:330
  66.2 14.5 %collective-permute-start.7 = (f32[96,128]{1,0:T(8,128)S(1)}, f32[96,128]{1,0:T(8,128)S(1)}, u32[]{:S(2)}, u32[]{:S(2)}) collective-permute-start(f32[96,128]{1,0:T(8,128)S(1)} %get-tuple-element.17), channel_id=1, source_target_pairs={{0,1},{1,2},{2,3},{3,0},{4,5},{5,6},{6,7},{7,4},{8,9},{9,10},{10,1... | collective-permute-start | bytes 147464 | tf_op jit(solution)/shard_map/ppermute | solution.py:329
  66.3 14.5 %collective-permute-start.8 = (f32[96,128]{1,0:T(8,128)S(1)}, f32[96,128]{1,0:T(8,128)S(1)}, u32[]{:S(2)}, u32[]{:S(2)}) collective-permute-start(f32[96,128]{1,0:T(8,128)S(1)} %get-tuple-element.18), channel_id=1, source_target_pairs={{1,0},{2,1},{3,2},{0,3},{5,4},{6,5},{7,6},{4,7},{9,8},{10,9},{11,1... | collective-permute-start | bytes 147464 | tf_op jit(solution)/shard_map/ppermute | solution.py:330

commit v3 on v2

--- a/solution.py
+++ b/solution.py
@@ -71,15 +71,38 @@
         scaled[y] = 6.0 * potential[y] - 6.0
 
 
-def gather_kernel(count, rows, where, *refs):
-    blocks, (whole, last, first) = refs[:count], refs[count:]
-    nz = last.shape[0]
-    ny = whole.shape[0] // nz
-    for k in range(count):
-        whole[pl.ds(pl.multiple_of(where[k] * rows, 8), rows), :] = blocks[k][...]
+def ring_of(n):
+    return [*range(0, n, 2), *range(n - 1 - n % 2, 0, -2)]
+
+
+def gather_kernel(n, rounds, *refs):
+    blocks, (whole, last, first) = refs[:-3], refs[-3:]
+    nz = last.shape[1]
+    ny = whole.shape[1] // nz
+    evens = (n + 1) // 2
+    me = lax.axis_index("cols")
+    spot = jnp.where(me % 2 == 0, me // 2, n - 1 - me // 2)
+    rows = blocks[0].shape[1]
+
+    def place(shift):
+        position = lax.rem(spot + shift + n, n)
+        device = jnp.where(position < evens, 2 * position, 2 * (n - 1 - position) + 1)
+        return device * rows
+
+    def put(block, start):
+        size = block.shape[1]
+        for r in range(rounds):
+            whole[r, pl.ds(pl.multiple_of(start, 8), size), :] = block[r]
+
+    put(blocks[0], place(0))
+    for k, block in enumerate(blocks[1:]):
+        step, ahead = k // 2 + 1, k % 2 == 0
+        start = place(-step if ahead else step)
+        put(block, start if ahead or block.shape[1] == rows else start + rows - block.shape[1])
     lane = lanes(nz)
-    last[...] = pack_edges(lambda y: whole[y * nz : (y + 1) * nz], ny, lane, False)
-    first[...] = pack_edges(lambda y: whole[y * nz : (y + 1) * nz], ny, lane, True)
+    for r in range(rounds):
+        last[r] = pack_edges(lambda y: whole[r, y * nz : (y + 1) * nz], ny, lane, False)
+        first[r] = pack_edges(lambda y: whole[r, y * nz : (y + 1) * nz], ny, lane, True)
 
 
 def clear_borders(ref, ny, nz):
@@ -145,8 +168,9 @@
     )
 
 
-def round_kernel(adds, psi, left, right, trial, trial_halo, scaled, scaled_halo, bands, halo_bands, *refs):
-    if adds:
+def round_kernel(turn, psi, left, right, trial, trial_halo, scaled, scaled_halo, bands, halo_bands, *refs):
+    psi, left, right = psi.at[turn], left.at[turn], right.at[turn]
+    if turn:
         total, *refs = refs
     out, w, u, v, w_halo, u_halo, v_halo, pieces, sums, halo_sums = refs
     columns, ny, nz, _ = trial.shape
@@ -234,7 +258,7 @@
 
     def finish(c, y, z, value):
         term = (FINAL * psi[y, pl.ds(z, CHUNK)]) * value
-        if adds:
+        if turn:
             term = term + total[c, y, pl.ds(z, CHUNK)]
         out[c, y, pl.ds(z, CHUNK)] = term
 
@@ -258,10 +282,6 @@
 
 def f32(*shape):
     return jax.ShapeDtypeStruct(shape, jnp.float32)
-
-
-def ring_of(n):
-    return [*range(0, n, 2), *range(n - 1 - n % 2, 0, -2)]
 
 
 def body(trial, orbitals, potential, owner):
@@ -284,29 +304,7 @@
     right = lax.ppermute(first, "sec", sec_down)
 
     mine = lax.all_to_all(orbitals.reshape(n, rows, nx), "cols", 0, 0)
-    ring = ring_of(n)
-    order = jnp.array(ring, jnp.int32)
-    spot = jnp.array([ring.index(i) for i in range(n)], jnp.int32)[lax.axis_index("cols")]
-    clockwise = [(ring[i], ring[(i + 1) % n]) for i in range(n)]
-    counter = [(j, i) for i, j in clockwise]
-
-    own = [lax.dynamic_index_in_dim(mine, owner[r], 0, False) for r in range(rounds)]
-    ahead, behind = list(own), list(own)
-    blocks = [[own[r]] for r in range(rounds)]
-    places = [spot]
-    for step in range(1, n // 2 + 1):
-        for r in range(rounds):
-            ahead[r] = lax.ppermute(ahead[r], "cols", clockwise)
-            blocks[r].append(ahead[r])
-            if 2 * step < n:
-                behind[r] = lax.ppermute(behind[r], "cols", counter)
-                blocks[r].append(behind[r])
-        places.append((spot - step) % n)
-        if 2 * step < n:
-            places.append((spot + step) % n)
-    where = order[jnp.stack(places)]
-
-    trial_halo, scaled, scaled_halo = pl.pallas_call(
+    prepared = pl.pallas_call(
         prepare_kernel,
         out_shape=[f32(ny // 2, nz, nx), f32(ny, nz, nx), f32(ny // 2, nz, nx)],
         in_specs=vmem(4),
@@ -314,26 +312,39 @@
         compiler_params=params(10),
         name="prepare",
     )(trial, potential, left, right)
-
+    mine, (trial_halo, scaled, scaled_halo) = lax.optimization_barrier((mine, prepared))
+
+    ring = ring_of(n)
+    clockwise = [(ring[i], ring[(i + 1) % n]) for i in range(n)]
+    counter = [(j, i) for i, j in clockwise]
+    own = jnp.concatenate([lax.dynamic_slice_in_dim(mine, owner[r], 1, 0) for r in range(rounds)])
+    ahead = behind = own
+    blocks = [own]
+    for step in range(1, n // 2 + 1):
+        if 2 * step == n:
+            cut = rows // 16 * 8
+            ahead, behind = ahead[:, :cut], behind[:, cut:]
+        ahead = lax.ppermute(ahead, "cols", clockwise)
+        behind = lax.ppermute(behind, "cols", counter)
+        blocks += [ahead, behind]
+
+    psi, psi_last, psi_first = pl.pallas_call(
+        functools.partial(gather_kernel, n, rounds),
+        out_shape=[f32(rounds, ny * nz, nx), f32(rounds, nz, nx), f32(rounds, nz, nx)],
+        in_specs=vmem(len(blocks)),
+        out_specs=vmem(3),
+        compiler_params=params(10),
+        name="gather",
+    )(*blocks)
+    psi = psi.reshape(rounds, ny, nz, nx)
+    psi_left = lax.ppermute(psi_last, "sec", sec_up)
+    psi_right = lax.ppermute(psi_first, "sec", sec_down)
     total = None
-    sections = []
-    for r in range(rounds):
-        psi, psi_last, psi_first = pl.pallas_call(
-            functools.partial(gather_kernel, n, rows),
-            out_shape=[f32(ny * nz, nx), f32(nz, nx), f32(nz, nx)],
-            in_specs=[pl.BlockSpec(memory_space=pltpu.SMEM)] + vmem(n),
-            out_specs=vmem(3),
-            compiler_params=params(6),
-            name="gather",
-        )(where, *blocks[r])
-        psi_left = lax.ppermute(psi_last, "sec", sec_up)
-        psi_right = lax.ppermute(psi_first, "sec", sec_down)
-        sections.append((psi.reshape(ny, nz, nx), psi_left, psi_right))
     matrices = bands()
     for r in range(rounds):
-        given = [*sections[r], trial, trial_halo, scaled, scaled_halo, *matrices] + ([total] if r else [])
+        given = [psi, psi_left, psi_right, trial, trial_halo, scaled, scaled_halo, *matrices] + ([total] if r else [])
         total = pl.pallas_call(
-            functools.partial(round_kernel, r > 0),
+            functools.partial(round_kernel, r),
             out_shape=f32(columns, ny, nz, nx),
             in_specs=vmem(len(given)),
             out_specs=pl.BlockSpec(memory_space=pltpu.VMEM),

time: 92.1 us -> 80.7 us (0.88); the launches traced: 91.7 us -> 79.3 us
  starting transfers between devices: 26.1 us -> 19.3 us
  between operations: 8.34 us -> 4.13 us
  Pallas kernels: 28.4 us -> 25.7 us
    all_to_all x1, waiting for transfers between devices: 15.9 us -> 4.53 us  [body(): mine = lax.all_to_all(orbitals.reshape(n, rows, nx), 'cols', 0, 0)]
    ppermute x14 -> x8, waiting for transfers between devices: 6.96 us -> 16.5 us  [the longest x4 15.3 us: body(): behind = lax.ppermute(behind, 'cols', counter)]
    ppermute x14 -> x8, starting transfers between devices: 14 us -> 8.26 us  [the longest x4 5.35 us: body(): behind = lax.ppermute(behind, 'cols', counter)]
    ppermute x2 -> x1, waiting for transfers between devices: 0.01 us -> 2.3 us  [body(): psi_left = lax.ppermute(psi_last, 'sec', sec_up)]
    pallas_call x4 -> x3, Pallas kernels: 23.7 us -> 21.5 us  [the longest x2 20.6 us: body(): pl.pallas_call(functools.partial(round_kernel, r), out_shape=f32(columns,...]
    ppermute x2 -> x1, starting transfers between devices: 3.43 us -> 1.73 us  [body(): psi_right = lax.ppermute(psi_first, 'sec', sec_down)]
    unnamed x22 -> x24, local copies, waits for them, and re-layouts: 3.34 us -> 5.02 us
  transfers between devices with their start and end apart: 21 -> 13, of which waited for: 7 -> 8; matrix products, arithmetic and copies ran while one was open for 3% -> 1% of each run, Pallas kernels for 19% -> 5%
where the time goes in v3:
time: 80.7 us; the launch traced here: 79.3 us
  Pallas kernels  25.7 us (32%)
  waiting for transfers between devices  23.4 us (29%)
  starting transfers between devices  19.3 us (24%)
  local copies, waits for them, and re-layouts  6.7 us (8%)
  between operations  4.13 us (5%)
    pallas_call x2, Pallas kernels, body(): pl.pallas_call(functools.partial(round_kernel, r), out_shape=f32(columns,...  20.6 us
    ppermute x4, waiting for transfers between devices, body(): behind = lax.ppermute(behind, 'cols', counter)  15.3 us
    all_to_all x1, starting transfers between devices, body(): mine = lax.all_to_all(orbitals.reshape(n, rows, nx), 'cols', 0, 0)  7.41 us
    ppermute x4, starting transfers between devices, body(): behind = lax.ppermute(behind, 'cols', counter)  5.35 us
    unnamed x24, local copies, waits for them, and re-layouts  5.02 us
    all_to_all x1, waiting for transfers between devices, body(): mine = lax.all_to_all(orbitals.reshape(n, rows, nx), 'cols', 0, 0)  4.53 us
    pallas_call x1, Pallas kernels, body(): pl.pallas_call(prepare_kernel, out_shape=[f32(ny // 2, nz, nx), f32(ny, n...  2.96 us
    ppermute x4, starting transfers between devices, body(): ahead = lax.ppermute(ahead, 'cols', clockwise)  2.91 us
  transfers between devices with their start and end apart: 13, of which 8 were waited for; matrix products, arithmetic and copies ran while one was open for 1% of the time, Pallas kernels for 5%

profile of v3, /device:TPU:0, one launch (start us, length us, event | category | flops | bytes accessed | tf_op | source)
XLA Modules:
  0.0 79.3 jit_solution(590128748401306002)
XLA Ops:
  0.0 0.0 copy-start
  0.0 7.4 %all-to-all-start = ((f32[8,192,128]{2,1,0:T(8,128)}), f32[8,192,128]{2,1,0:T(8,128)}, u32[]{:S(2)}, u32[]{:S(2)}) async-start(f32[8,192,128]{2,1,0:T(8,128)} %bitcast.6), calls=%async_computation | async-start | bytes 1572864 | tf_op jit(solution)/shard_map/all_to_all | solution.py:306
  7.4 0.0 copy-done
  7.4 0.0 copy-start.2
  7.4 1.1 %copy-done.2 = f32[16,96,128]{2,1,0:T(8,128)S(1)} copy-done((f32[16,96,128]{2,1,0:T(8,128)S(1)}, f32[16,96,128]{2,1,0:T(8,128)}, u32[]{:S(2)}) %copy-start.2) | copy-done | bytes 786456
  8.6 0.0 copy-start.11
  8.6 0.0 copy-start.3
  8.6 1.2 %pack.1 = (f32[3,96,128]{2,1,0:T(8,128)S(1)}, f32[3,96,128]{2,1,0:T(8,128)S(1)}) custom-call(f32[2,16,96,128]{3,2,1,0:T(8,128)S(1)} %copy-done, f32[16,96,128]{2,1,0:T(8,128)S(1)} %copy-done.2), custom_call_target="tpu_custom_call" | custom-call | tf_op jit(solution)/shard_map/pack/pallas_call | solution.py:295
  9.8 0.1 collective-permute-start
  9.9 1.7 %collective-permute-start.1 = (f32[3,96,128]{2,1,0:T(8,128)S(1)}, f32[3,96,128]{2,1,0:T(8,128)S(1)}, u32[]{:S(2)}, u32[]{:S(2)}) collective-permute-start(f32[3,96,128]{2,1,0:T(8,128)S(1)} %get-tuple-element.18), channel_id=1, source_target_pairs={{1,0},{2,1},{3,2},{0,3},{5,4},{6,5},{7,6},{4,7},{9,8},{10,9},{11,1... | collective-permute-start | bytes 442376 | tf_op jit(solution)/shard_map/ppermute | solution.py:304
  11.6 0.0 copy-done.11
  11.6 0.7 fusion
  16.3 0.0 collective-permute-done.left
  16.3 0.0 copy-start.7
  16.3 0.7 copy-done.7
  17.0 0.0 collective-permute-done.1.right
  17.0 0.0 copy-start.9
  17.0 0.7 copy-done.9
  17.6 0.0 copy-done.3
  17.6 0.0 copy-start.8
  17.6 0.9 %copy-done.8 = f32[3,96,128]{2,1,0:T(8,128)S(1)} copy-done((f32[3,96,128]{2,1,0:T(8,128)S(1)}, f32[3,96,128]{2,1,0:T(8,128)}, u32[]{:S(2)}) %copy-start.8) | copy-done | bytes 147480
  18.5 0.0 copy-start.10
  18.5 0.9 %copy-done.10 = f32[3,96,128]{2,1,0:T(8,128)S(1)} copy-done((f32[3,96,128]{2,1,0:T(8,128)S(1)}, f32[3,96,128]{2,1,0:T(8,128)}, u32[]{:S(2)}) %copy-start.10) | copy-done | bytes 147480
  19.4 3.0 %prepare.1 = (f32[8,96,128]{2,1,0:T(8,128)S(1)}, f32[16,96,128]{2,1,0:T(8,128)S(1)}, f32[8,96,128]{2,1,0:T(8,128)S(1)}) custom-call(f32[2,16,96,128]{3,2,1,0:T(8,128)S(1)} %copy-done, f32[16,96,128]{2,1,0:T(8,128)S(1)} %copy-done.3, f32[3,96,128]{2,1,0:T(8,128)S(1)} %copy-done.8, f32[3,96,128]{2,1,0:T(8,128)S(1)} %copy-done.10), custom_call_target="tpu_custom_call" | custom-call | tf_op jit(solution)/shard_map/prepare/pallas_call | solution.py:307
  22.4 0.0 copy-start.4
  22.4 0.7 copy-done.4
  23.2 0.0 copy-start.1
  23.2 4.5 %all-to-all-done = f32[8,192,128]{2,1,0:T(8,128)} async-done(((f32[8,192,128]{2,1,0:T(8,128)}), f32[8,192,128]{2,1,0:T(8,128)}, u32[]{:S(2)}, u32[]{:S(2)}) %all-to-all-start) | async-done | bytes 786464 | tf_op jit(solution)/shard_map/all_to_all | solution.py:306
  27.7 0.0 copy-start.5
  27.7 0.0 copy-start.6
  27.7 1.0 %constant_dynamic-slice_fusion.1 = (f32[1,192,128]{2,1,0:T(8,128)S(1)}, f32[1,192,128]{2,1,0:T(8,128)S(1)}) fusion(f32[8,192,128]{2,1,0:T(8,128)} %all-to-all-done, s32[]{:T(128)S(6)} %select_n.6, s32[]{:T(128)S(6)} %select_n.7), kind=kLoop, calls=%fused_computation.2 | loop fusion | bytes 393224 | tf_op jit(solution)/shard_map/dynamic_slice | solution.py:320
  28.7 1.4 %collective-permute-start.3 = (f32[2,192,128]{2,1,0:T(8,128)S(1)}, f32[2,192,128]{2,1,0:T(8,128)S(1)}, u32[]{:S(2)}, u32[]{:S(2)}) collective-permute-start(f32[2,192,128]{2,1,0:T(8,128)S(1)} %pad_maximum_fusion.refs_0_), channel_id=1, source_target_pairs={{8,0},{16,8},{24,16},{28,24},{20,28},{12,20},{4,12},{0,4},{9,1},{1... | collective-permute-start | bytes 589832 | tf_op jit(solution)/shard_map/ppermute | solution.py:328
  30.2 0.6 collective-permute-start.2
  30.8 3.6 %collective-permute-done.3.refs_2_ = f32[2,192,128]{2,1,0:T(8,128)S(1)} collective-permute-done((f32[2,192,128]{2,1,0:T(8,128)S(1)}, f32[2,192,128]{2,1,0:T(8,128)S(1)}, u32[]{:S(2)}, u32[]{:S(2)}) %collective-permute-start.3) | collective-permute-done | bytes 196640 | tf_op jit(solution)/shard_map/ppermute | solution.py:328
  34.5 1.6 %collective-permute-start.5 = (f32[2,192,128]{2,1,0:T(8,128)S(1)}, f32[2,192,128]{2,1,0:T(8,128)S(1)}, u32[]{:S(2)}, u32[]{:S(2)}) collective-permute-start(f32[2,192,128]{2,1,0:T(8,128)S(1)} %collective-permute-done.3.refs_2_), channel_id=1, source_target_pairs={{8,0},{16,8},{24,16},{28,24},{20,28},{12,20},{4,12},{0,4},{9,1},{1... | collective-permute-start | bytes 589832 | tf_op jit(solution)/shard_map/ppermute | solution.py:328
  36.1 0.0 collective-permute-done.2.refs_1_
  36.1 0.4 collective-permute-start.4
  36.5 4.5 %collective-permute-done.5.refs_4_ = f32[2,192,128]{2,1,0:T(8,128)S(1)} collective-permute-done((f32[2,192,128]{2,1,0:T(8,128)S(1)}, f32[2,192,128]{2,1,0:T(8,128)S(1)}, u32[]{:S(2)}, u32[]{:S(2)}) %collective-permute-start.5) | collective-permute-done | bytes 196640 | tf_op jit(solution)/shard_map/ppermute | solution.py:328
  41.0 1.1 %collective-permute-start.7 = (f32[2,192,128]{2,1,0:T(8,128)S(1)}, f32[2,192,128]{2,1,0:T(8,128)S(1)}, u32[]{:S(2)}, u32[]{:S(2)}) collective-permute-start(f32[2,192,128]{2,1,0:T(8,128)S(1)} %collective-permute-done.5.refs_4_), channel_id=1, source_target_pairs={{8,0},{16,8},{24,16},{28,24},{20,28},{12,20},{4,12},{0,4},{9,1},{1... | collective-permute-start | bytes 589832 | tf_op jit(solution)/shard_map/ppermute | solution.py:328
  42.1 0.0 collective-permute-done.4.refs_3_
  42.1 0.9 %collective-permute-start.6 = (f32[2,192,128]{2,1,0:T(8,128)S(1)}, f32[2,192,128]{2,1,0:T(8,128)S(1)}, u32[]{:S(2)}, u32[]{:S(2)}) collective-permute-start(f32[2,192,128]{2,1,0:T(8,128)S(1)} %collective-permute-done.4.refs_3_), channel_id=1, source_target_pairs={{0,8},{8,16},{16,24},{24,28},{28,20},{20,12},{12,4},{4,0},{1,9},{9... | collective-permute-start | bytes 589832 | tf_op jit(solution)/shard_map/ppermute | solution.py:327
  43.0 4.7 %collective-permute-done.7.refs_6_ = f32[2,192,128]{2,1,0:T(8,128)S(1)} collective-permute-done((f32[2,192,128]{2,1,0:T(8,128)S(1)}, f32[2,192,128]{2,1,0:T(8,128)S(1)}, u32[]{:S(2)}, u32[]{:S(2)}) %collective-permute-start.7) | collective-permute-done | bytes 196640 | tf_op jit(solution)/shard_map/ppermute | solution.py:328
  47.7 1.2 %collective-permute-start.9 = (f32[2,96,128]{2,1,0:T(8,128)S(1)}, f32[2,96,128]{2,1,0:T(8,128)S(1)}, u32[]{:S(2)}, u32[]{:S(2)}) collective-permute-start(f32[2,96,128]{2,1,0:T(8,128)S(1)} %slice.17), channel_id=1, source_target_pairs={{8,0},{16,8},{24,16},{28,24},{20,28},{12,20},{4,12},{0,4},{9,1},{1... | collective-permute-start | bytes 294920 | tf_op jit(solution)/shard_map/ppermute | solution.py:328
  48.9 0.0 collective-permute-done.6.refs_5_
  48.9 1.0 %collective-permute-start.8 = (f32[2,96,128]{2,1,0:T(8,128)S(1)}, f32[2,96,128]{2,1,0:T(8,128)S(1)}, u32[]{:S(2)}, u32[]{:S(2)}) collective-permute-start(f32[2,96,128]{2,1,0:T(8,128)S(1)} %slice.16), channel_id=1, source_target_pairs={{0,8},{8,16},{16,24},{24,28},{28,20},{20,12},{12,4},{4,0},{1,9},{9... | collective-permute-start | bytes 294920 | tf_op jit(solution)/shard_map/ppermute | solution.py:327
  49.8 2.5 %collective-permute-done.9.refs_8_ = f32[2,96,128]{2,1,0:T(8,128)S(1)} collective-permute-done((f32[2,96,128]{2,1,0:T(8,128)S(1)}, f32[2,96,128]{2,1,0:T(8,128)S(1)}, u32[]{:S(2)}, u32[]{:S(2)}) %collective-permute-start.9) | collective-permute-done | bytes 98336 | tf_op jit(solution)/shard_map/ppermute | solution.py:328
  52.4 1.2 %collective-permute-done.8.refs_7_ = f32[2,96,128]{2,1,0:T(8,128)S(1)} collective-permute-done((f32[2,96,128]{2,1,0:T(8,128)S(1)}, f32[2,96,128]{2,1,0:T(8,128)S(1)}, u32[]{:S(2)}, u32[]{:S(2)}) %collective-permute-start.8) | collective-permute-done | bytes 98336 | tf_op jit(solution)/shard_map/ppermute | solution.py:327
  53.5 1.0 %gather.1 = (f32[2,1536,128]{2,1,0:T(8,128)S(1)}, f32[2,96,128]{2,1,0:T(8,128)S(1)}, f32[2,96,128]{2,1,0:T(8,128)S(1)}) custom-call(f32[2,192,128]{2,1,0:T(8,128)S(1)} %pad_maximum_fusion.refs_0_, f32[2,192,128]{2,1,0:T(8,128)S(1)} %collective-permute-done.2.refs_1_, f32[2,192,128]{2,1,0:T(8,128)S(1)} %collective-permute-done.3.refs_2_, ...), custom_call_target="tpu_custom_call" | custom-call | tf_op jit(solution)/shard_map/gather/pallas_call | solution.py:331
  54.5 0.1 collective-permute-start.10
  54.6 1.7 %collective-permute-start.11 = (f32[2,96,128]{2,1,0:T(8,128)S(1)}, f32[2,96,128]{2,1,0:T(8,128)S(1)}, u32[]{:S(2)}, u32[]{:S(2)}) collective-permute-start(f32[2,96,128]{2,1,0:T(8,128)S(1)} %get-tuple-element.25), channel_id=1, source_target_pairs={{1,0},{2,1},{3,2},{0,3},{5,4},{6,5},{7,6},{4,7},{9,8},{10,9},{11,1... | collective-permute-start | bytes 294920 | tf_op jit(solution)/shard_map/ppermute | solution.py:341
  56.3 2.3 %collective-permute-done.10.left = f32[2,96,128]{2,1,0:T(8,128)S(1)} collective-permute-done((f32[2,96,128]{2,1,0:T(8,128)S(1)}, f32[2,96,128]{2,1,0:T(8,128)S(1)}, u32[]{:S(2)}, u32[]{:S(2)}) %collective-permute-start.10) | collective-permute-done | bytes 98336 | tf_op jit(solution)/shard_map/ppermute | solution.py:340
  58.6 0.1 collective-permute-done.11.right
  58.7 0.0 copy-done.1
  58.7 0.0 copy-done.5
  58.7 0.0 copy-done.6
  58.7 9.6 %round.2.refs_0_ = f32[2,16,96,128]{3,2,1,0:T(8,128)S(1)} custom-call(f32[2,16,96,128]{3,2,1,0:T(8,128)S(1)} %bitcast.4, f32[2,96,128]{2,1,0:T(8,128)S(1)} %collective-permute-done.10.left, f32[2,96,128]{2,1,0:T(8,128)S(1)} %collective-permute-done.11.right, f32[2,16,96,128]{3,2,1,0:T(8,128)S(1)} %copy-done, f32[8,96,128]{2,1,0:T(8,128)S(1)} %get-tuple-element.26.trial_halo, ...), custom_call_target="tpu_custom_call" | custom-call | tf_op jit(solution)/shard_map/round/pallas_call | solution.py:346
  68.4 10.9 %round.3 = f32[2,16,96,128]{3,2,1,0:T(8,128)} custom-call(f32[2,16,96,128]{3,2,1,0:T(8,128)S(1)} %bitcast.5, f32[2,96,128]{2,1,0:T(8,128)S(1)} %collective-permute-done.10.left, f32[2,96,128]{2,1,0:T(8,128)S(1)} %collective-permute-done.11.right, f32[2,16,96,128]{3,2,1,0:T(8,128)S(1)} %copy-done, f32[8,96,128]{2,1,0:T(8,128)S(1)} %get-tuple-element.26.trial_halo, ...), custom_call_target="tpu_custom_call" | custom-call | tf_op jit(solution)/shard_map/round/pallas_call | solution.py:346
  (3 shorter events, 0.0 us)
Async XLA Ops:
  0.0 7.4 %copy-start = (f32[2,16,96,128]{3,2,1,0:T(8,128)S(1)}, f32[2,16,96,128]{3,2,1,0:T(8,128)}, u32[]{:S(2)}) copy-start(f32[2,16,96,128]{3,2,1,0:T(8,128)} %trial.7) | copy-start | bytes 4718596
  0.0 27.7 %all-to-all-start = ((f32[8,192,128]{2,1,0:T(8,128)}), f32[8,192,128]{2,1,0:T(8,128)}, u32[]{:S(2)}, u32[]{:S(2)}) async-start(f32[8,192,128]{2,1,0:T(8,128)} %bitcast.6), calls=%async_computation | async-start | bytes 1572864 | tf_op jit(solution)/shard_map/all_to_all | solution.py:306
  7.4 1.1 %copy-start.2 = (f32[16,96,128]{2,1,0:T(8,128)S(1)}, f32[16,96,128]{2,1,0:T(8,128)}, u32[]{:S(2)}) copy-start(f32[16,96,128]{2,1,0:T(8,128)} %potential.3) | copy-start | bytes 2359300
  8.6 3.1 %copy-start.11 = (s32[2]{0:T(128)S(1)}, s32[2]{0:T(128)}, u32[]{:S(2)}) copy-start(s32[2]{0:T(128)} %param.9) | copy-start | bytes 28
  8.6 9.1 %copy-start.3 = (f32[16,96,128]{2,1,0:T(8,128)S(1)}, f32[16,96,128]{2,1,0:T(8,128)}, u32[]{:S(2)}) copy-start(f32[16,96,128]{2,1,0:T(8,128)} %potential.3) | copy-start | bytes 2359300
  9.8 6.5 %collective-permute-start = (f32[3,96,128]{2,1,0:T(8,128)S(1)}, f32[3,96,128]{2,1,0:T(8,128)S(1)}, u32[]{:S(2)}, u32[]{:S(2)}) collective-permute-start(f32[3,96,128]{2,1,0:T(8,128)S(1)} %get-tuple-element.17), channel_id=1, source_target_pairs={{0,1},{1,2},{2,3},{3,0},{4,5},{5,6},{6,7},{7,4},{8,9},{9,10},{10,1... | collective-permute-start | bytes 442376 | tf_op jit(solution)/shard_map/ppermute | solution.py:303
  9.9 7.1 %collective-permute-start.1 = (f32[3,96,128]{2,1,0:T(8,128)S(1)}, f32[3,96,128]{2,1,0:T(8,128)S(1)}, u32[]{:S(2)}, u32[]{:S(2)}) collective-permute-start(f32[3,96,128]{2,1,0:T(8,128)S(1)} %get-tuple-element.18), channel_id=1, source_target_pairs={{1,0},{2,1},{3,2},{0,3},{5,4},{6,5},{7,6},{4,7},{9,8},{10,9},{11,1... | collective-permute-start | bytes 442376 | tf_op jit(solution)/shard_map/ppermute | solution.py:304
  16.3 0.7 copy-start.7
  17.0 0.7 copy-start.9
  17.6 0.9 %copy-start.8 = (f32[3,96,128]{2,1,0:T(8,128)S(1)}, f32[3,96,128]{2,1,0:T(8,128)}, u32[]{:S(2)}) copy-start(f32[3,96,128]{2,1,0:T(8,128)} %copy-done.7) | copy-start | bytes 442372
  18.5 0.9 %copy-start.10 = (f32[3,96,128]{2,1,0:T(8,128)S(1)}, f32[3,96,128]{2,1,0:T(8,128)}, u32[]{:S(2)}) copy-start(f32[3,96,128]{2,1,0:T(8,128)} %copy-done.9) | copy-start | bytes 442372
  22.4 0.7 copy-start.4
  23.2 35.5 %copy-start.1 = (bf16[2,768,256]{2,1,0:T(8,128)(2,1)S(1)}, bf16[2,768,256]{2,1,0:T(8,128)(2,1)}, u32[]{:S(2)}) copy-start(bf16[2,768,256]{2,1,0:T(8,128)(2,1)} %constant.8.clone.bands) | copy-start | bytes 2359300
  27.7 31.0 %copy-start.5 = (f32[8,96,128]{2,1,0:T(8,128)S(1)}, f32[8,96,128]{2,1,0:T(8,128)}, u32[]{:S(2)}) copy-start(f32[8,96,128]{2,1,0:T(8,128)} %copy-done.4) | copy-start | bytes 1179652
  27.7 31.0 %copy-start.6 = (bf16[256,128]{1,0:T(8,128)(2,1)S(1)}, bf16[256,128]{1,0:T(8,128)(2,1)}, u32[]{:S(2)}) copy-start(bf16[256,128]{1,0:T(8,128)(2,1)} %constant.9.clone.halo_bands) | copy-start | bytes 196612
  28.7 5.7 %collective-permute-start.3 = (f32[2,192,128]{2,1,0:T(8,128)S(1)}, f32[2,192,128]{2,1,0:T(8,128)S(1)}, u32[]{:S(2)}, u32[]{:S(2)}) collective-permute-start(f32[2,192,128]{2,1,0:T(8,128)S(1)} %pad_maximum_fusion.refs_0_), channel_id=1, source_target_pairs={{8,0},{16,8},{24,16},{28,24},{20,28},{12,20},{4,12},{0,4},{9,1},{1... | collective-permute-start | bytes 589832 | tf_op jit(solution)/shard_map/ppermute | solution.py:328
  30.2 5.9 %collective-permute-start.2 = (f32[2,192,128]{2,1,0:T(8,128)S(1)}, f32[2,192,128]{2,1,0:T(8,128)S(1)}, u32[]{:S(2)}, u32[]{:S(2)}) collective-permute-start(f32[2,192,128]{2,1,0:T(8,128)S(1)} %pad_maximum_fusion.refs_0_), channel_id=1, source_target_pairs={{0,8},{8,16},{16,24},{24,28},{28,20},{20,12},{12,4},{4,0},{1,9},{9... | collective-permute-start | bytes 589832 | tf_op jit(solution)/shard_map/ppermute | solution.py:327
  34.5 6.5 %collective-permute-start.5 = (f32[2,192,128]{2,1,0:T(8,128)S(1)}, f32[2,192,128]{2,1,0:T(8,128)S(1)}, u32[]{:S(2)}, u32[]{:S(2)}) collective-permute-start(f32[2,192,128]{2,1,0:T(8,128)S(1)} %collective-permute-done.3.refs_2_), channel_id=1, source_target_pairs={{8,0},{16,8},{24,16},{28,24},{20,28},{12,20},{4,12},{0,4},{9,1},{1... | collective-permute-start | bytes 589832 | tf_op jit(solution)/shard_map/ppermute | solution.py:328
  36.1 6.0 %collective-permute-start.4 = (f32[2,192,128]{2,1,0:T(8,128)S(1)}, f32[2,192,128]{2,1,0:T(8,128)S(1)}, u32[]{:S(2)}, u32[]{:S(2)}) collective-permute-start(f32[2,192,128]{2,1,0:T(8,128)S(1)} %collective-permute-done.2.refs_1_), channel_id=1, source_target_pairs={{0,8},{8,16},{16,24},{24,28},{28,20},{20,12},{12,4},{4,0},{1,9},{9... | collective-permute-start | bytes 589832 | tf_op jit(solution)/shard_map/ppermute | solution.py:327
  41.0 6.7 %collective-permute-start.7 = (f32[2,192,128]{2,1,0:T(8,128)S(1)}, f32[2,192,128]{2,1,0:T(8,128)S(1)}, u32[]{:S(2)}, u32[]{:S(2)}) collective-permute-start(f32[2,192,128]{2,1,0:T(8,128)S(1)} %collective-permute-done.5.refs_4_), channel_id=1, source_target_pairs={{8,0},{16,8},{24,16},{28,24},{20,28},{12,20},{4,12},{0,4},{9,1},{1... | collective-permute-start | bytes 589832 | tf_op jit(solution)/shard_map/ppermute | solution.py:328
  42.1 6.8 %collective-permute-start.6 = (f32[2,192,128]{2,1,0:T(8,128)S(1)}, f32[2,192,128]{2,1,0:T(8,128)S(1)}, u32[]{:S(2)}, u32[]{:S(2)}) collective-permute-start(f32[2,192,128]{2,1,0:T(8,128)S(1)} %collective-permute-done.4.refs_3_), channel_id=1, source_target_pairs={{0,8},{8,16},{16,24},{24,28},{28,20},{20,12},{12,4},{4,0},{1,9},{9... | collective-permute-start | bytes 589832 | tf_op jit(solution)/shard_map/ppermute | solution.py:327
  47.7 4.7 %collective-permute-start.9 = (f32[2,96,128]{2,1,0:T(8,128)S(1)}, f32[2,96,128]{2,1,0:T(8,128)S(1)}, u32[]{:S(2)}, u32[]{:S(2)}) collective-permute-start(f32[2,96,128]{2,1,0:T(8,128)S(1)} %slice.17), channel_id=1, source_target_pairs={{8,0},{16,8},{24,16},{28,24},{20,28},{12,20},{4,12},{0,4},{9,1},{1... | collective-permute-start | bytes 294920 | tf_op jit(solution)/shard_map/ppermute | solution.py:328
  48.9 4.7 %collective-permute-start.8 = (f32[2,96,128]{2,1,0:T(8,128)S(1)}, f32[2,96,128]{2,1,0:T(8,128)S(1)}, u32[]{:S(2)}, u32[]{:S(2)}) collective-permute-start(f32[2,96,128]{2,1,0:T(8,128)S(1)} %slice.16), channel_id=1, source_target_pairs={{0,8},{8,16},{16,24},{24,28},{28,20},{20,12},{12,4},{4,0},{1,9},{9... | collective-permute-start | bytes 294920 | tf_op jit(solution)/shard_map/ppermute | solution.py:327
  54.5 4.1 %collective-permute-start.10 = (f32[2,96,128]{2,1,0:T(8,128)S(1)}, f32[2,96,128]{2,1,0:T(8,128)S(1)}, u32[]{:S(2)}, u32[]{:S(2)}) collective-permute-start(f32[2,96,128]{2,1,0:T(8,128)S(1)} %get-tuple-element.24), channel_id=1, source_target_pairs={{0,1},{1,2},{2,3},{3,0},{4,5},{5,6},{6,7},{7,4},{8,9},{9,10},{10,1... | collective-permute-start | bytes 294920 | tf_op jit(solution)/shard_map/ppermute | solution.py:340
  54.6 4.1 %collective-permute-start.11 = (f32[2,96,128]{2,1,0:T(8,128)S(1)}, f32[2,96,128]{2,1,0:T(8,128)S(1)}, u32[]{:S(2)}, u32[]{:S(2)}) collective-permute-start(f32[2,96,128]{2,1,0:T(8,128)S(1)} %get-tuple-element.25), channel_id=1, source_target_pairs={{1,0},{2,1},{3,2},{0,3},{5,4},{6,5},{7,6},{4,7},{9,8},{10,9},{11,1... | collective-permute-start | bytes 294920 | tf_op jit(solution)/shard_map/ppermute | solution.py:341

commit v4 on v3

--- a/solution.py
+++ b/solution.py
@@ -75,7 +75,7 @@
     return [*range(0, n, 2), *range(n - 1 - n % 2, 0, -2)]
 
 
-def gather_kernel(n, rounds, *refs):
+def gather_kernel(n, rounds, owner, *refs):
     blocks, (whole, last, first) = refs[:-3], refs[-3:]
     nz = last.shape[1]
     ny = whole.shape[1] // nz
@@ -84,21 +84,18 @@
     spot = jnp.where(me % 2 == 0, me // 2, n - 1 - me // 2)
     rows = blocks[0].shape[1]
 
-    def place(shift):
+    def put(block, shift, last_part):
         position = lax.rem(spot + shift + n, n)
         device = jnp.where(position < evens, 2 * position, 2 * (n - 1 - position) + 1)
-        return device * rows
-
-    def put(block, start):
         size = block.shape[1]
         for r in range(rounds):
+            start = (device ^ owner[r]) * rows + (rows - size if last_part else 0)
             whole[r, pl.ds(pl.multiple_of(start, 8), size), :] = block[r]
 
-    put(blocks[0], place(0))
+    put(blocks[0], 0, False)
     for k, block in enumerate(blocks[1:]):
         step, ahead = k // 2 + 1, k % 2 == 0
-        start = place(-step if ahead else step)
-        put(block, start if ahead or block.shape[1] == rows else start + rows - block.shape[1])
+        put(block, -step if ahead else step, not ahead)
     lane = lanes(nz)
     for r in range(rounds):
         last[r] = pack_edges(lambda y: whole[r, y * nz : (y + 1) * nz], ny, lane, False)
@@ -284,6 +281,37 @@
     return jax.ShapeDtypeStruct(shape, jnp.float32)
 
 
+def exchange(pieces):
+    n = pieces.shape[0]
+    if n > 16:
+        arranged = jnp.take(pieces, lax.axis_index("cols") ^ jnp.arange(n), axis=0)
+        got = lax.all_to_all(arranged, "cols", 0, 0)
+        return [got[s : s + 1] for s in range(n)]
+    got = {0: pieces[:1]}
+    reach = 1 << (n - 1).bit_length() - 1
+    for group in ([k for k in range(reach, n)], [k for k in range(1, reach)]):
+        sent = [pieces[k : k + 1] for k in group]
+        pieces, *sent = lax.optimization_barrier([pieces, *sent])
+        for k, piece in sorted(zip(group, sent), key=lambda pair: (-pair[0].bit_length(), pair[0] & 1, pair[0])):
+            got[k] = lax.ppermute(piece, "cols", [(i, i ^ k) for i in range(n)])
+    return [got[k] for k in range(n)]
+
+
+def pick_kernel(owner, *refs):
+    got, own = refs[:-1], refs[-1]
+    me = lax.axis_index("cols") if len(got) <= 16 else 0
+    for r in range(own.shape[0]):
+        for k, piece in enumerate(got):
+
+            @pl.when((me ^ owner[r]) == k)
+            def _():
+                own[r] = piece[0]
+
+
+def cost(mib):
+    return pl.CostEstimate(flops=0, transcendentals=0, bytes_accessed=mib << 20)
+
+
 def body(trial, orbitals, potential, owner):
     columns, ny, nz, nx = trial.shape
     n, parts = lax.axis_size("cols"), lax.axis_size("sec")
@@ -292,32 +320,39 @@
     sec_up = [(i, (i + 1) % parts) for i in range(parts)]
     sec_down = [(j, i) for i, j in sec_up]
 
+    got = exchange(orbitals.reshape(n, rows, nx))
     last, first = pl.pallas_call(
         pack_kernel,
         out_shape=[f32(columns + 1, nz, nx)] * 2,
         in_specs=vmem(2),
         out_specs=vmem(2),
         compiler_params=params(8),
-        name="pack",
+        cost_estimate=cost(6),
     )(trial, potential)
     left = lax.ppermute(last, "sec", sec_up)
     right = lax.ppermute(first, "sec", sec_down)
-
-    mine = lax.all_to_all(orbitals.reshape(n, rows, nx), "cols", 0, 0)
     prepared = pl.pallas_call(
         prepare_kernel,
         out_shape=[f32(ny // 2, nz, nx), f32(ny, nz, nx), f32(ny // 2, nz, nx)],
         in_specs=vmem(4),
         out_specs=vmem(3),
         compiler_params=params(10),
-        name="prepare",
+        cost_estimate=cost(10),
     )(trial, potential, left, right)
-    mine, (trial_halo, scaled, scaled_halo) = lax.optimization_barrier((mine, prepared))
+    trial_halo, scaled, scaled_halo = prepared
 
     ring = ring_of(n)
     clockwise = [(ring[i], ring[(i + 1) % n]) for i in range(n)]
     counter = [(j, i) for i, j in clockwise]
-    own = jnp.concatenate([lax.dynamic_slice_in_dim(mine, owner[r], 1, 0) for r in range(rounds)])
+    smem = [pl.BlockSpec(memory_space=pltpu.SMEM)]
+    own = pl.pallas_call(
+        pick_kernel,
+        out_shape=f32(rounds, rows, nx),
+        in_specs=smem + vmem(n),
+        out_specs=pl.BlockSpec(memory_space=pltpu.VMEM),
+        compiler_params=params(4),
+        name="pick",
+    )(owner, *got)
     ahead = behind = own
     blocks = [own]
     for step in range(1, n // 2 + 1):
@@ -331,11 +366,11 @@
     psi, psi_last, psi_first = pl.pallas_call(
         functools.partial(gather_kernel, n, rounds),
         out_shape=[f32(rounds, ny * nz, nx), f32(rounds, nz, nx), f32(rounds, nz, nx)],
-        in_specs=vmem(len(blocks)),
+        in_specs=smem + vmem(len(blocks)),
         out_specs=vmem(3),
         compiler_params=params(10),
         name="gather",
-    )(*blocks)
+    )(owner, *blocks)
     psi = psi.reshape(rounds, ny, nz, nx)
     psi_left = lax.ppermute(psi_last, "sec", sec_up)
     psi_right = lax.ppermute(psi_first, "sec", sec_down)
@@ -357,6 +392,5 @@
 
 def solution(mesh):
     placed = (P("cols", None, None, "sec"), P("cols", None, None, "sec"), P(None, None, "sec"), P())
-    return jax.shard_map(
-        body, mesh=mesh, in_specs=placed, out_specs=P("cols", None, None, "sec"), check_vma=False
-    )
+
+    return jax.shard_map(body, mesh=mesh, in_specs=placed, out_specs=P("cols", None, None, "sec"), check_vma=False)

time: 80.7 us -> 78.9 us (0.978)
  local copies, waits for them, and re-layouts: 6.7 us -> 2.31 us
  between operations: 4.13 us -> 0.14 us
  starting transfers between devices: 19.3 us -> 22.3 us
  waiting for transfers between devices: 23.4 us -> 26.3 us
  Pallas kernels: 25.7 us -> 27 us
    ppermute x0 -> x7, waiting for transfers between devices: none -> 13.2 us  [exchange(): got[k] = lax.ppermute(piece, 'cols', [(i, i ^ k) for i in range(n)])]
    ppermute x0 -> x7, starting transfers between devices: none -> 10.8 us  [exchange(): got[k] = lax.ppermute(piece, 'cols', [(i, i ^ k) for i in range(n)])]
    all_to_all x1 -> x0, starting transfers between devices: 7.41 us -> none  [body(): mine = lax.all_to_all(orbitals.reshape(n, rows, nx), 'cols', 0, 0)]
    unnamed x24 -> x10, local copies, waits for them, and re-layouts: 5.02 us -> 0.02 us
    all_to_all x1 -> x0, waiting for transfers between devices: 4.53 us -> none  [body(): mine = lax.all_to_all(orbitals.reshape(n, rows, nx), 'cols', 0, 0)]
    ppermute x4, waiting for transfers between devices: 15.3 us -> 11.4 us  [body(): behind = lax.ppermute(behind, 'cols', counter)]
    ppermute x1, waiting for transfers between devices: 2.3 us -> 0.01 us  [body(): psi_left = lax.ppermute(psi_last, 'sec', sec_up)]
    slice x1 -> x2, local copies, waits for them, and re-layouts: 0.66 us -> 2.27 us  [exchange(): sent = [pieces[k:k + 1] for k in group]]
  transfers between devices with their start and end apart: 13 -> 19, of which waited for: 8 -> 10; matrix products, arithmetic and copies ran while one was open for 1% -> 1% of each run, Pallas kernels for 5% -> 7%
where the time goes in v4:
time: 78.9 us; the launch traced here: 78 us
  Pallas kernels  27 us (34%)
  waiting for transfers between devices  26.3 us (33%)
  starting transfers between devices  22.3 us (28%)
  local copies, waits for them, and re-layouts  2.31 us (3%)
    pallas_call x2, Pallas kernels, body(): pl.pallas_call(functools.partial(round_kernel, r), out_shape=f32(columns,...  20.6 us
    ppermute x7, waiting for transfers between devices, exchange(): got[k] = lax.ppermute(piece, 'cols', [(i, i ^ k) for i in range(n)])  13.2 us
    ppermute x4, waiting for transfers between devices, body(): behind = lax.ppermute(behind, 'cols', counter)  11.4 us
    ppermute x7, starting transfers between devices, exchange(): got[k] = lax.ppermute(piece, 'cols', [(i, i ^ k) for i in range(n)])  10.8 us
    ppermute x4, starting transfers between devices, body(): behind = lax.ppermute(behind, 'cols', counter)  4.1 us
    ppermute x4, starting transfers between devices, body(): ahead = lax.ppermute(ahead, 'cols', clockwise)  3.81 us
    pallas_call x1, Pallas kernels, body(): pl.pallas_call(prepare_kernel, out_shape=[f32(ny // 2, nz, nx), f32(ny, n...  2.96 us
    slice x2, local copies, waits for them, and re-layouts, exchange(): sent = [pieces[k:k + 1] for k in group]  2.27 us
  transfers between devices with their start and end apart: 19, of which 10 were waited for; matrix products, arithmetic and copies ran while one was open for 1% of the time, Pallas kernels for 7%

profile of v4, /device:TPU:0, one launch (start us, length us, event | category | flops | bytes accessed | tf_op | source)
XLA Modules:
  0.0 78.0 jit_solution(11670569643271951869)
XLA Ops:
  0.0 0.0 copy-start.4
  0.0 0.0 copy-start
  0.0 0.0 copy-start.2
  0.0 1.3 %fusion.1 = (f32[1,2,96,128]{3,2,1,0:T(8,128)S(1)}, f32[1,2,96,128]{3,2,1,0:T(8,128)S(1)}, f32[1,2,96,128]{3,2,1,0:T(8,128)S(1)}, f32[1,2,96,128]{3,2,1,0:T(8,128)S(1)}, f32[1,2,96,128]{3,2,1,0:T(8,128)S(1)}) fusion(f32[1,16,96,128]{3,2,1,0:T(8,128)} %param.7), kind=kLoop, calls=%fused_computation.1 | loop fusion | bytes 983040 | tf_op jit(solution)/shard_map/slice | solution.py:293
  1.3 4.1 %collective-permute-start.3 = (f32[1,192,128]{2,1,0:T(8,128)S(1)}, f32[1,192,128]{2,1,0:T(8,128)S(1)}, u32[]{:S(2)}, u32[]{:S(2)}) collective-permute-start(f32[1,192,128]{2,1,0:T(8,128)S(1)} %bitcast.14), channel_id=1, source_target_pairs={{0,16},{4,20},{8,24},{12,28},{16,0},{20,4},{24,8},{28,12},{1,17},{... | collective-permute-start | bytes 294920 | tf_op jit(solution)/shard_map/ppermute | solution.py:296
  5.4 1.3 %collective-permute-start.4 = (f32[1,192,128]{2,1,0:T(8,128)S(1)}, f32[1,192,128]{2,1,0:T(8,128)S(1)}, u32[]{:S(2)}, u32[]{:S(2)}) collective-permute-start(f32[1,192,128]{2,1,0:T(8,128)S(1)} %bitcast.13), channel_id=1, source_target_pairs={{0,20},{4,16},{8,28},{12,24},{16,4},{20,0},{24,12},{28,8},{1,21},{... | collective-permute-start | bytes 294920 | tf_op jit(solution)/shard_map/ppermute | solution.py:296
  6.7 3.6 %collective-permute-start.5 = (f32[1,192,128]{2,1,0:T(8,128)S(1)}, f32[1,192,128]{2,1,0:T(8,128)S(1)}, u32[]{:S(2)}, u32[]{:S(2)}) collective-permute-start(f32[1,192,128]{2,1,0:T(8,128)S(1)} %bitcast.12), channel_id=1, source_target_pairs={{0,24},{4,28},{8,16},{12,20},{16,8},{20,12},{24,0},{28,4},{1,25},{... | collective-permute-start | bytes 294920 | tf_op jit(solution)/shard_map/ppermute | solution.py:296
  10.3 0.0 collective-permute-start.6
  10.3 1.0 %fusion = (f32[1,192,128]{2,1,0:T(8,128)S(1)}, f32[1,192,128]{2,1,0:T(8,128)S(1)}, f32[1,192,128]{2,1,0:T(8,128)S(1)}) fusion(f32[8,192,128]{2,1,0:T(8,128)} %bitcast.10), kind=kLoop, calls=%fused_computation | loop fusion | bytes 589824 | tf_op jit(solution)/shard_map/slice | solution.py:293
  11.3 1.7 %collective-permute-start = (f32[1,192,128]{2,1,0:T(8,128)S(1)}, f32[1,192,128]{2,1,0:T(8,128)S(1)}, u32[]{:S(2)}, u32[]{:S(2)}) collective-permute-start(f32[1,192,128]{2,1,0:T(8,128)S(1)} %get-tuple-element.22), channel_id=1, source_target_pairs={{0,4},{4,0},{8,12},{12,8},{16,20},{20,16},{24,28},{28,24},{1,5},{5... | collective-permute-start | bytes 294920 | tf_op jit(solution)/shard_map/ppermute | solution.py:296
  13.0 4.5 %collective-permute-done.3.refs_4_ = f32[1,192,128]{2,1,0:T(8,128)S(1)} collective-permute-done((f32[1,192,128]{2,1,0:T(8,128)S(1)}, f32[1,192,128]{2,1,0:T(8,128)S(1)}, u32[]{:S(2)}, u32[]{:S(2)}) %collective-permute-start.3) | collective-permute-done | bytes 98336 | tf_op jit(solution)/shard_map/ppermute | solution.py:296
  17.5 0.0 collective-permute-start.1
  17.5 3.2 %collective-permute-done.4.refs_5_ = f32[1,192,128]{2,1,0:T(8,128)S(1)} collective-permute-done((f32[1,192,128]{2,1,0:T(8,128)S(1)}, f32[1,192,128]{2,1,0:T(8,128)S(1)}, u32[]{:S(2)}, u32[]{:S(2)}) %collective-permute-start.4) | collective-permute-done | bytes 98336 | tf_op jit(solution)/shard_map/ppermute | solution.py:296
  20.7 0.0 collective-permute-start.2
  20.7 0.0 collective-permute-done.5.refs_6_
  20.7 0.0 collective-permute-done.6.refs_7_
  20.7 0.0 collective-permute-done.refs_1_
  20.7 2.1 %collective-permute-done.1.refs_2_ = f32[1,192,128]{2,1,0:T(8,128)S(1)} collective-permute-done((f32[1,192,128]{2,1,0:T(8,128)S(1)}, f32[1,192,128]{2,1,0:T(8,128)S(1)}, u32[]{:S(2)}, u32[]{:S(2)}) %collective-permute-start.1) | collective-permute-done | bytes 98336 | tf_op jit(solution)/shard_map/ppermute | solution.py:296
  22.8 3.4 %collective-permute-done.2.refs_3_ = f32[1,192,128]{2,1,0:T(8,128)S(1)} collective-permute-done((f32[1,192,128]{2,1,0:T(8,128)S(1)}, f32[1,192,128]{2,1,0:T(8,128)S(1)}, u32[]{:S(2)}, u32[]{:S(2)}) %collective-permute-start.2) | collective-permute-done | bytes 98336 | tf_op jit(solution)/shard_map/ppermute | solution.py:296
  26.2 0.0 copy-done.4
  26.2 0.7 pick.1.refs_0_
  26.9 0.4 collective-permute-start.8
  27.3 1.7 %collective-permute-start.7 = (f32[2,192,128]{2,1,0:T(8,128)S(1)}, f32[2,192,128]{2,1,0:T(8,128)S(1)}, u32[]{:S(2)}, u32[]{:S(2)}) collective-permute-start(f32[2,192,128]{2,1,0:T(8,128)S(1)} %pick.1.refs_0_), channel_id=1, source_target_pairs={{0,8},{8,16},{16,24},{24,28},{28,20},{20,12},{12,4},{4,0},{1,9},{9... | collective-permute-start | bytes 589832 | tf_op jit(solution)/shard_map/ppermute | solution.py:362
  29.0 3.6 %collective-permute-done.8.refs_2_ = f32[2,192,128]{2,1,0:T(8,128)S(1)} collective-permute-done((f32[2,192,128]{2,1,0:T(8,128)S(1)}, f32[2,192,128]{2,1,0:T(8,128)S(1)}, u32[]{:S(2)}, u32[]{:S(2)}) %collective-permute-start.8) | collective-permute-done | bytes 196640 | tf_op jit(solution)/shard_map/ppermute | solution.py:363
  32.7 1.0 %collective-permute-start.10 = (f32[2,192,128]{2,1,0:T(8,128)S(1)}, f32[2,192,128]{2,1,0:T(8,128)S(1)}, u32[]{:S(2)}, u32[]{:S(2)}) collective-permute-start(f32[2,192,128]{2,1,0:T(8,128)S(1)} %collective-permute-done.8.refs_2_), channel_id=1, source_target_pairs={{8,0},{16,8},{24,16},{28,24},{20,28},{12,20},{4,12},{0,4},{9,1},{1... | collective-permute-start | bytes 589832 | tf_op jit(solution)/shard_map/ppermute | solution.py:363
  33.6 0.0 collective-permute-done.7.refs_1_
  33.6 1.0 %collective-permute-start.9 = (f32[2,192,128]{2,1,0:T(8,128)S(1)}, f32[2,192,128]{2,1,0:T(8,128)S(1)}, u32[]{:S(2)}, u32[]{:S(2)}) collective-permute-start(f32[2,192,128]{2,1,0:T(8,128)S(1)} %collective-permute-done.7.refs_1_), channel_id=1, source_target_pairs={{0,8},{8,16},{16,24},{24,28},{28,20},{20,12},{12,4},{4,0},{1,9},{9... | collective-permute-start | bytes 589832 | tf_op jit(solution)/shard_map/ppermute | solution.py:362
  34.7 3.7 %collective-permute-done.10.refs_4_ = f32[2,192,128]{2,1,0:T(8,128)S(1)} collective-permute-done((f32[2,192,128]{2,1,0:T(8,128)S(1)}, f32[2,192,128]{2,1,0:T(8,128)S(1)}, u32[]{:S(2)}, u32[]{:S(2)}) %collective-permute-start.10) | collective-permute-done | bytes 196640 | tf_op jit(solution)/shard_map/ppermute | solution.py:363
  38.3 1.0 %collective-permute-start.12 = (f32[2,192,128]{2,1,0:T(8,128)S(1)}, f32[2,192,128]{2,1,0:T(8,128)S(1)}, u32[]{:S(2)}, u32[]{:S(2)}) collective-permute-start(f32[2,192,128]{2,1,0:T(8,128)S(1)} %collective-permute-done.10.refs_4_), channel_id=1, source_target_pairs={{8,0},{16,8},{24,16},{28,24},{20,28},{12,20},{4,12},{0,4},{9,1},{1... | collective-permute-start | bytes 589832 | tf_op jit(solution)/shard_map/ppermute | solution.py:363
  39.4 0.3 collective-permute-done.9.refs_3_
  39.7 0.7 collective-permute-start.11
  40.4 4.1 %collective-permute-done.12.refs_6_ = f32[2,192,128]{2,1,0:T(8,128)S(1)} collective-permute-done((f32[2,192,128]{2,1,0:T(8,128)S(1)}, f32[2,192,128]{2,1,0:T(8,128)S(1)}, u32[]{:S(2)}, u32[]{:S(2)}) %collective-permute-start.12) | collective-permute-done | bytes 196640 | tf_op jit(solution)/shard_map/ppermute | solution.py:363
  44.5 1.7 %collective-permute-start.14 = (f32[2,96,128]{2,1,0:T(8,128)S(1)}, f32[2,96,128]{2,1,0:T(8,128)S(1)}, u32[]{:S(2)}, u32[]{:S(2)}) collective-permute-start(f32[2,96,128]{2,1,0:T(8,128)S(1)} %slice.61), channel_id=1, source_target_pairs={{8,0},{16,8},{24,16},{28,24},{20,28},{12,20},{4,12},{0,4},{9,1},{1... | collective-permute-start | bytes 294920 | tf_op jit(solution)/shard_map/ppermute | solution.py:363
  46.2 0.2 collective-permute-done.11.refs_5_
  46.4 0.4 collective-permute-start.13
  46.8 0.0 copy-done
  46.8 0.0 copy-done.2
  46.8 1.2 %shard_map.64 = (f32[3,96,128]{2,1,0:T(8,128)S(1)}, f32[3,96,128]{2,1,0:T(8,128)S(1)}) custom-call(f32[2,16,96,128]{3,2,1,0:T(8,128)S(1)} %copy-done, f32[16,96,128]{2,1,0:T(8,128)S(1)} %copy-done.2), custom_call_target="tpu_custom_call" | custom-call | bytes 6291456 | tf_op jit(solution)/shard_map/pallas_call | solution.py:324
  48.0 0.1 collective-permute-start.17
  48.1 1.7 %collective-permute-start.18 = (f32[3,96,128]{2,1,0:T(8,128)S(1)}, f32[3,96,128]{2,1,0:T(8,128)S(1)}, u32[]{:S(2)}, u32[]{:S(2)}) collective-permute-start(f32[3,96,128]{2,1,0:T(8,128)S(1)} %get-tuple-element.33), channel_id=1, source_target_pairs={{1,0},{2,1},{3,2},{0,3},{5,4},{6,5},{7,6},{4,7},{9,8},{10,9},{11,1... | collective-permute-start | bytes 442376 | tf_op jit(solution)/shard_map/ppermute | solution.py:333
  49.8 0.0 collective-permute-done.14.refs_8_
  49.8 1.2 %collective-permute-done.13.refs_7_ = f32[2,96,128]{2,1,0:T(8,128)S(1)} collective-permute-done((f32[2,96,128]{2,1,0:T(8,128)S(1)}, f32[2,96,128]{2,1,0:T(8,128)S(1)}, u32[]{:S(2)}, u32[]{:S(2)}) %collective-permute-start.13) | collective-permute-done | bytes 98336 | tf_op jit(solution)/shard_map/ppermute | solution.py:362
  51.1 1.5 %gather.1 = (f32[2,1536,128]{2,1,0:T(8,128)S(1)}, f32[2,96,128]{2,1,0:T(8,128)S(1)}, f32[2,96,128]{2,1,0:T(8,128)S(1)}) custom-call(s32[2]{0:T(128)S(1)} %copy-done.4, f32[2,192,128]{2,1,0:T(8,128)S(1)} %pick.1.refs_0_, f32[2,192,128]{2,1,0:T(8,128)S(1)} %collective-permute-done.7.refs_1_, f32[2,192,128]{2,1,0:T(8,128)S(1)} %collective-permute-done.8.refs_2_, ...), custom_call_target="tpu_custom_call" | custom-call | tf_op jit(solution)/shard_map/gather/pallas_call | solution.py:366
  52.6 0.0 copy-start.1
  52.6 0.0 copy-start.3
  52.6 0.1 collective-permute-start.15
  52.7 1.7 %collective-permute-start.16 = (f32[2,96,128]{2,1,0:T(8,128)S(1)}, f32[2,96,128]{2,1,0:T(8,128)S(1)}, u32[]{:S(2)}, u32[]{:S(2)}) collective-permute-start(f32[2,96,128]{2,1,0:T(8,128)S(1)} %get-tuple-element.31), channel_id=1, source_target_pairs={{1,0},{2,1},{3,2},{0,3},{5,4},{6,5},{7,6},{4,7},{9,8},{10,9},{11,1... | collective-permute-start | bytes 294920 | tf_op jit(solution)/shard_map/ppermute | solution.py:376
  54.4 0.0 collective-permute-done.17.left
  54.4 0.0 collective-permute-done.18.right
  54.4 3.0 %shard_map.65 = (f32[8,96,128]{2,1,0:T(8,128)S(1)}, f32[16,96,128]{2,1,0:T(8,128)S(1)}, f32[8,96,128]{2,1,0:T(8,128)S(1)}) custom-call(f32[2,16,96,128]{3,2,1,0:T(8,128)S(1)} %copy-done, f32[16,96,128]{2,1,0:T(8,128)S(1)} %copy-done.2, f32[3,96,128]{2,1,0:T(8,128)S(1)} %collective-permute-done.17.left, f32[3,96,128]{2,1,0:T(8,128)S(1)} %collective-permute-done.18.right), custom_call_target="tpu_custom_call" | custom-call | bytes 10485760 | tf_op jit(solution)/shard_map/pallas_call | solution.py:334
  57.4 0.0 collective-permute-done.15.left
  57.4 0.0 collective-permute-done.16.right
  57.4 0.0 copy-done.1
  57.4 0.0 copy-done.3
  57.4 9.7 %round.2.refs_0_ = f32[2,16,96,128]{3,2,1,0:T(8,128)S(1)} custom-call(f32[2,16,96,128]{3,2,1,0:T(8,128)S(1)} %bitcast.7, f32[2,96,128]{2,1,0:T(8,128)S(1)} %collective-permute-done.15.left, f32[2,96,128]{2,1,0:T(8,128)S(1)} %collective-permute-done.16.right, f32[2,16,96,128]{3,2,1,0:T(8,128)S(1)} %copy-done, f32[8,96,128]{2,1,0:T(8,128)S(1)} %get-tuple-element.34.trial_halo, ...), custom_call_target="tpu_custom_call" | custom-call | tf_op jit(solution)/shard_map/round/pallas_call | solution.py:381
  67.1 10.9 %round.3 = f32[2,16,96,128]{3,2,1,0:T(8,128)} custom-call(f32[2,16,96,128]{3,2,1,0:T(8,128)S(1)} %bitcast.8, f32[2,96,128]{2,1,0:T(8,128)S(1)} %collective-permute-done.15.left, f32[2,96,128]{2,1,0:T(8,128)S(1)} %collective-permute-done.16.right, f32[2,16,96,128]{3,2,1,0:T(8,128)S(1)} %copy-done, f32[8,96,128]{2,1,0:T(8,128)S(1)} %get-tuple-element.34.trial_halo, ...), custom_call_target="tpu_custom_call" | custom-call | tf_op jit(solution)/shard_map/round/pallas_call | solution.py:381
  (2 shorter events, 0.0 us)
Async XLA Ops:
  0.0 26.2 %copy-start.4 = (s32[2]{0:T(128)S(1)}, s32[2]{0:T(128)}, u32[]{:S(2)}) copy-start(s32[2]{0:T(128)} %owner.3) | copy-start | bytes 28
  0.0 46.8 %copy-start = (f32[2,16,96,128]{3,2,1,0:T(8,128)S(1)}, f32[2,16,96,128]{3,2,1,0:T(8,128)}, u32[]{:S(2)}) copy-start(f32[2,16,96,128]{3,2,1,0:T(8,128)} %trial.7) | copy-start | bytes 4718596
  0.0 46.8 %copy-start.2 = (f32[16,96,128]{2,1,0:T(8,128)S(1)}, f32[16,96,128]{2,1,0:T(8,128)}, u32[]{:S(2)}) copy-start(f32[16,96,128]{2,1,0:T(8,128)} %potential.3) | copy-start | bytes 2359300
  1.3 16.3 %collective-permute-start.3 = (f32[1,192,128]{2,1,0:T(8,128)S(1)}, f32[1,192,128]{2,1,0:T(8,128)S(1)}, u32[]{:S(2)}, u32[]{:S(2)}) collective-permute-start(f32[1,192,128]{2,1,0:T(8,128)S(1)} %bitcast.14), channel_id=1, source_target_pairs={{0,16},{4,20},{8,24},{12,28},{16,0},{20,4},{24,8},{28,12},{1,17},{... | collective-permute-start | bytes 294920 | tf_op jit(solution)/shard_map/ppermute | solution.py:296
  5.4 15.3 %collective-permute-start.4 = (f32[1,192,128]{2,1,0:T(8,128)S(1)}, f32[1,192,128]{2,1,0:T(8,128)S(1)}, u32[]{:S(2)}, u32[]{:S(2)}) collective-permute-start(f32[1,192,128]{2,1,0:T(8,128)S(1)} %bitcast.13), channel_id=1, source_target_pairs={{0,20},{4,16},{8,28},{12,24},{16,4},{20,0},{24,12},{28,8},{1,21},{... | collective-permute-start | bytes 294920 | tf_op jit(solution)/shard_map/ppermute | solution.py:296
  6.7 14.0 %collective-permute-start.5 = (f32[1,192,128]{2,1,0:T(8,128)S(1)}, f32[1,192,128]{2,1,0:T(8,128)S(1)}, u32[]{:S(2)}, u32[]{:S(2)}) collective-permute-start(f32[1,192,128]{2,1,0:T(8,128)S(1)} %bitcast.12), channel_id=1, source_target_pairs={{0,24},{4,28},{8,16},{12,20},{16,8},{20,12},{24,0},{28,4},{1,25},{... | collective-permute-start | bytes 294920 | tf_op jit(solution)/shard_map/ppermute | solution.py:296
  10.3 10.4 %collective-permute-start.6 = (f32[1,192,128]{2,1,0:T(8,128)S(1)}, f32[1,192,128]{2,1,0:T(8,128)S(1)}, u32[]{:S(2)}, u32[]{:S(2)}) collective-permute-start(f32[1,192,128]{2,1,0:T(8,128)S(1)} %bitcast.11), channel_id=1, source_target_pairs={{0,28},{4,24},{8,20},{12,16},{16,12},{20,8},{24,4},{28,0},{1,29},{... | collective-permute-start | bytes 294920 | tf_op jit(solution)/shard_map/ppermute | solution.py:296
  11.3 9.4 %collective-permute-start = (f32[1,192,128]{2,1,0:T(8,128)S(1)}, f32[1,192,128]{2,1,0:T(8,128)S(1)}, u32[]{:S(2)}, u32[]{:S(2)}) collective-permute-start(f32[1,192,128]{2,1,0:T(8,128)S(1)} %get-tuple-element.22), channel_id=1, source_target_pairs={{0,4},{4,0},{8,12},{12,8},{16,20},{20,16},{24,28},{28,24},{1,5},{5... | collective-permute-start | bytes 294920 | tf_op jit(solution)/shard_map/ppermute | solution.py:296
  17.5 5.3 %collective-permute-start.1 = (f32[1,192,128]{2,1,0:T(8,128)S(1)}, f32[1,192,128]{2,1,0:T(8,128)S(1)}, u32[]{:S(2)}, u32[]{:S(2)}) collective-permute-start(f32[1,192,128]{2,1,0:T(8,128)S(1)} %get-tuple-element.23), channel_id=1, source_target_pairs={{0,8},{4,12},{8,0},{12,4},{16,24},{20,28},{24,16},{28,20},{1,9},{5... | collective-permute-start | bytes 294920 | tf_op jit(solution)/shard_map/ppermute | solution.py:296
  20.7 5.5 %collective-permute-start.2 = (f32[1,192,128]{2,1,0:T(8,128)S(1)}, f32[1,192,128]{2,1,0:T(8,128)S(1)}, u32[]{:S(2)}, u32[]{:S(2)}) collective-permute-start(f32[1,192,128]{2,1,0:T(8,128)S(1)} %get-tuple-element.24), channel_id=1, source_target_pairs={{0,12},{4,8},{8,4},{12,0},{16,28},{20,24},{24,20},{28,16},{1,13},{... | collective-permute-start | bytes 294920 | tf_op jit(solution)/shard_map/ppermute | solution.py:296
  26.9 5.7 %collective-permute-start.8 = (f32[2,192,128]{2,1,0:T(8,128)S(1)}, f32[2,192,128]{2,1,0:T(8,128)S(1)}, u32[]{:S(2)}, u32[]{:S(2)}) collective-permute-start(f32[2,192,128]{2,1,0:T(8,128)S(1)} %pick.1.refs_0_), channel_id=1, source_target_pairs={{8,0},{16,8},{24,16},{28,24},{20,28},{12,20},{4,12},{0,4},{9,1},{1... | collective-permute-start | bytes 589832 | tf_op jit(solution)/shard_map/ppermute | solution.py:363
  27.3 6.3 %collective-permute-start.7 = (f32[2,192,128]{2,1,0:T(8,128)S(1)}, f32[2,192,128]{2,1,0:T(8,128)S(1)}, u32[]{:S(2)}, u32[]{:S(2)}) collective-permute-start(f32[2,192,128]{2,1,0:T(8,128)S(1)} %pick.1.refs_0_), channel_id=1, source_target_pairs={{0,8},{8,16},{16,24},{24,28},{28,20},{20,12},{12,4},{4,0},{1,9},{9... | collective-permute-start | bytes 589832 | tf_op jit(solution)/shard_map/ppermute | solution.py:362
  32.7 5.7 %collective-permute-start.10 = (f32[2,192,128]{2,1,0:T(8,128)S(1)}, f32[2,192,128]{2,1,0:T(8,128)S(1)}, u32[]{:S(2)}, u32[]{:S(2)}) collective-permute-start(f32[2,192,128]{2,1,0:T(8,128)S(1)} %collective-permute-done.8.refs_2_), channel_id=1, source_target_pairs={{8,0},{16,8},{24,16},{28,24},{20,28},{12,20},{4,12},{0,4},{9,1},{1... | collective-permute-start | bytes 589832 | tf_op jit(solution)/shard_map/ppermute | solution.py:363
  33.6 6.0 %collective-permute-start.9 = (f32[2,192,128]{2,1,0:T(8,128)S(1)}, f32[2,192,128]{2,1,0:T(8,128)S(1)}, u32[]{:S(2)}, u32[]{:S(2)}) collective-permute-start(f32[2,192,128]{2,1,0:T(8,128)S(1)} %collective-permute-done.7.refs_1_), channel_id=1, source_target_pairs={{0,8},{8,16},{16,24},{24,28},{28,20},{20,12},{12,4},{4,0},{1,9},{9... | collective-permute-start | bytes 589832 | tf_op jit(solution)/shard_map/ppermute | solution.py:362
  38.3 6.1 %collective-permute-start.12 = (f32[2,192,128]{2,1,0:T(8,128)S(1)}, f32[2,192,128]{2,1,0:T(8,128)S(1)}, u32[]{:S(2)}, u32[]{:S(2)}) collective-permute-start(f32[2,192,128]{2,1,0:T(8,128)S(1)} %collective-permute-done.10.refs_4_), channel_id=1, source_target_pairs={{8,0},{16,8},{24,16},{28,24},{20,28},{12,20},{4,12},{0,4},{9,1},{1... | collective-permute-start | bytes 589832 | tf_op jit(solution)/shard_map/ppermute | solution.py:363
  39.7 6.7 %collective-permute-start.11 = (f32[2,192,128]{2,1,0:T(8,128)S(1)}, f32[2,192,128]{2,1,0:T(8,128)S(1)}, u32[]{:S(2)}, u32[]{:S(2)}) collective-permute-start(f32[2,192,128]{2,1,0:T(8,128)S(1)} %collective-permute-done.9.refs_3_), channel_id=1, source_target_pairs={{0,8},{8,16},{16,24},{24,28},{28,20},{20,12},{12,4},{4,0},{1,9},{9... | collective-permute-start | bytes 589832 | tf_op jit(solution)/shard_map/ppermute | solution.py:362
  44.5 5.4 %collective-permute-start.14 = (f32[2,96,128]{2,1,0:T(8,128)S(1)}, f32[2,96,128]{2,1,0:T(8,128)S(1)}, u32[]{:S(2)}, u32[]{:S(2)}) collective-permute-start(f32[2,96,128]{2,1,0:T(8,128)S(1)} %slice.61), channel_id=1, source_target_pairs={{8,0},{16,8},{24,16},{28,24},{20,28},{12,20},{4,12},{0,4},{9,1},{1... | collective-permute-start | bytes 294920 | tf_op jit(solution)/shard_map/ppermute | solution.py:363
  46.4 4.7 %collective-permute-start.13 = (f32[2,96,128]{2,1,0:T(8,128)S(1)}, f32[2,96,128]{2,1,0:T(8,128)S(1)}, u32[]{:S(2)}, u32[]{:S(2)}) collective-permute-start(f32[2,96,128]{2,1,0:T(8,128)S(1)} %slice.60), channel_id=1, source_target_pairs={{0,8},{8,16},{16,24},{24,28},{28,20},{20,12},{12,4},{4,0},{1,9},{9... | collective-permute-start | bytes 294920 | tf_op jit(solution)/shard_map/ppermute | solution.py:362
  48.0 6.4 %collective-permute-start.17 = (f32[3,96,128]{2,1,0:T(8,128)S(1)}, f32[3,96,128]{2,1,0:T(8,128)S(1)}, u32[]{:S(2)}, u32[]{:S(2)}) collective-permute-start(f32[3,96,128]{2,1,0:T(8,128)S(1)} %get-tuple-element.32), channel_id=1, source_target_pairs={{0,1},{1,2},{2,3},{3,0},{4,5},{5,6},{6,7},{7,4},{8,9},{9,10},{10,1... | collective-permute-start | bytes 442376 | tf_op jit(solution)/shard_map/ppermute | solution.py:332
  48.1 6.3 %collective-permute-start.18 = (f32[3,96,128]{2,1,0:T(8,128)S(1)}, f32[3,96,128]{2,1,0:T(8,128)S(1)}, u32[]{:S(2)}, u32[]{:S(2)}) collective-permute-start(f32[3,96,128]{2,1,0:T(8,128)S(1)} %get-tuple-element.33), channel_id=1, source_target_pairs={{1,0},{2,1},{3,2},{0,3},{5,4},{6,5},{7,6},{4,7},{9,8},{10,9},{11,1... | collective-permute-start | bytes 442376 | tf_op jit(solution)/shard_map/ppermute | solution.py:333
  52.6 4.8 %copy-start.1 = (bf16[2,768,256]{2,1,0:T(8,128)(2,1)S(1)}, bf16[2,768,256]{2,1,0:T(8,128)(2,1)}, u32[]{:S(2)}) copy-start(bf16[2,768,256]{2,1,0:T(8,128)(2,1)} %constant.4.clone.bands) | copy-start | bytes 2359300
  52.6 4.8 %copy-start.3 = (bf16[256,128]{1,0:T(8,128)(2,1)S(1)}, bf16[256,128]{1,0:T(8,128)(2,1)}, u32[]{:S(2)}) copy-start(bf16[256,128]{1,0:T(8,128)(2,1)} %constant.5.clone.halo_bands) | copy-start | bytes 196612
  52.6 4.8 %collective-permute-start.15 = (f32[2,96,128]{2,1,0:T(8,128)S(1)}, f32[2,96,128]{2,1,0:T(8,128)S(1)}, u32[]{:S(2)}, u32[]{:S(2)}) collective-permute-start(f32[2,96,128]{2,1,0:T(8,128)S(1)} %get-tuple-element.30), channel_id=1, source_target_pairs={{0,1},{1,2},{2,3},{3,0},{4,5},{5,6},{6,7},{7,4},{8,9},{9,10},{10,1... | collective-permute-start | bytes 294920 | tf_op jit(solution)/shard_map/ppermute | solution.py:375
  52.7 4.7 %collective-permute-start.16 = (f32[2,96,128]{2,1,0:T(8,128)S(1)}, f32[2,96,128]{2,1,0:T(8,128)S(1)}, u32[]{:S(2)}, u32[]{:S(2)}) collective-permute-start(f32[2,96,128]{2,1,0:T(8,128)S(1)} %get-tuple-element.31), channel_id=1, source_target_pairs={{1,0},{2,1},{3,2},{0,3},{5,4},{6,5},{7,6},{4,7},{9,8},{10,9},{11,1... | collective-permute-start | bytes 294920 | tf_op jit(solution)/shard_map/ppermute | solution.py:376

commit v5 on v4

--- a/solution.py
+++ b/solution.py
@@ -16,6 +16,8 @@
 HALO = 6
 ZP = 8
 CHUNK = 32
+SHORT = 16
+DEPTH = 4
 
 
 def lanes(rows):
@@ -35,15 +37,21 @@
     return tile
 
 
-def halo_plane(left, right, low, high, lane, y):
+def outer_lanes(left, right, lane, y):
     inner = lane % 64
     tile = jnp.where(inner < 6, pltpu.roll(left, (-8 * y) % 128, 1), 0.0)
-    tile = jnp.where(between(inner, 22, 28), pltpu.roll(right, (22 - 8 * y) % 128, 1), tile)
-    tile = jnp.where(between(lane, 6, 12), pltpu.roll(low, 6, 1), tile)
+    return jnp.where(between(inner, 22, 28), pltpu.roll(right, (22 - 8 * y) % 128, 1), tile)
+
+
+def inner_lanes(low, high, lane):
+    tile = jnp.where(between(lane, 6, 12), pltpu.roll(low, 6, 1), 0.0)
     tile = jnp.where(between(lane, 16, 22), pltpu.roll(low, 22, 1), tile)
     tile = jnp.where(between(lane, 70, 76), pltpu.roll(high, 70, 1), tile)
-    tile = jnp.where(between(lane, 80, 86), pltpu.roll(high, 86, 1), tile)
-    return tile
+    return jnp.where(between(lane, 80, 86), pltpu.roll(high, 86, 1), tile)
+
+
+def halo_plane(left, right, low, high, lane, y):
+    return outer_lanes(left, right, lane, y) + inner_lanes(low, high, lane)
 
 
 def pack_kernel(trial, potential, last, first):
@@ -102,24 +110,20 @@
         first[r] = pack_edges(lambda y: whole[r, y * nz : (y + 1) * nz], ny, lane, True)
 
 
-def clear_borders(ref, ny, nz):
+def clear_borders(ref, nz, planes):
+    zero = jnp.zeros((ZP, 128), jnp.float32)
     for c in range(ref.shape[0]):
-        for y in (0, 1, ny + 2, ny + 3):
-            ref[c, y] = jnp.zeros_like(ref[c, y])
-
-        @pl.loop(2, ny + 2)
-        def _(y):
-            ref[c, y, 0:ZP] = jnp.zeros((ZP, 128), jnp.float32)
-            ref[c, y, ZP + nz : 2 * ZP + nz] = jnp.zeros((ZP, 128), jnp.float32)
-
-
-def neighbours(ref, c, y, at, rows):
-    near = (ref[c, y - 1, pl.ds(at, rows)] + ref[c, y + 1, pl.ds(at, rows)]) + (
-        ref[c, y, pl.ds(at - 1, rows)] + ref[c, y, pl.ds(at + 1, rows)]
-    )
-    far = (ref[c, y - 2, pl.ds(at, rows)] + ref[c, y + 2, pl.ds(at, rows)]) + (
-        ref[c, y, pl.ds(at - 2, rows)] + ref[c, y, pl.ds(at + 2, rows)]
-    )
+        for y in range(ref.shape[1]):
+            if y in planes:
+                ref[c, y] = jnp.zeros_like(ref[c, y])
+            else:
+                ref[c, y, 0:ZP] = zero
+                ref[c, y, ZP + nz : 2 * ZP + nz] = zero
+
+
+def rows_around(ref, c, y, at, rows):
+    near = ref[c, y, pl.ds(at - 1, rows)] + ref[c, y, pl.ds(at + 1, rows)]
+    far = ref[c, y, pl.ds(at - 2, rows)] + ref[c, y, pl.ds(at + 2, rows)]
     return near, far
 
 
@@ -152,121 +156,140 @@
     return jnp.asarray(sections.reshape(2, 768, 256), jnp.bfloat16), jnp.asarray(halo.reshape(256, 128), jnp.bfloat16)
 
 
-def round_scratch(columns, ny, nz, nx):
+def split(pieces, value, row, first, second):
+    rows = pl.ds(pl.multiple_of(row, 16), value.shape[0])
+    high = value.astype(jnp.bfloat16)
+    pieces[rows, 128 * first : 128 * (first + 1)] = high
+    rest = (value - high.astype(jnp.float32)).astype(jnp.bfloat16)
+    pieces[rows, 128 * second : 128 * (second + 1)] = rest
+
+
+def begin_kernel(psi, trial, own_ends, *refs):
+    rounds, ny, nz, _ = psi.shape
+    columns = trial.shape[0]
+    lane = lanes(nz)
+    for r in range(rounds):
+        w, u, v, pieces = refs[4 * r : 4 * r + 4]
+        for ref in (w, u, v):
+            clear_borders(ref, nz, (0, 1, ny + 2, ny + 3))
+
+        @pl.loop(0, ny)
+        def _(y):
+            for z in range(0, nz, CHUNK):
+                here = psi[r, y, pl.ds(z, CHUNK)]
+                for c in range(columns):
+                    value = here * trial[c, y, pl.ds(z, CHUNK)]
+                    w[c, y + 2, pl.ds(ZP + z, CHUNK)] = value
+                    split(pieces, value, y * nz + z, c, 2 + c)
+
+        for y in range(ny // 2):
+            own_ends[r, y] = inner_lanes(psi[r, y], psi[r, y + ny // 2], lane)
+
+
+def main_scratch(rounds, ny, nz, nx):
     half = ny // 2
     return (
-        [pltpu.VMEM((columns, ny + 4, nz + 2 * ZP, nx), jnp.float32)] * 3
-        + [pltpu.VMEM((1, half + 4, nz + 2 * ZP, nx), jnp.float32)] * 3
-        + [
-            pltpu.VMEM((ny * nz, 6 * nx), jnp.bfloat16),
-            pltpu.VMEM((ny * nz, 2 * nx), jnp.float32),
-            pltpu.VMEM((half * nz, nx), jnp.float32),
-        ]
+        [pltpu.VMEM((1, half + 4, nz + 2 * ZP, nx), jnp.float32)] * (3 * rounds)
+        + [pltpu.VMEM((ny * nz, 2 * nx), jnp.float32)] * rounds
+        + [pltpu.VMEM((half * nz, nx), jnp.float32)]
     )
 
 
-def round_kernel(turn, psi, left, right, trial, trial_halo, scaled, scaled_halo, bands, halo_bands, *refs):
-    psi, left, right = psi.at[turn], left.at[turn], right.at[turn]
-    if turn:
-        total, *refs = refs
-    out, w, u, v, w_halo, u_halo, v_halo, pieces, sums, halo_sums = refs
-    columns, ny, nz, _ = trial.shape
+def main_kernel(rounds, psi, left, right, trial_halo, scaled, scaled_halo, bands, halo_bands, own_ends, *refs):
+    given, refs = refs[: 4 * rounds], refs[4 * rounds :]
+    out, changed, refs = refs[0], refs[1 : 1 + 3 * rounds], refs[1 + 3 * rounds :]
+    arrays = [ref for r in range(rounds) for ref in (given[4 * r], *changed[3 * r : 3 * r + 3])]
+    halos, sums, halo_sums = refs[: 3 * rounds], refs[3 * rounds : 4 * rounds], refs[4 * rounds]
+    columns, ny, nz, _ = out.shape
     half = ny // 2
     full = lanes(nz)
-    for ref in (w, u, v):
-        clear_borders(ref, ny, nz)
-    for ref in (w_halo, u_halo, v_halo):
-        clear_borders(ref, half, nz)
-
-    def split(value, row, first, second):
-        high = value.astype(jnp.bfloat16)
-        pieces[pl.ds(row, CHUNK), 128 * first : 128 * (first + 1)] = high
-        rest = (value - high.astype(jnp.float32)).astype(jnp.bfloat16)
-        pieces[pl.ds(row, CHUNK), 128 * second : 128 * (second + 1)] = rest
-
-    def row_of(y, z):
-        return pl.multiple_of(y * nz + z, CHUNK)
-
-    def put(target, c, y, z, value):
-        target[c, y + 2, pl.ds(ZP + z, CHUNK)] = value
-        split(value, row_of(y, z), c, 2 + c)
-
-    def put_halo(target, y, z, value):
-        target[0, y + 2, pl.ds(ZP + z, CHUNK)] = value
+    blocks = ny // DEPTH
+
+    def multiply(r, block):
+        rows = pl.ds(pl.multiple_of(block * (DEPTH * nz), 16), DEPTH * nz)
+        matrix = bands[block // (blocks // 2)]
+        sums[r][rows, :] = jnp.dot(arrays[4 * r + 3][rows, :], matrix, preferred_element_type=jnp.float32)
+
+    def put_halo(r, target, y, z, value):
+        target[0, y + 2, pl.ds(ZP + z, value.shape[0])] = value
         for h in range(2):
-            split(value, row_of(y + h * half, z), 4, 5)
-
-    for y in range(half):
-        part = halo_plane(left[...], right[...], psi[y], psi[y + half], full, y)
-        w_halo[0, y + 2, pl.ds(ZP, nz)] = (part + pltpu.roll(part, 32, 1)) * trial_halo[y]
-    wrap_halo(w_halo, half, nz, full)
-
-    @pl.loop(0, half)
-    def _(y):
-        for z in range(0, nz, CHUNK):
-            put_halo(w_halo, y, z, w_halo[0, y + 2, pl.ds(ZP + z, CHUNK)])
-
-    @pl.loop(0, ny)
-    def _(y):
-        for z in range(0, nz, CHUNK):
-            here = psi[y, pl.ds(z, CHUNK)]
-            for c in range(columns):
-                put(w, c, y, z, here * trial[c, y, pl.ds(z, CHUNK)])
-
-    def multiply():
-        for h in range(2):
-            rows = pl.ds(h * half * nz, half * nz)
-            sums[rows, :] = jnp.dot(pieces[rows, :], bands[h], preferred_element_type=jnp.float32)
-
-    def halo_stage(source, target, shift, weight):
-        halo_sums[...] = jnp.dot(pieces[: half * nz, 512:], halo_bands[...], preferred_element_type=jnp.float32)
+            split(arrays[4 * r + 3], value, (y + h * half) * nz + z, 4, 5)
+
+    def start(r):
+        for ref in halos[3 * r : 3 * r + 3]:
+            clear_borders(ref, nz, ())
+        for y in range(half):
+            part = outer_lanes(left[r], right[r], full, y) + own_ends[r, y]
+            put_halo(r, halos[3 * r], y, 0, (part + pltpu.roll(part, 32, 1)) * trial_halo[y])
+        wrap_halo(halos[3 * r], half, nz, full)
+
+    def halo_stage(r, step, shift, weight):
+        first, source, target = halos[3 * r], halos[3 * r + step], halos[3 * r + step + 1]
+        halo_sums[...] = jnp.dot(
+            arrays[4 * r + 3][: half * nz, 512:], halo_bands[...], preferred_element_type=jnp.float32
+        )
 
         @pl.loop(0, half)
         def _(y):
             for z in range(0, nz, CHUNK):
-                at = ZP + z
-                f = source[0, y + 2, pl.ds(at, CHUNK)]
-                near, far = neighbours(source, 0, y + 2, at, CHUNK)
-                value = (far + halo_sums[pl.ds(row_of(y, z), CHUNK), :]) - 16.0 * near
-                value = value + (scaled_halo[y, pl.ds(z, CHUNK)] - shift) * f
+                rows = pl.ds(ZP + z, CHUNK)
+                f = source[0, y + 2, rows]
+                near, far = rows_around(source, 0, y + 2, ZP + z, CHUNK)
+                near = near + (source[0, y + 1, rows] + source[0, y + 3, rows])
+                far = far + (source[0, y, rows] + source[0, y + 4, rows])
+                along = halo_sums[pl.ds(pl.multiple_of(y * nz + z, CHUNK), CHUNK), :]
+                value = (far + along) - 16.0 * near + (scaled_halo[y, pl.ds(z, CHUNK)] - shift) * f
                 if weight:
-                    value = value - weight * w_halo[0, y + 2, pl.ds(at, CHUNK)]
-                put_halo(target, y, z, value)
+                    value = value - weight * first[0, y + 2, rows]
+                put_halo(r, target, y, z, value)
 
         wrap_halo(target, half, nz, full)
 
-    def stage(source, shift, weight, store):
-        @pl.loop(0, ny)
-        def _(y):
-            for z in range(0, nz, CHUNK):
-                at = ZP + z
-                diagonal = scaled[y, pl.ds(z, CHUNK)] - shift if shift else scaled[y, pl.ds(z, CHUNK)]
+    def stage(r, step, shift, weight, beside):
+        first, source = arrays[4 * r], arrays[4 * r + step]
+
+        @pl.loop(0, blocks)
+        def _(block):
+            if beside is not None:
+                multiply(beside, block)
+            for z in range(0, nz, SHORT):
+                rows = pl.ds(ZP + z, SHORT)
                 for c in range(columns):
-                    f = source[c, y + 2, pl.ds(at, CHUNK)]
-                    near, far = neighbours(source, c, y + 2, at, CHUNK)
-                    value = (far + sums[pl.ds(row_of(y, z), CHUNK), 128 * c : 128 * (c + 1)]) - 16.0 * near
-                    value = value + diagonal * f
-                    if weight:
-                        value = value - weight * w[c, y + 2, pl.ds(at, CHUNK)]
-                    store(c, y, z, value)
-
-    def into(target):
-        return lambda c, y, z, value: put(target, c, y, z, value)
-
-    def finish(c, y, z, value):
-        term = (FINAL * psi[y, pl.ds(z, CHUNK)]) * value
-        if turn:
-            term = term + total[c, y, pl.ds(z, CHUNK)]
-        out[c, y, pl.ds(z, CHUNK)] = term
-
-    multiply()
-    halo_stage(w_halo, u_halo, ALPHA, None)
-    stage(w, ALPHA, None, into(u))
-    multiply()
-    halo_stage(u_halo, v_halo, 0.0, BETA)
-    stage(u, 0.0, BETA, into(v))
-    multiply()
-    stage(v, 0.0, GAMMA, finish)
+                    planes = [source[c, block * DEPTH + k, rows] for k in range(DEPTH + 4)]
+                    for k in range(DEPTH):
+                        y = block * DEPTH + k
+                        near, far = rows_around(source, c, y + 2, ZP + z, SHORT)
+                        near = near + (planes[k + 1] + planes[k + 3])
+                        far = far + (planes[k] + planes[k + 4])
+                        along = sums[r][pl.ds(pl.multiple_of(y * nz + z, SHORT), SHORT), 128 * c : 128 * (c + 1)]
+                        diagonal = scaled[y, pl.ds(z, SHORT)]
+                        if shift:
+                            diagonal = diagonal - shift
+                        value = (far + along) - 16.0 * near + diagonal * planes[k + 2]
+                        if weight:
+                            value = value - weight * first[c, y + 2, rows]
+                        if step < 2:
+                            arrays[4 * r + step + 1][c, y + 2, rows] = value
+                            split(arrays[4 * r + 3], value, y * nz + z, c, 2 + c)
+                        else:
+                            term = (FINAL * psi[r, y, pl.ds(z, SHORT)]) * value
+                            if r:
+                                term = term + out[c, y, pl.ds(z, SHORT)]
+                            out[c, y, pl.ds(z, SHORT)] = term
+
+    steps = ((ALPHA, None), (0.0, BETA), (0.0, GAMMA))
+    turns = [(step, r) for step in range(3) for r in range(rounds)]
+    for r in range(rounds):
+        start(r)
+
+    @pl.loop(0, blocks)
+    def _(block):
+        multiply(0, block)
+
+    for at, (step, r) in enumerate(turns):
+        if step < 2:
+            halo_stage(r, step, *steps[step])
+        stage(r, step, *steps[step], turns[at + 1][1] if at + 1 < len(turns) else None)
 
 
 def vmem(count):
@@ -374,20 +397,28 @@
     psi = psi.reshape(rounds, ny, nz, nx)
     psi_left = lax.ppermute(psi_last, "sec", sec_up)
     psi_right = lax.ppermute(psi_first, "sec", sec_down)
-    total = None
-    matrices = bands()
-    for r in range(rounds):
-        given = [psi, psi_left, psi_right, trial, trial_halo, scaled, scaled_halo, *matrices] + ([total] if r else [])
-        total = pl.pallas_call(
-            functools.partial(round_kernel, r),
-            out_shape=f32(columns, ny, nz, nx),
-            in_specs=vmem(len(given)),
-            out_specs=pl.BlockSpec(memory_space=pltpu.VMEM),
-            scratch_shapes=round_scratch(columns, ny, nz, nx),
-            compiler_params=params(32),
-            name="round",
-        )(*given)
-    return total
+    padded = f32(columns, ny + 4, nz + 2 * ZP, nx)
+    pieces = jax.ShapeDtypeStruct((ny * nz, 6 * nx), jnp.bfloat16)
+    own_ends, *arrays = pl.pallas_call(
+        begin_kernel,
+        out_shape=[f32(rounds, ny // 2, nz, nx)] + [padded, padded, padded, pieces] * rounds,
+        in_specs=vmem(2),
+        out_specs=vmem(1 + 4 * rounds),
+        compiler_params=params(20),
+        cost_estimate=cost(8),
+    )(psi, trial)
+    given = [psi, psi_left, psi_right, trial_halo, scaled, scaled_halo, *bands(), own_ends, *arrays]
+    changed = [len(given) - 4 * rounds + 4 * r + k for r in range(rounds) for k in (1, 2, 3)]
+    return pl.pallas_call(
+        functools.partial(main_kernel, rounds),
+        out_shape=[f32(columns, ny, nz, nx)] + [padded, padded, pieces] * rounds,
+        in_specs=vmem(len(given)),
+        out_specs=vmem(1 + 3 * rounds),
+        input_output_aliases={i: 1 + k for k, i in enumerate(changed)},
+        scratch_shapes=main_scratch(rounds, ny, nz, nx),
+        compiler_params=params(20),
+        name="main",
+    )(*given)[0]
 
 
 def solution(mesh):

time: 78.9 us -> 77.7 us (0.985)
  Pallas kernels: 27 us -> 25.5 us
    pallas_call x2, Pallas kernels: 20.6 us -> 19.1 us  [the longest x1 17 us: body(): pl.pallas_call(functools.partial(main_kernel, rounds), out_shape=[f32(col...]
  transfers between devices with their start and end apart: 19 -> 19, of which waited for: 10 -> 10; matrix products, arithmetic and copies ran while one was open for 1% -> 1% of each run, Pallas kernels for 7% -> 10%
where the time goes in v5:
time: 77.7 us; the launch traced here: 77.5 us
  waiting for transfers between devices  26.7 us (34%)
  Pallas kernels  25.5 us (33%)
  starting transfers between devices  22.2 us (29%)
  local copies, waits for them, and re-layouts  2.97 us (4%)
    pallas_call x1, Pallas kernels, body(): pl.pallas_call(functools.partial(main_kernel, rounds), out_shape=[f32(col...  17 us
    ppermute x7, waiting for transfers between devices, exchange(): got[k] = lax.ppermute(piece, 'cols', [(i, i ^ k) for i in range(n)])  13.2 us
    ppermute x4, waiting for transfers between devices, body(): behind = lax.ppermute(behind, 'cols', counter)  11.7 us
    ppermute x7, starting transfers between devices, exchange(): got[k] = lax.ppermute(piece, 'cols', [(i, i ^ k) for i in range(n)])  10.7 us
    ppermute x4, starting transfers between devices, body(): behind = lax.ppermute(behind, 'cols', counter)  4.47 us
    ppermute x4, starting transfers between devices, body(): ahead = lax.ppermute(ahead, 'cols', clockwise)  3.43 us
    pallas_call x1, Pallas kernels, body(): pl.pallas_call(prepare_kernel, out_shape=[f32(ny // 2, nz, nx), f32(ny, n...  2.96 us
    slice x2, local copies, waits for them, and re-layouts, exchange(): sent = [pieces[k:k + 1] for k in group]  2.27 us
  transfers between devices with their start and end apart: 19, of which 10 were waited for; matrix products, arithmetic and copies ran while one was open for 1% of the time, Pallas kernels for 10%

profile of v5, /device:TPU:0, one launch (start us, length us, event | category | flops | bytes accessed | tf_op | source)
XLA Modules:
  0.0 77.5 jit_solution(160253388042303435)
XLA Ops:
  0.0 0.0 copy-start
  0.0 0.0 copy-start.1
  0.0 1.3 %fusion.1 = (f32[1,2,96,128]{3,2,1,0:T(8,128)S(1)}, f32[1,2,96,128]{3,2,1,0:T(8,128)S(1)}, f32[1,2,96,128]{3,2,1,0:T(8,128)S(1)}, f32[1,2,96,128]{3,2,1,0:T(8,128)S(1)}, f32[1,2,96,128]{3,2,1,0:T(8,128)S(1)}) fusion(f32[1,16,96,128]{3,2,1,0:T(8,128)} %param.7), kind=kLoop, calls=%fused_computation.1 | loop fusion | bytes 983040 | tf_op jit(solution)/shard_map/slice | solution.py:316
  1.3 4.1 %collective-permute-start.3 = (f32[1,192,128]{2,1,0:T(8,128)S(1)}, f32[1,192,128]{2,1,0:T(8,128)S(1)}, u32[]{:S(2)}, u32[]{:S(2)}) collective-permute-start(f32[1,192,128]{2,1,0:T(8,128)S(1)} %bitcast.14), channel_id=1, source_target_pairs={{0,16},{4,20},{8,24},{12,28},{16,0},{20,4},{24,8},{28,12},{1,17},{... | collective-permute-start | bytes 294920 | tf_op jit(solution)/shard_map/ppermute | solution.py:319
  5.4 1.3 %collective-permute-start.4 = (f32[1,192,128]{2,1,0:T(8,128)S(1)}, f32[1,192,128]{2,1,0:T(8,128)S(1)}, u32[]{:S(2)}, u32[]{:S(2)}) collective-permute-start(f32[1,192,128]{2,1,0:T(8,128)S(1)} %bitcast.13), channel_id=1, source_target_pairs={{0,20},{4,16},{8,28},{12,24},{16,4},{20,0},{24,12},{28,8},{1,21},{... | collective-permute-start | bytes 294920 | tf_op jit(solution)/shard_map/ppermute | solution.py:319
  6.7 3.6 %collective-permute-start.5 = (f32[1,192,128]{2,1,0:T(8,128)S(1)}, f32[1,192,128]{2,1,0:T(8,128)S(1)}, u32[]{:S(2)}, u32[]{:S(2)}) collective-permute-start(f32[1,192,128]{2,1,0:T(8,128)S(1)} %bitcast.12), channel_id=1, source_target_pairs={{0,24},{4,28},{8,16},{12,20},{16,8},{20,12},{24,0},{28,4},{1,25},{... | collective-permute-start | bytes 294920 | tf_op jit(solution)/shard_map/ppermute | solution.py:319
  10.3 0.0 collective-permute-start.6
  10.3 1.0 %fusion = (f32[1,192,128]{2,1,0:T(8,128)S(1)}, f32[1,192,128]{2,1,0:T(8,128)S(1)}, f32[1,192,128]{2,1,0:T(8,128)S(1)}) fusion(f32[8,192,128]{2,1,0:T(8,128)} %bitcast.10), kind=kLoop, calls=%fused_computation | loop fusion | bytes 589824 | tf_op jit(solution)/shard_map/slice | solution.py:316
  11.3 1.7 %collective-permute-start = (f32[1,192,128]{2,1,0:T(8,128)S(1)}, f32[1,192,128]{2,1,0:T(8,128)S(1)}, u32[]{:S(2)}, u32[]{:S(2)}) collective-permute-start(f32[1,192,128]{2,1,0:T(8,128)S(1)} %get-tuple-element.32), channel_id=1, source_target_pairs={{0,4},{4,0},{8,12},{12,8},{16,20},{20,16},{24,28},{28,24},{1,5},{5... | collective-permute-start | bytes 294920 | tf_op jit(solution)/shard_map/ppermute | solution.py:319
  13.0 4.5 %collective-permute-done.3.refs_4_ = f32[1,192,128]{2,1,0:T(8,128)S(1)} collective-permute-done((f32[1,192,128]{2,1,0:T(8,128)S(1)}, f32[1,192,128]{2,1,0:T(8,128)S(1)}, u32[]{:S(2)}, u32[]{:S(2)}) %collective-permute-start.3) | collective-permute-done | bytes 98336 | tf_op jit(solution)/shard_map/ppermute | solution.py:319
  17.5 0.0 collective-permute-start.1
  17.5 3.2 %collective-permute-done.4.refs_5_ = f32[1,192,128]{2,1,0:T(8,128)S(1)} collective-permute-done((f32[1,192,128]{2,1,0:T(8,128)S(1)}, f32[1,192,128]{2,1,0:T(8,128)S(1)}, u32[]{:S(2)}, u32[]{:S(2)}) %collective-permute-start.4) | collective-permute-done | bytes 98336 | tf_op jit(solution)/shard_map/ppermute | solution.py:319
  20.7 0.0 collective-permute-start.2
  20.7 0.0 collective-permute-done.5.refs_6_
  20.7 0.0 collective-permute-done.6.refs_7_
  20.7 0.0 collective-permute-done.refs_1_
  20.7 2.1 %collective-permute-done.1.refs_2_ = f32[1,192,128]{2,1,0:T(8,128)S(1)} collective-permute-done((f32[1,192,128]{2,1,0:T(8,128)S(1)}, f32[1,192,128]{2,1,0:T(8,128)S(1)}, u32[]{:S(2)}, u32[]{:S(2)}) %collective-permute-start.1) | collective-permute-done | bytes 98336 | tf_op jit(solution)/shard_map/ppermute | solution.py:319
  22.8 3.4 %collective-permute-done.2.refs_3_ = f32[1,192,128]{2,1,0:T(8,128)S(1)} collective-permute-done((f32[1,192,128]{2,1,0:T(8,128)S(1)}, f32[1,192,128]{2,1,0:T(8,128)S(1)}, u32[]{:S(2)}, u32[]{:S(2)}) %collective-permute-start.2) | collective-permute-done | bytes 98336 | tf_op jit(solution)/shard_map/ppermute | solution.py:319
  26.2 0.0 copy-start.4
  26.2 0.7 copy-done.4
  26.9 0.0 copy-start.5
  26.9 0.7 pick.1.refs_0_
  27.6 0.4 collective-permute-start.8
  28.0 1.7 %collective-permute-start.7 = (f32[2,192,128]{2,1,0:T(8,128)S(1)}, f32[2,192,128]{2,1,0:T(8,128)S(1)}, u32[]{:S(2)}, u32[]{:S(2)}) collective-permute-start(f32[2,192,128]{2,1,0:T(8,128)S(1)} %pick.1.refs_0_), channel_id=1, source_target_pairs={{0,8},{8,16},{16,24},{24,28},{28,20},{20,12},{12,4},{4,0},{1,9},{9... | collective-permute-start | bytes 589832 | tf_op jit(solution)/shard_map/ppermute | solution.py:385
  29.7 3.6 %collective-permute-done.8.refs_2_ = f32[2,192,128]{2,1,0:T(8,128)S(1)} collective-permute-done((f32[2,192,128]{2,1,0:T(8,128)S(1)}, f32[2,192,128]{2,1,0:T(8,128)S(1)}, u32[]{:S(2)}, u32[]{:S(2)}) %collective-permute-start.8) | collective-permute-done | bytes 196640 | tf_op jit(solution)/shard_map/ppermute | solution.py:386
  33.3 1.0 %collective-permute-start.10 = (f32[2,192,128]{2,1,0:T(8,128)S(1)}, f32[2,192,128]{2,1,0:T(8,128)S(1)}, u32[]{:S(2)}, u32[]{:S(2)}) collective-permute-start(f32[2,192,128]{2,1,0:T(8,128)S(1)} %collective-permute-done.8.refs_2_), channel_id=1, source_target_pairs={{8,0},{16,8},{24,16},{28,24},{20,28},{12,20},{4,12},{0,4},{9,1},{1... | collective-permute-start | bytes 589832 | tf_op jit(solution)/shard_map/ppermute | solution.py:386
  34.3 0.0 collective-permute-done.7.refs_1_
  34.3 1.0 %collective-permute-start.9 = (f32[2,192,128]{2,1,0:T(8,128)S(1)}, f32[2,192,128]{2,1,0:T(8,128)S(1)}, u32[]{:S(2)}, u32[]{:S(2)}) collective-permute-start(f32[2,192,128]{2,1,0:T(8,128)S(1)} %collective-permute-done.7.refs_1_), channel_id=1, source_target_pairs={{0,8},{8,16},{16,24},{24,28},{28,20},{20,12},{12,4},{4,0},{1,9},{9... | collective-permute-start | bytes 589832 | tf_op jit(solution)/shard_map/ppermute | solution.py:385
  35.3 3.6 %collective-permute-done.10.refs_4_ = f32[2,192,128]{2,1,0:T(8,128)S(1)} collective-permute-done((f32[2,192,128]{2,1,0:T(8,128)S(1)}, f32[2,192,128]{2,1,0:T(8,128)S(1)}, u32[]{:S(2)}, u32[]{:S(2)}) %collective-permute-start.10) | collective-permute-done | bytes 196640 | tf_op jit(solution)/shard_map/ppermute | solution.py:386
  39.0 1.4 %collective-permute-start.12 = (f32[2,192,128]{2,1,0:T(8,128)S(1)}, f32[2,192,128]{2,1,0:T(8,128)S(1)}, u32[]{:S(2)}, u32[]{:S(2)}) collective-permute-start(f32[2,192,128]{2,1,0:T(8,128)S(1)} %collective-permute-done.10.refs_4_), channel_id=1, source_target_pairs={{8,0},{16,8},{24,16},{28,24},{20,28},{12,20},{4,12},{0,4},{9,1},{1... | collective-permute-start | bytes 589832 | tf_op jit(solution)/shard_map/ppermute | solution.py:386
  40.3 0.3 collective-permute-done.9.refs_3_
  40.6 0.4 collective-permute-start.11
  41.0 4.4 %collective-permute-done.12.refs_6_ = f32[2,192,128]{2,1,0:T(8,128)S(1)} collective-permute-done((f32[2,192,128]{2,1,0:T(8,128)S(1)}, f32[2,192,128]{2,1,0:T(8,128)S(1)}, u32[]{:S(2)}, u32[]{:S(2)}) %collective-permute-start.12) | collective-permute-done | bytes 196640 | tf_op jit(solution)/shard_map/ppermute | solution.py:386
  45.4 1.7 %collective-permute-start.14 = (f32[2,96,128]{2,1,0:T(8,128)S(1)}, f32[2,96,128]{2,1,0:T(8,128)S(1)}, u32[]{:S(2)}, u32[]{:S(2)}) collective-permute-start(f32[2,96,128]{2,1,0:T(8,128)S(1)} %slice.61), channel_id=1, source_target_pairs={{8,0},{16,8},{24,16},{28,24},{20,28},{12,20},{4,12},{0,4},{9,1},{1... | collective-permute-start | bytes 294920 | tf_op jit(solution)/shard_map/ppermute | solution.py:386
  47.1 0.2 collective-permute-done.11.refs_5_
  47.4 0.3 collective-permute-start.13
  47.7 0.0 copy-done
  47.7 0.0 copy-done.1
  47.7 1.2 %shard_map.64 = (f32[3,96,128]{2,1,0:T(8,128)S(1)}, f32[3,96,128]{2,1,0:T(8,128)S(1)}) custom-call(f32[2,16,96,128]{3,2,1,0:T(8,128)S(1)} %copy-done, f32[16,96,128]{2,1,0:T(8,128)S(1)} %copy-done.1), custom_call_target="tpu_custom_call" | custom-call | bytes 6291456 | tf_op jit(solution)/shard_map/pallas_call | solution.py:347
  49.0 0.1 collective-permute-start.17
  49.0 1.7 %collective-permute-start.18 = (f32[3,96,128]{2,1,0:T(8,128)S(1)}, f32[3,96,128]{2,1,0:T(8,128)S(1)}, u32[]{:S(2)}, u32[]{:S(2)}) collective-permute-start(f32[3,96,128]{2,1,0:T(8,128)S(1)} %get-tuple-element.43), channel_id=1, source_target_pairs={{1,0},{2,1},{3,2},{0,3},{5,4},{6,5},{7,6},{4,7},{9,8},{10,9},{11,1... | collective-permute-start | bytes 442376 | tf_op jit(solution)/shard_map/ppermute | solution.py:356
  50.8 0.0 collective-permute-done.14.refs_8_
  50.8 1.3 %collective-permute-done.13.refs_7_ = f32[2,96,128]{2,1,0:T(8,128)S(1)} collective-permute-done((f32[2,96,128]{2,1,0:T(8,128)S(1)}, f32[2,96,128]{2,1,0:T(8,128)S(1)}, u32[]{:S(2)}, u32[]{:S(2)}) %collective-permute-start.13) | collective-permute-done | bytes 98336 | tf_op jit(solution)/shard_map/ppermute | solution.py:385
  52.0 0.0 copy-done.5
  52.0 1.5 %gather.1 = (f32[2,1536,128]{2,1,0:T(8,128)S(1)}, f32[2,96,128]{2,1,0:T(8,128)S(1)}, f32[2,96,128]{2,1,0:T(8,128)S(1)}) custom-call(s32[2]{0:T(128)S(1)} %copy-done.5, f32[2,192,128]{2,1,0:T(8,128)S(1)} %pick.1.refs_0_, f32[2,192,128]{2,1,0:T(8,128)S(1)} %collective-permute-done.7.refs_1_, f32[2,192,128]{2,1,0:T(8,128)S(1)} %collective-permute-done.8.refs_2_, ...), custom_call_target="tpu_custom_call" | custom-call | tf_op jit(solution)/shard_map/gather/pallas_call | solution.py:389
  53.6 0.1 collective-permute-start.15
  53.6 0.0 copy-start.2
  53.6 0.0 copy-start.3
  53.6 1.7 %collective-permute-start.16 = (f32[2,96,128]{2,1,0:T(8,128)S(1)}, f32[2,96,128]{2,1,0:T(8,128)S(1)}, u32[]{:S(2)}, u32[]{:S(2)}) collective-permute-start(f32[2,96,128]{2,1,0:T(8,128)S(1)} %get-tuple-element.41), channel_id=1, source_target_pairs={{1,0},{2,1},{3,2},{0,3},{5,4},{6,5},{7,6},{4,7},{9,8},{10,9},{11,1... | collective-permute-start | bytes 294920 | tf_op jit(solution)/shard_map/ppermute | solution.py:399
  55.4 0.0 collective-permute-done.17.left
  55.4 0.0 collective-permute-done.18.right
  55.4 3.0 %shard_map.65 = (f32[8,96,128]{2,1,0:T(8,128)S(1)}, f32[16,96,128]{2,1,0:T(8,128)S(1)}, f32[8,96,128]{2,1,0:T(8,128)S(1)}) custom-call(f32[2,16,96,128]{3,2,1,0:T(8,128)S(1)} %copy-done, f32[16,96,128]{2,1,0:T(8,128)S(1)} %copy-done.1, f32[3,96,128]{2,1,0:T(8,128)S(1)} %collective-permute-done.17.left, f32[3,96,128]{2,1,0:T(8,128)S(1)} %collective-permute-done.18.right), custom_call_target="tpu_custom_call" | custom-call | bytes 10485760 | tf_op jit(solution)/shard_map/pallas_call | solution.py:357
  58.3 2.1 %shard_map.66 = (f32[2,8,96,128]{3,2,1,0:T(8,128)S(1)}, f32[2,20,112,128]{3,2,1,0:T(8,128)S(1)}, f32[2,20,112,128]{3,2,1,0:T(8,128)S(1)}, f32[2,20,112,128]{3,2,...) custom-call(f32[2,16,96,128]{3,2,1,0:T(8,128)S(1)} %bitcast.7, ...), custom_call_target="tpu_custom_call" | custom-call | bytes 8388608 | tf_op jit(solution)/shard_map/pallas_call | solution.py:402
  60.4 0.0 collective-permute-done.15.left
  60.5 0.0 collective-permute-done.16.right
  60.5 0.0 copy-done.2
  60.5 0.0 copy-done.3
  60.5 17.0 %main.1 = (f32[2,16,96,128]{3,2,1,0:T(8,128)}, f32[2,20,112,128]{3,2,1,0:T(8,128)S(1)}, f32[2,20,112,128]{3,2,1,0:T(8,128)S(1)}, bf16[1536,768]{1,0:T(8,128)(2,1...) custom-call(f32[2,16,96,128]{3,2,1,0:T(8,128)S(1)} %bitcast.8, ...), custom_call_target="tpu_custom_call", output_to_operand_aliasing={{1}: (10, {}), {2}: (11, {}), {3}: (12, {}), {4}: (14, {}),... | custom-call | tf_op jit(solution)/shard_map/main/pallas_call | solution.py:412
  (2 shorter events, 0.0 us)
Async XLA Ops:
  0.0 47.7 %copy-start = (f32[2,16,96,128]{3,2,1,0:T(8,128)S(1)}, f32[2,16,96,128]{3,2,1,0:T(8,128)}, u32[]{:S(2)}) copy-start(f32[2,16,96,128]{3,2,1,0:T(8,128)} %trial.5) | copy-start | bytes 4718596
  0.0 47.7 %copy-start.1 = (f32[16,96,128]{2,1,0:T(8,128)S(1)}, f32[16,96,128]{2,1,0:T(8,128)}, u32[]{:S(2)}) copy-start(f32[16,96,128]{2,1,0:T(8,128)} %potential.3) | copy-start | bytes 2359300
  1.3 16.2 %collective-permute-start.3 = (f32[1,192,128]{2,1,0:T(8,128)S(1)}, f32[1,192,128]{2,1,0:T(8,128)S(1)}, u32[]{:S(2)}, u32[]{:S(2)}) collective-permute-start(f32[1,192,128]{2,1,0:T(8,128)S(1)} %bitcast.14), channel_id=1, source_target_pairs={{0,16},{4,20},{8,24},{12,28},{16,0},{20,4},{24,8},{28,12},{1,17},{... | collective-permute-start | bytes 294920 | tf_op jit(solution)/shard_map/ppermute | solution.py:319
  5.4 15.3 %collective-permute-start.4 = (f32[1,192,128]{2,1,0:T(8,128)S(1)}, f32[1,192,128]{2,1,0:T(8,128)S(1)}, u32[]{:S(2)}, u32[]{:S(2)}) collective-permute-start(f32[1,192,128]{2,1,0:T(8,128)S(1)} %bitcast.13), channel_id=1, source_target_pairs={{0,20},{4,16},{8,28},{12,24},{16,4},{20,0},{24,12},{28,8},{1,21},{... | collective-permute-start | bytes 294920 | tf_op jit(solution)/shard_map/ppermute | solution.py:319
  6.7 14.0 %collective-permute-start.5 = (f32[1,192,128]{2,1,0:T(8,128)S(1)}, f32[1,192,128]{2,1,0:T(8,128)S(1)}, u32[]{:S(2)}, u32[]{:S(2)}) collective-permute-start(f32[1,192,128]{2,1,0:T(8,128)S(1)} %bitcast.12), channel_id=1, source_target_pairs={{0,24},{4,28},{8,16},{12,20},{16,8},{20,12},{24,0},{28,4},{1,25},{... | collective-permute-start | bytes 294920 | tf_op jit(solution)/shard_map/ppermute | solution.py:319
  10.3 10.4 %collective-permute-start.6 = (f32[1,192,128]{2,1,0:T(8,128)S(1)}, f32[1,192,128]{2,1,0:T(8,128)S(1)}, u32[]{:S(2)}, u32[]{:S(2)}) collective-permute-start(f32[1,192,128]{2,1,0:T(8,128)S(1)} %bitcast.11), channel_id=1, source_target_pairs={{0,28},{4,24},{8,20},{12,16},{16,12},{20,8},{24,4},{28,0},{1,29},{... | collective-permute-start | bytes 294920 | tf_op jit(solution)/shard_map/ppermute | solution.py:319
  11.3 9.4 %collective-permute-start = (f32[1,192,128]{2,1,0:T(8,128)S(1)}, f32[1,192,128]{2,1,0:T(8,128)S(1)}, u32[]{:S(2)}, u32[]{:S(2)}) collective-permute-start(f32[1,192,128]{2,1,0:T(8,128)S(1)} %get-tuple-element.32), channel_id=1, source_target_pairs={{0,4},{4,0},{8,12},{12,8},{16,20},{20,16},{24,28},{28,24},{1,5},{5... | collective-permute-start | bytes 294920 | tf_op jit(solution)/shard_map/ppermute | solution.py:319
  17.5 5.3 %collective-permute-start.1 = (f32[1,192,128]{2,1,0:T(8,128)S(1)}, f32[1,192,128]{2,1,0:T(8,128)S(1)}, u32[]{:S(2)}, u32[]{:S(2)}) collective-permute-start(f32[1,192,128]{2,1,0:T(8,128)S(1)} %get-tuple-element.33), channel_id=1, source_target_pairs={{0,8},{4,12},{8,0},{12,4},{16,24},{20,28},{24,16},{28,20},{1,9},{5... | collective-permute-start | bytes 294920 | tf_op jit(solution)/shard_map/ppermute | solution.py:319
  20.7 5.5 %collective-permute-start.2 = (f32[1,192,128]{2,1,0:T(8,128)S(1)}, f32[1,192,128]{2,1,0:T(8,128)S(1)}, u32[]{:S(2)}, u32[]{:S(2)}) collective-permute-start(f32[1,192,128]{2,1,0:T(8,128)S(1)} %get-tuple-element.34), channel_id=1, source_target_pairs={{0,12},{4,8},{8,4},{12,0},{16,28},{20,24},{24,20},{28,16},{1,13},{... | collective-permute-start | bytes 294920 | tf_op jit(solution)/shard_map/ppermute | solution.py:319
  26.2 0.7 copy-start.4
  26.9 25.2 %copy-start.5 = (s32[2]{0:T(128)S(1)}, s32[2]{0:T(128)}, u32[]{:S(2)}) copy-start(s32[2]{0:T(128)} %owner.3) | copy-start | bytes 28
  27.6 5.7 %collective-permute-start.8 = (f32[2,192,128]{2,1,0:T(8,128)S(1)}, f32[2,192,128]{2,1,0:T(8,128)S(1)}, u32[]{:S(2)}, u32[]{:S(2)}) collective-permute-start(f32[2,192,128]{2,1,0:T(8,128)S(1)} %pick.1.refs_0_), channel_id=1, source_target_pairs={{8,0},{16,8},{24,16},{28,24},{20,28},{12,20},{4,12},{0,4},{9,1},{1... | collective-permute-start | bytes 589832 | tf_op jit(solution)/shard_map/ppermute | solution.py:386
  28.0 6.3 %collective-permute-start.7 = (f32[2,192,128]{2,1,0:T(8,128)S(1)}, f32[2,192,128]{2,1,0:T(8,128)S(1)}, u32[]{:S(2)}, u32[]{:S(2)}) collective-permute-start(f32[2,192,128]{2,1,0:T(8,128)S(1)} %pick.1.refs_0_), channel_id=1, source_target_pairs={{0,8},{8,16},{16,24},{24,28},{28,20},{20,12},{12,4},{4,0},{1,9},{9... | collective-permute-start | bytes 589832 | tf_op jit(solution)/shard_map/ppermute | solution.py:385
  33.3 5.7 %collective-permute-start.10 = (f32[2,192,128]{2,1,0:T(8,128)S(1)}, f32[2,192,128]{2,1,0:T(8,128)S(1)}, u32[]{:S(2)}, u32[]{:S(2)}) collective-permute-start(f32[2,192,128]{2,1,0:T(8,128)S(1)} %collective-permute-done.8.refs_2_), channel_id=1, source_target_pairs={{8,0},{16,8},{24,16},{28,24},{20,28},{12,20},{4,12},{0,4},{9,1},{1... | collective-permute-start | bytes 589832 | tf_op jit(solution)/shard_map/ppermute | solution.py:386
  34.3 6.3 %collective-permute-start.9 = (f32[2,192,128]{2,1,0:T(8,128)S(1)}, f32[2,192,128]{2,1,0:T(8,128)S(1)}, u32[]{:S(2)}, u32[]{:S(2)}) collective-permute-start(f32[2,192,128]{2,1,0:T(8,128)S(1)} %collective-permute-done.7.refs_1_), channel_id=1, source_target_pairs={{0,8},{8,16},{16,24},{24,28},{28,20},{20,12},{12,4},{4,0},{1,9},{9... | collective-permute-start | bytes 589832 | tf_op jit(solution)/shard_map/ppermute | solution.py:385
  39.0 6.4 %collective-permute-start.12 = (f32[2,192,128]{2,1,0:T(8,128)S(1)}, f32[2,192,128]{2,1,0:T(8,128)S(1)}, u32[]{:S(2)}, u32[]{:S(2)}) collective-permute-start(f32[2,192,128]{2,1,0:T(8,128)S(1)} %collective-permute-done.10.refs_4_), channel_id=1, source_target_pairs={{8,0},{16,8},{24,16},{28,24},{20,28},{12,20},{4,12},{0,4},{9,1},{1... | collective-permute-start | bytes 589832 | tf_op jit(solution)/shard_map/ppermute | solution.py:386
  40.6 6.7 %collective-permute-start.11 = (f32[2,192,128]{2,1,0:T(8,128)S(1)}, f32[2,192,128]{2,1,0:T(8,128)S(1)}, u32[]{:S(2)}, u32[]{:S(2)}) collective-permute-start(f32[2,192,128]{2,1,0:T(8,128)S(1)} %collective-permute-done.9.refs_3_), channel_id=1, source_target_pairs={{0,8},{8,16},{16,24},{24,28},{28,20},{20,12},{12,4},{4,0},{1,9},{9... | collective-permute-start | bytes 589832 | tf_op jit(solution)/shard_map/ppermute | solution.py:385
  45.4 5.3 %collective-permute-start.14 = (f32[2,96,128]{2,1,0:T(8,128)S(1)}, f32[2,96,128]{2,1,0:T(8,128)S(1)}, u32[]{:S(2)}, u32[]{:S(2)}) collective-permute-start(f32[2,96,128]{2,1,0:T(8,128)S(1)} %slice.61), channel_id=1, source_target_pairs={{8,0},{16,8},{24,16},{28,24},{20,28},{12,20},{4,12},{0,4},{9,1},{1... | collective-permute-start | bytes 294920 | tf_op jit(solution)/shard_map/ppermute | solution.py:386
  47.4 4.7 %collective-permute-start.13 = (f32[2,96,128]{2,1,0:T(8,128)S(1)}, f32[2,96,128]{2,1,0:T(8,128)S(1)}, u32[]{:S(2)}, u32[]{:S(2)}) collective-permute-start(f32[2,96,128]{2,1,0:T(8,128)S(1)} %slice.60), channel_id=1, source_target_pairs={{0,8},{8,16},{16,24},{24,28},{28,20},{20,12},{12,4},{4,0},{1,9},{9... | collective-permute-start | bytes 294920 | tf_op jit(solution)/shard_map/ppermute | solution.py:385
  49.0 6.4 %collective-permute-start.17 = (f32[3,96,128]{2,1,0:T(8,128)S(1)}, f32[3,96,128]{2,1,0:T(8,128)S(1)}, u32[]{:S(2)}, u32[]{:S(2)}) collective-permute-start(f32[3,96,128]{2,1,0:T(8,128)S(1)} %get-tuple-element.42), channel_id=1, source_target_pairs={{0,1},{1,2},{2,3},{3,0},{4,5},{5,6},{6,7},{7,4},{8,9},{9,10},{10,1... | collective-permute-start | bytes 442376 | tf_op jit(solution)/shard_map/ppermute | solution.py:355
  49.0 6.3 %collective-permute-start.18 = (f32[3,96,128]{2,1,0:T(8,128)S(1)}, f32[3,96,128]{2,1,0:T(8,128)S(1)}, u32[]{:S(2)}, u32[]{:S(2)}) collective-permute-start(f32[3,96,128]{2,1,0:T(8,128)S(1)} %get-tuple-element.43), channel_id=1, source_target_pairs={{1,0},{2,1},{3,2},{0,3},{5,4},{6,5},{7,6},{4,7},{9,8},{10,9},{11,1... | collective-permute-start | bytes 442376 | tf_op jit(solution)/shard_map/ppermute | solution.py:356
  53.6 6.9 %collective-permute-start.15 = (f32[2,96,128]{2,1,0:T(8,128)S(1)}, f32[2,96,128]{2,1,0:T(8,128)S(1)}, u32[]{:S(2)}, u32[]{:S(2)}) collective-permute-start(f32[2,96,128]{2,1,0:T(8,128)S(1)} %get-tuple-element.40), channel_id=1, source_target_pairs={{0,1},{1,2},{2,3},{3,0},{4,5},{5,6},{6,7},{7,4},{8,9},{9,10},{10,1... | collective-permute-start | bytes 294920 | tf_op jit(solution)/shard_map/ppermute | solution.py:398
  53.6 6.8 %copy-start.2 = (bf16[2,768,256]{2,1,0:T(8,128)(2,1)S(1)}, bf16[2,768,256]{2,1,0:T(8,128)(2,1)}, u32[]{:S(2)}) copy-start(bf16[2,768,256]{2,1,0:T(8,128)(2,1)} %constant.4.clone.bands) | copy-start | bytes 2359300
  53.6 6.8 %copy-start.3 = (bf16[256,128]{1,0:T(8,128)(2,1)S(1)}, bf16[256,128]{1,0:T(8,128)(2,1)}, u32[]{:S(2)}) copy-start(bf16[256,128]{1,0:T(8,128)(2,1)} %constant.5.clone.halo_bands) | copy-start | bytes 196612
  53.6 6.8 %collective-permute-start.16 = (f32[2,96,128]{2,1,0:T(8,128)S(1)}, f32[2,96,128]{2,1,0:T(8,128)S(1)}, u32[]{:S(2)}, u32[]{:S(2)}) collective-permute-start(f32[2,96,128]{2,1,0:T(8,128)S(1)} %get-tuple-element.41), channel_id=1, source_target_pairs={{1,0},{2,1},{3,2},{0,3},{5,4},{6,5},{7,6},{4,7},{9,8},{10,9},{11,1... | collective-permute-start | bytes 294920 | tf_op jit(solution)/shard_map/ppermute | solution.py:399

commit v6 on v5

--- a/solution.py
+++ b/solution.py
@@ -17,7 +17,7 @@
 ZP = 8
 CHUNK = 32
 SHORT = 16
-DEPTH = 4
+DEPTH = 8
 
 
 def lanes(rows):
@@ -229,19 +229,24 @@
             arrays[4 * r + 3][: half * nz, 512:], halo_bands[...], preferred_element_type=jnp.float32
         )
 
-        @pl.loop(0, half)
-        def _(y):
-            for z in range(0, nz, CHUNK):
-                rows = pl.ds(ZP + z, CHUNK)
-                f = source[0, y + 2, rows]
-                near, far = rows_around(source, 0, y + 2, ZP + z, CHUNK)
-                near = near + (source[0, y + 1, rows] + source[0, y + 3, rows])
-                far = far + (source[0, y, rows] + source[0, y + 4, rows])
-                along = halo_sums[pl.ds(pl.multiple_of(y * nz + z, CHUNK), CHUNK), :]
-                value = (far + along) - 16.0 * near + (scaled_halo[y, pl.ds(z, CHUNK)] - shift) * f
-                if weight:
-                    value = value - weight * first[0, y + 2, rows]
-                put_halo(r, target, y, z, value)
+        @pl.loop(0, half // 4)
+        def _(block):
+            for z in range(0, nz, SHORT):
+                rows = pl.ds(ZP + z, SHORT)
+                planes = [source[0, 4 * block + k, rows] for k in range(8)]
+                for k in range(4):
+                    y = 4 * block + k
+                    near, far = rows_around(source, 0, y + 2, ZP + z, SHORT)
+                    near = near + (planes[k + 1] + planes[k + 3])
+                    far = far + (planes[k] + planes[k + 4])
+                    along = halo_sums[pl.ds(pl.multiple_of(y * nz + z, SHORT), SHORT), :]
+                    diagonal = scaled_halo[y, pl.ds(z, SHORT)]
+                    if shift:
+                        diagonal = diagonal - shift
+                    value = (far + along) - 16.0 * near + diagonal * planes[k + 2]
+                    if weight:
+                        value = value - weight * first[0, y + 2, rows]
+                    put_halo(r, target, y, z, value)
 
         wrap_halo(target, half, nz, full)
 
@@ -279,12 +284,11 @@
 
     steps = ((ALPHA, None), (0.0, BETA), (0.0, GAMMA))
     turns = [(step, r) for step in range(3) for r in range(rounds)]
-    for r in range(rounds):
+    start(0)
+    for block in range(blocks):
+        multiply(0, block)
+    for r in range(1, rounds):
         start(r)
-
-    @pl.loop(0, blocks)
-    def _(block):
-        multiply(0, block)
 
     for at, (step, r) in enumerate(turns):
         if step < 2:

time: 77.7 us -> 73.1 us (0.941)
  Pallas kernels: 25.5 us -> 21 us
    pallas_call x1, Pallas kernels: 17 us -> 12.5 us  [body(): pl.pallas_call(functools.partial(main_kernel, rounds), out_shape=[f32(col...]
  transfers between devices with their start and end apart: 19 -> 19, of which waited for: 10 -> 10; matrix products, arithmetic and copies ran while one was open for 1% -> 1% of each run, Pallas kernels for 10% -> 11%
where the time goes in v6:
time: 73.1 us; the launch traced here: 72.9 us
  waiting for transfers between devices  26.7 us (37%)
  starting transfers between devices  22.2 us (30%)
  Pallas kernels  21 us (29%)
  local copies, waits for them, and re-layouts  2.97 us (4%)
    ppermute x7, waiting for transfers between devices, exchange(): got[k] = lax.ppermute(piece, 'cols', [(i, i ^ k) for i in range(n)])  13.2 us
    pallas_call x1, Pallas kernels, body(): pl.pallas_call(functools.partial(main_kernel, rounds), out_shape=[f32(col...  12.5 us
    ppermute x4, waiting for transfers between devices, body(): behind = lax.ppermute(behind, 'cols', counter)  11.7 us
    ppermute x7, starting transfers between devices, exchange(): got[k] = lax.ppermute(piece, 'cols', [(i, i ^ k) for i in range(n)])  10.7 us
    ppermute x4, starting transfers between devices, body(): behind = lax.ppermute(behind, 'cols', counter)  4.47 us
    ppermute x4, starting transfers between devices, body(): ahead = lax.ppermute(ahead, 'cols', clockwise)  3.43 us
    pallas_call x1, Pallas kernels, body(): pl.pallas_call(prepare_kernel, out_shape=[f32(ny // 2, nz, nx), f32(ny, n...  2.96 us
    slice x2, local copies, waits for them, and re-layouts, exchange(): sent = [pieces[k:k + 1] for k in group]  2.27 us
  transfers between devices with their start and end apart: 19, of which 10 were waited for; matrix products, arithmetic and copies ran while one was open for 1% of the time, Pallas kernels for 11%

profile of v6, /device:TPU:0, one launch (start us, length us, event | category | flops | bytes accessed | tf_op | source)
XLA Modules:
  0.0 72.9 jit_solution(2132788823179477959)
XLA Ops:
  0.0 0.0 copy-start
  0.0 0.0 copy-start.1
  0.0 1.3 %fusion.1 = (f32[1,2,96,128]{3,2,1,0:T(8,128)S(1)}, f32[1,2,96,128]{3,2,1,0:T(8,128)S(1)}, f32[1,2,96,128]{3,2,1,0:T(8,128)S(1)}, f32[1,2,96,128]{3,2,1,0:T(8,128)S(1)}, f32[1,2,96,128]{3,2,1,0:T(8,128)S(1)}) fusion(f32[1,16,96,128]{3,2,1,0:T(8,128)} %param.7), kind=kLoop, calls=%fused_computation.1 | loop fusion | bytes 983040 | tf_op jit(solution)/shard_map/slice | solution.py:320
  1.3 4.1 %collective-permute-start.3 = (f32[1,192,128]{2,1,0:T(8,128)S(1)}, f32[1,192,128]{2,1,0:T(8,128)S(1)}, u32[]{:S(2)}, u32[]{:S(2)}) collective-permute-start(f32[1,192,128]{2,1,0:T(8,128)S(1)} %bitcast.14), channel_id=1, source_target_pairs={{0,16},{4,20},{8,24},{12,28},{16,0},{20,4},{24,8},{28,12},{1,17},{... | collective-permute-start | bytes 294920 | tf_op jit(solution)/shard_map/ppermute | solution.py:323
  5.4 1.3 %collective-permute-start.4 = (f32[1,192,128]{2,1,0:T(8,128)S(1)}, f32[1,192,128]{2,1,0:T(8,128)S(1)}, u32[]{:S(2)}, u32[]{:S(2)}) collective-permute-start(f32[1,192,128]{2,1,0:T(8,128)S(1)} %bitcast.13), channel_id=1, source_target_pairs={{0,20},{4,16},{8,28},{12,24},{16,4},{20,0},{24,12},{28,8},{1,21},{... | collective-permute-start | bytes 294920 | tf_op jit(solution)/shard_map/ppermute | solution.py:323
  6.7 3.6 %collective-permute-start.5 = (f32[1,192,128]{2,1,0:T(8,128)S(1)}, f32[1,192,128]{2,1,0:T(8,128)S(1)}, u32[]{:S(2)}, u32[]{:S(2)}) collective-permute-start(f32[1,192,128]{2,1,0:T(8,128)S(1)} %bitcast.12), channel_id=1, source_target_pairs={{0,24},{4,28},{8,16},{12,20},{16,8},{20,12},{24,0},{28,4},{1,25},{... | collective-permute-start | bytes 294920 | tf_op jit(solution)/shard_map/ppermute | solution.py:323
  10.3 0.0 collective-permute-start.6
  10.3 1.0 %fusion = (f32[1,192,128]{2,1,0:T(8,128)S(1)}, f32[1,192,128]{2,1,0:T(8,128)S(1)}, f32[1,192,128]{2,1,0:T(8,128)S(1)}) fusion(f32[8,192,128]{2,1,0:T(8,128)} %bitcast.10), kind=kLoop, calls=%fused_computation | loop fusion | bytes 589824 | tf_op jit(solution)/shard_map/slice | solution.py:320
  11.3 1.7 %collective-permute-start = (f32[1,192,128]{2,1,0:T(8,128)S(1)}, f32[1,192,128]{2,1,0:T(8,128)S(1)}, u32[]{:S(2)}, u32[]{:S(2)}) collective-permute-start(f32[1,192,128]{2,1,0:T(8,128)S(1)} %get-tuple-element.32), channel_id=1, source_target_pairs={{0,4},{4,0},{8,12},{12,8},{16,20},{20,16},{24,28},{28,24},{1,5},{5... | collective-permute-start | bytes 294920 | tf_op jit(solution)/shard_map/ppermute | solution.py:323
  13.0 4.5 %collective-permute-done.3.refs_4_ = f32[1,192,128]{2,1,0:T(8,128)S(1)} collective-permute-done((f32[1,192,128]{2,1,0:T(8,128)S(1)}, f32[1,192,128]{2,1,0:T(8,128)S(1)}, u32[]{:S(2)}, u32[]{:S(2)}) %collective-permute-start.3) | collective-permute-done | bytes 98336 | tf_op jit(solution)/shard_map/ppermute | solution.py:323
  17.5 0.0 collective-permute-start.1
  17.5 3.2 %collective-permute-done.4.refs_5_ = f32[1,192,128]{2,1,0:T(8,128)S(1)} collective-permute-done((f32[1,192,128]{2,1,0:T(8,128)S(1)}, f32[1,192,128]{2,1,0:T(8,128)S(1)}, u32[]{:S(2)}, u32[]{:S(2)}) %collective-permute-start.4) | collective-permute-done | bytes 98336 | tf_op jit(solution)/shard_map/ppermute | solution.py:323
  20.7 0.0 collective-permute-start.2
  20.7 0.0 collective-permute-done.5.refs_6_
  20.7 0.0 collective-permute-done.6.refs_7_
  20.7 0.0 collective-permute-done.refs_1_
  20.7 2.1 %collective-permute-done.1.refs_2_ = f32[1,192,128]{2,1,0:T(8,128)S(1)} collective-permute-done((f32[1,192,128]{2,1,0:T(8,128)S(1)}, f32[1,192,128]{2,1,0:T(8,128)S(1)}, u32[]{:S(2)}, u32[]{:S(2)}) %collective-permute-start.1) | collective-permute-done | bytes 98336 | tf_op jit(solution)/shard_map/ppermute | solution.py:323
  22.8 3.4 %collective-permute-done.2.refs_3_ = f32[1,192,128]{2,1,0:T(8,128)S(1)} collective-permute-done((f32[1,192,128]{2,1,0:T(8,128)S(1)}, f32[1,192,128]{2,1,0:T(8,128)S(1)}, u32[]{:S(2)}, u32[]{:S(2)}) %collective-permute-start.2) | collective-permute-done | bytes 98336 | tf_op jit(solution)/shard_map/ppermute | solution.py:323
  26.2 0.0 copy-start.4
  26.2 0.7 copy-done.4
  26.9 0.0 copy-start.5
  26.9 0.7 pick.1.refs_0_
  27.6 0.4 collective-permute-start.8
  28.0 1.7 %collective-permute-start.7 = (f32[2,192,128]{2,1,0:T(8,128)S(1)}, f32[2,192,128]{2,1,0:T(8,128)S(1)}, u32[]{:S(2)}, u32[]{:S(2)}) collective-permute-start(f32[2,192,128]{2,1,0:T(8,128)S(1)} %pick.1.refs_0_), channel_id=1, source_target_pairs={{0,8},{8,16},{16,24},{24,28},{28,20},{20,12},{12,4},{4,0},{1,9},{9... | collective-permute-start | bytes 589832 | tf_op jit(solution)/shard_map/ppermute | solution.py:389
  29.7 3.6 %collective-permute-done.8.refs_2_ = f32[2,192,128]{2,1,0:T(8,128)S(1)} collective-permute-done((f32[2,192,128]{2,1,0:T(8,128)S(1)}, f32[2,192,128]{2,1,0:T(8,128)S(1)}, u32[]{:S(2)}, u32[]{:S(2)}) %collective-permute-start.8) | collective-permute-done | bytes 196640 | tf_op jit(solution)/shard_map/ppermute | solution.py:390
  33.3 1.0 %collective-permute-start.10 = (f32[2,192,128]{2,1,0:T(8,128)S(1)}, f32[2,192,128]{2,1,0:T(8,128)S(1)}, u32[]{:S(2)}, u32[]{:S(2)}) collective-permute-start(f32[2,192,128]{2,1,0:T(8,128)S(1)} %collective-permute-done.8.refs_2_), channel_id=1, source_target_pairs={{8,0},{16,8},{24,16},{28,24},{20,28},{12,20},{4,12},{0,4},{9,1},{1... | collective-permute-start | bytes 589832 | tf_op jit(solution)/shard_map/ppermute | solution.py:390
  34.3 0.0 collective-permute-done.7.refs_1_
  34.3 1.0 %collective-permute-start.9 = (f32[2,192,128]{2,1,0:T(8,128)S(1)}, f32[2,192,128]{2,1,0:T(8,128)S(1)}, u32[]{:S(2)}, u32[]{:S(2)}) collective-permute-start(f32[2,192,128]{2,1,0:T(8,128)S(1)} %collective-permute-done.7.refs_1_), channel_id=1, source_target_pairs={{0,8},{8,16},{16,24},{24,28},{28,20},{20,12},{12,4},{4,0},{1,9},{9... | collective-permute-start | bytes 589832 | tf_op jit(solution)/shard_map/ppermute | solution.py:389
  35.3 3.6 %collective-permute-done.10.refs_4_ = f32[2,192,128]{2,1,0:T(8,128)S(1)} collective-permute-done((f32[2,192,128]{2,1,0:T(8,128)S(1)}, f32[2,192,128]{2,1,0:T(8,128)S(1)}, u32[]{:S(2)}, u32[]{:S(2)}) %collective-permute-start.10) | collective-permute-done | bytes 196640 | tf_op jit(solution)/shard_map/ppermute | solution.py:390
  39.0 1.4 %collective-permute-start.12 = (f32[2,192,128]{2,1,0:T(8,128)S(1)}, f32[2,192,128]{2,1,0:T(8,128)S(1)}, u32[]{:S(2)}, u32[]{:S(2)}) collective-permute-start(f32[2,192,128]{2,1,0:T(8,128)S(1)} %collective-permute-done.10.refs_4_), channel_id=1, source_target_pairs={{8,0},{16,8},{24,16},{28,24},{20,28},{12,20},{4,12},{0,4},{9,1},{1... | collective-permute-start | bytes 589832 | tf_op jit(solution)/shard_map/ppermute | solution.py:390
  40.3 0.3 collective-permute-done.9.refs_3_
  40.6 0.4 collective-permute-start.11
  41.0 4.4 %collective-permute-done.12.refs_6_ = f32[2,192,128]{2,1,0:T(8,128)S(1)} collective-permute-done((f32[2,192,128]{2,1,0:T(8,128)S(1)}, f32[2,192,128]{2,1,0:T(8,128)S(1)}, u32[]{:S(2)}, u32[]{:S(2)}) %collective-permute-start.12) | collective-permute-done | bytes 196640 | tf_op jit(solution)/shard_map/ppermute | solution.py:390
  45.4 1.7 %collective-permute-start.14 = (f32[2,96,128]{2,1,0:T(8,128)S(1)}, f32[2,96,128]{2,1,0:T(8,128)S(1)}, u32[]{:S(2)}, u32[]{:S(2)}) collective-permute-start(f32[2,96,128]{2,1,0:T(8,128)S(1)} %slice.61), channel_id=1, source_target_pairs={{8,0},{16,8},{24,16},{28,24},{20,28},{12,20},{4,12},{0,4},{9,1},{1... | collective-permute-start | bytes 294920 | tf_op jit(solution)/shard_map/ppermute | solution.py:390
  47.1 0.2 collective-permute-done.11.refs_5_
  47.4 0.3 collective-permute-start.13
  47.7 0.0 copy-done
  47.7 0.0 copy-done.1
  47.7 1.2 %shard_map.64 = (f32[3,96,128]{2,1,0:T(8,128)S(1)}, f32[3,96,128]{2,1,0:T(8,128)S(1)}) custom-call(f32[2,16,96,128]{3,2,1,0:T(8,128)S(1)} %copy-done, f32[16,96,128]{2,1,0:T(8,128)S(1)} %copy-done.1), custom_call_target="tpu_custom_call" | custom-call | bytes 6291456 | tf_op jit(solution)/shard_map/pallas_call | solution.py:351
  49.0 0.1 collective-permute-start.17
  49.0 1.7 %collective-permute-start.18 = (f32[3,96,128]{2,1,0:T(8,128)S(1)}, f32[3,96,128]{2,1,0:T(8,128)S(1)}, u32[]{:S(2)}, u32[]{:S(2)}) collective-permute-start(f32[3,96,128]{2,1,0:T(8,128)S(1)} %get-tuple-element.43), channel_id=1, source_target_pairs={{1,0},{2,1},{3,2},{0,3},{5,4},{6,5},{7,6},{4,7},{9,8},{10,9},{11,1... | collective-permute-start | bytes 442376 | tf_op jit(solution)/shard_map/ppermute | solution.py:360
  50.8 0.0 collective-permute-done.14.refs_8_
  50.8 1.3 %collective-permute-done.13.refs_7_ = f32[2,96,128]{2,1,0:T(8,128)S(1)} collective-permute-done((f32[2,96,128]{2,1,0:T(8,128)S(1)}, f32[2,96,128]{2,1,0:T(8,128)S(1)}, u32[]{:S(2)}, u32[]{:S(2)}) %collective-permute-start.13) | collective-permute-done | bytes 98336 | tf_op jit(solution)/shard_map/ppermute | solution.py:389
  52.0 0.0 copy-done.5
  52.0 1.5 %gather.1 = (f32[2,1536,128]{2,1,0:T(8,128)S(1)}, f32[2,96,128]{2,1,0:T(8,128)S(1)}, f32[2,96,128]{2,1,0:T(8,128)S(1)}) custom-call(s32[2]{0:T(128)S(1)} %copy-done.5, f32[2,192,128]{2,1,0:T(8,128)S(1)} %pick.1.refs_0_, f32[2,192,128]{2,1,0:T(8,128)S(1)} %collective-permute-done.7.refs_1_, f32[2,192,128]{2,1,0:T(8,128)S(1)} %collective-permute-done.8.refs_2_, ...), custom_call_target="tpu_custom_call" | custom-call | tf_op jit(solution)/shard_map/gather/pallas_call | solution.py:393
  53.6 0.1 collective-permute-start.15
  53.6 0.0 copy-start.2
  53.6 0.0 copy-start.3
  53.6 1.7 %collective-permute-start.16 = (f32[2,96,128]{2,1,0:T(8,128)S(1)}, f32[2,96,128]{2,1,0:T(8,128)S(1)}, u32[]{:S(2)}, u32[]{:S(2)}) collective-permute-start(f32[2,96,128]{2,1,0:T(8,128)S(1)} %get-tuple-element.41), channel_id=1, source_target_pairs={{1,0},{2,1},{3,2},{0,3},{5,4},{6,5},{7,6},{4,7},{9,8},{10,9},{11,1... | collective-permute-start | bytes 294920 | tf_op jit(solution)/shard_map/ppermute | solution.py:403
  55.4 0.0 collective-permute-done.17.left
  55.4 0.0 collective-permute-done.18.right
  55.4 3.0 %shard_map.65 = (f32[8,96,128]{2,1,0:T(8,128)S(1)}, f32[16,96,128]{2,1,0:T(8,128)S(1)}, f32[8,96,128]{2,1,0:T(8,128)S(1)}) custom-call(f32[2,16,96,128]{3,2,1,0:T(8,128)S(1)} %copy-done, f32[16,96,128]{2,1,0:T(8,128)S(1)} %copy-done.1, f32[3,96,128]{2,1,0:T(8,128)S(1)} %collective-permute-done.17.left, f32[3,96,128]{2,1,0:T(8,128)S(1)} %collective-permute-done.18.right), custom_call_target="tpu_custom_call" | custom-call | bytes 10485760 | tf_op jit(solution)/shard_map/pallas_call | solution.py:361
  58.3 2.1 %shard_map.66 = (f32[2,8,96,128]{3,2,1,0:T(8,128)S(1)}, f32[2,20,112,128]{3,2,1,0:T(8,128)S(1)}, f32[2,20,112,128]{3,2,1,0:T(8,128)S(1)}, f32[2,20,112,128]{3,2,...) custom-call(f32[2,16,96,128]{3,2,1,0:T(8,128)S(1)} %bitcast.7, ...), custom_call_target="tpu_custom_call" | custom-call | bytes 8388608 | tf_op jit(solution)/shard_map/pallas_call | solution.py:406
  60.4 0.0 collective-permute-done.15.left
  60.5 0.0 collective-permute-done.16.right
  60.5 0.0 copy-done.2
  60.5 0.0 copy-done.3
  60.5 12.5 %main.1 = (f32[2,16,96,128]{3,2,1,0:T(8,128)}, f32[2,20,112,128]{3,2,1,0:T(8,128)S(1)}, f32[2,20,112,128]{3,2,1,0:T(8,128)S(1)}, bf16[1536,768]{1,0:T(8,128)(2,1...) custom-call(f32[2,16,96,128]{3,2,1,0:T(8,128)S(1)} %bitcast.8, ...), custom_call_target="tpu_custom_call", output_to_operand_aliasing={{1}: (10, {}), {2}: (11, {}), {3}: (12, {}), {4}: (14, {}),... | custom-call | tf_op jit(solution)/shard_map/main/pallas_call | solution.py:416
  (2 shorter events, 0.0 us)
Async XLA Ops:
  0.0 47.7 %copy-start = (f32[2,16,96,128]{3,2,1,0:T(8,128)S(1)}, f32[2,16,96,128]{3,2,1,0:T(8,128)}, u32[]{:S(2)}) copy-start(f32[2,16,96,128]{3,2,1,0:T(8,128)} %trial.5) | copy-start | bytes 4718596
  0.0 47.7 %copy-start.1 = (f32[16,96,128]{2,1,0:T(8,128)S(1)}, f32[16,96,128]{2,1,0:T(8,128)}, u32[]{:S(2)}) copy-start(f32[16,96,128]{2,1,0:T(8,128)} %potential.3) | copy-start | bytes 2359300
  1.3 16.2 %collective-permute-start.3 = (f32[1,192,128]{2,1,0:T(8,128)S(1)}, f32[1,192,128]{2,1,0:T(8,128)S(1)}, u32[]{:S(2)}, u32[]{:S(2)}) collective-permute-start(f32[1,192,128]{2,1,0:T(8,128)S(1)} %bitcast.14), channel_id=1, source_target_pairs={{0,16},{4,20},{8,24},{12,28},{16,0},{20,4},{24,8},{28,12},{1,17},{... | collective-permute-start | bytes 294920 | tf_op jit(solution)/shard_map/ppermute | solution.py:323
  5.4 15.3 %collective-permute-start.4 = (f32[1,192,128]{2,1,0:T(8,128)S(1)}, f32[1,192,128]{2,1,0:T(8,128)S(1)}, u32[]{:S(2)}, u32[]{:S(2)}) collective-permute-start(f32[1,192,128]{2,1,0:T(8,128)S(1)} %bitcast.13), channel_id=1, source_target_pairs={{0,20},{4,16},{8,28},{12,24},{16,4},{20,0},{24,12},{28,8},{1,21},{... | collective-permute-start | bytes 294920 | tf_op jit(solution)/shard_map/ppermute | solution.py:323
  6.7 14.0 %collective-permute-start.5 = (f32[1,192,128]{2,1,0:T(8,128)S(1)}, f32[1,192,128]{2,1,0:T(8,128)S(1)}, u32[]{:S(2)}, u32[]{:S(2)}) collective-permute-start(f32[1,192,128]{2,1,0:T(8,128)S(1)} %bitcast.12), channel_id=1, source_target_pairs={{0,24},{4,28},{8,16},{12,20},{16,8},{20,12},{24,0},{28,4},{1,25},{... | collective-permute-start | bytes 294920 | tf_op jit(solution)/shard_map/ppermute | solution.py:323
  10.3 10.4 %collective-permute-start.6 = (f32[1,192,128]{2,1,0:T(8,128)S(1)}, f32[1,192,128]{2,1,0:T(8,128)S(1)}, u32[]{:S(2)}, u32[]{:S(2)}) collective-permute-start(f32[1,192,128]{2,1,0:T(8,128)S(1)} %bitcast.11), channel_id=1, source_target_pairs={{0,28},{4,24},{8,20},{12,16},{16,12},{20,8},{24,4},{28,0},{1,29},{... | collective-permute-start | bytes 294920 | tf_op jit(solution)/shard_map/ppermute | solution.py:323
  11.3 9.4 %collective-permute-start = (f32[1,192,128]{2,1,0:T(8,128)S(1)}, f32[1,192,128]{2,1,0:T(8,128)S(1)}, u32[]{:S(2)}, u32[]{:S(2)}) collective-permute-start(f32[1,192,128]{2,1,0:T(8,128)S(1)} %get-tuple-element.32), channel_id=1, source_target_pairs={{0,4},{4,0},{8,12},{12,8},{16,20},{20,16},{24,28},{28,24},{1,5},{5... | collective-permute-start | bytes 294920 | tf_op jit(solution)/shard_map/ppermute | solution.py:323
  17.5 5.3 %collective-permute-start.1 = (f32[1,192,128]{2,1,0:T(8,128)S(1)}, f32[1,192,128]{2,1,0:T(8,128)S(1)}, u32[]{:S(2)}, u32[]{:S(2)}) collective-permute-start(f32[1,192,128]{2,1,0:T(8,128)S(1)} %get-tuple-element.33), channel_id=1, source_target_pairs={{0,8},{4,12},{8,0},{12,4},{16,24},{20,28},{24,16},{28,20},{1,9},{5... | collective-permute-start | bytes 294920 | tf_op jit(solution)/shard_map/ppermute | solution.py:323
  20.7 5.5 %collective-permute-start.2 = (f32[1,192,128]{2,1,0:T(8,128)S(1)}, f32[1,192,128]{2,1,0:T(8,128)S(1)}, u32[]{:S(2)}, u32[]{:S(2)}) collective-permute-start(f32[1,192,128]{2,1,0:T(8,128)S(1)} %get-tuple-element.34), channel_id=1, source_target_pairs={{0,12},{4,8},{8,4},{12,0},{16,28},{20,24},{24,20},{28,16},{1,13},{... | collective-permute-start | bytes 294920 | tf_op jit(solution)/shard_map/ppermute | solution.py:323
  26.2 0.7 copy-start.4
  26.9 25.2 %copy-start.5 = (s32[2]{0:T(128)S(1)}, s32[2]{0:T(128)}, u32[]{:S(2)}) copy-start(s32[2]{0:T(128)} %owner.3) | copy-start | bytes 28
  27.6 5.7 %collective-permute-start.8 = (f32[2,192,128]{2,1,0:T(8,128)S(1)}, f32[2,192,128]{2,1,0:T(8,128)S(1)}, u32[]{:S(2)}, u32[]{:S(2)}) collective-permute-start(f32[2,192,128]{2,1,0:T(8,128)S(1)} %pick.1.refs_0_), channel_id=1, source_target_pairs={{8,0},{16,8},{24,16},{28,24},{20,28},{12,20},{4,12},{0,4},{9,1},{1... | collective-permute-start | bytes 589832 | tf_op jit(solution)/shard_map/ppermute | solution.py:390
  28.0 6.3 %collective-permute-start.7 = (f32[2,192,128]{2,1,0:T(8,128)S(1)}, f32[2,192,128]{2,1,0:T(8,128)S(1)}, u32[]{:S(2)}, u32[]{:S(2)}) collective-permute-start(f32[2,192,128]{2,1,0:T(8,128)S(1)} %pick.1.refs_0_), channel_id=1, source_target_pairs={{0,8},{8,16},{16,24},{24,28},{28,20},{20,12},{12,4},{4,0},{1,9},{9... | collective-permute-start | bytes 589832 | tf_op jit(solution)/shard_map/ppermute | solution.py:389
  33.3 5.7 %collective-permute-start.10 = (f32[2,192,128]{2,1,0:T(8,128)S(1)}, f32[2,192,128]{2,1,0:T(8,128)S(1)}, u32[]{:S(2)}, u32[]{:S(2)}) collective-permute-start(f32[2,192,128]{2,1,0:T(8,128)S(1)} %collective-permute-done.8.refs_2_), channel_id=1, source_target_pairs={{8,0},{16,8},{24,16},{28,24},{20,28},{12,20},{4,12},{0,4},{9,1},{1... | collective-permute-start | bytes 589832 | tf_op jit(solution)/shard_map/ppermute | solution.py:390
  34.3 6.3 %collective-permute-start.9 = (f32[2,192,128]{2,1,0:T(8,128)S(1)}, f32[2,192,128]{2,1,0:T(8,128)S(1)}, u32[]{:S(2)}, u32[]{:S(2)}) collective-permute-start(f32[2,192,128]{2,1,0:T(8,128)S(1)} %collective-permute-done.7.refs_1_), channel_id=1, source_target_pairs={{0,8},{8,16},{16,24},{24,28},{28,20},{20,12},{12,4},{4,0},{1,9},{9... | collective-permute-start | bytes 589832 | tf_op jit(solution)/shard_map/ppermute | solution.py:389
  39.0 6.4 %collective-permute-start.12 = (f32[2,192,128]{2,1,0:T(8,128)S(1)}, f32[2,192,128]{2,1,0:T(8,128)S(1)}, u32[]{:S(2)}, u32[]{:S(2)}) collective-permute-start(f32[2,192,128]{2,1,0:T(8,128)S(1)} %collective-permute-done.10.refs_4_), channel_id=1, source_target_pairs={{8,0},{16,8},{24,16},{28,24},{20,28},{12,20},{4,12},{0,4},{9,1},{1... | collective-permute-start | bytes 589832 | tf_op jit(solution)/shard_map/ppermute | solution.py:390
  40.6 6.7 %collective-permute-start.11 = (f32[2,192,128]{2,1,0:T(8,128)S(1)}, f32[2,192,128]{2,1,0:T(8,128)S(1)}, u32[]{:S(2)}, u32[]{:S(2)}) collective-permute-start(f32[2,192,128]{2,1,0:T(8,128)S(1)} %collective-permute-done.9.refs_3_), channel_id=1, source_target_pairs={{0,8},{8,16},{16,24},{24,28},{28,20},{20,12},{12,4},{4,0},{1,9},{9... | collective-permute-start | bytes 589832 | tf_op jit(solution)/shard_map/ppermute | solution.py:389
  45.4 5.3 %collective-permute-start.14 = (f32[2,96,128]{2,1,0:T(8,128)S(1)}, f32[2,96,128]{2,1,0:T(8,128)S(1)}, u32[]{:S(2)}, u32[]{:S(2)}) collective-permute-start(f32[2,96,128]{2,1,0:T(8,128)S(1)} %slice.61), channel_id=1, source_target_pairs={{8,0},{16,8},{24,16},{28,24},{20,28},{12,20},{4,12},{0,4},{9,1},{1... | collective-permute-start | bytes 294920 | tf_op jit(solution)/shard_map/ppermute | solution.py:390
  47.4 4.7 %collective-permute-start.13 = (f32[2,96,128]{2,1,0:T(8,128)S(1)}, f32[2,96,128]{2,1,0:T(8,128)S(1)}, u32[]{:S(2)}, u32[]{:S(2)}) collective-permute-start(f32[2,96,128]{2,1,0:T(8,128)S(1)} %slice.60), channel_id=1, source_target_pairs={{0,8},{8,16},{16,24},{24,28},{28,20},{20,12},{12,4},{4,0},{1,9},{9... | collective-permute-start | bytes 294920 | tf_op jit(solution)/shard_map/ppermute | solution.py:389
  49.0 6.4 %collective-permute-start.17 = (f32[3,96,128]{2,1,0:T(8,128)S(1)}, f32[3,96,128]{2,1,0:T(8,128)S(1)}, u32[]{:S(2)}, u32[]{:S(2)}) collective-permute-start(f32[3,96,128]{2,1,0:T(8,128)S(1)} %get-tuple-element.42), channel_id=1, source_target_pairs={{0,1},{1,2},{2,3},{3,0},{4,5},{5,6},{6,7},{7,4},{8,9},{9,10},{10,1... | collective-permute-start | bytes 442376 | tf_op jit(solution)/shard_map/ppermute | solution.py:359
  49.0 6.3 %collective-permute-start.18 = (f32[3,96,128]{2,1,0:T(8,128)S(1)}, f32[3,96,128]{2,1,0:T(8,128)S(1)}, u32[]{:S(2)}, u32[]{:S(2)}) collective-permute-start(f32[3,96,128]{2,1,0:T(8,128)S(1)} %get-tuple-element.43), channel_id=1, source_target_pairs={{1,0},{2,1},{3,2},{0,3},{5,4},{6,5},{7,6},{4,7},{9,8},{10,9},{11,1... | collective-permute-start | bytes 442376 | tf_op jit(solution)/shard_map/ppermute | solution.py:360
  53.6 6.9 %collective-permute-start.15 = (f32[2,96,128]{2,1,0:T(8,128)S(1)}, f32[2,96,128]{2,1,0:T(8,128)S(1)}, u32[]{:S(2)}, u32[]{:S(2)}) collective-permute-start(f32[2,96,128]{2,1,0:T(8,128)S(1)} %get-tuple-element.40), channel_id=1, source_target_pairs={{0,1},{1,2},{2,3},{3,0},{4,5},{5,6},{6,7},{7,4},{8,9},{9,10},{10,1... | collective-permute-start | bytes 294920 | tf_op jit(solution)/shard_map/ppermute | solution.py:402
  53.6 6.8 %copy-start.2 = (bf16[2,768,256]{2,1,0:T(8,128)(2,1)S(1)}, bf16[2,768,256]{2,1,0:T(8,128)(2,1)}, u32[]{:S(2)}) copy-start(bf16[2,768,256]{2,1,0:T(8,128)(2,1)} %constant.4.clone.bands) | copy-start | bytes 2359300
  53.6 6.8 %copy-start.3 = (bf16[256,128]{1,0:T(8,128)(2,1)S(1)}, bf16[256,128]{1,0:T(8,128)(2,1)}, u32[]{:S(2)}) copy-start(bf16[256,128]{1,0:T(8,128)(2,1)} %constant.5.clone.halo_bands) | copy-start | bytes 196612
  53.6 6.8 %collective-permute-start.16 = (f32[2,96,128]{2,1,0:T(8,128)S(1)}, f32[2,96,128]{2,1,0:T(8,128)S(1)}, u32[]{:S(2)}, u32[]{:S(2)}) collective-permute-start(f32[2,96,128]{2,1,0:T(8,128)S(1)} %get-tuple-element.41), channel_id=1, source_target_pairs={{1,0},{2,1},{3,2},{0,3},{5,4},{6,5},{7,6},{4,7},{9,8},{10,9},{11,1... | collective-permute-start | bytes 294920 | tf_op jit(solution)/shard_map/ppermute | solution.py:403

commit v7 on v6

--- a/solution.py
+++ b/solution.py
@@ -316,10 +316,12 @@
         return [got[s : s + 1] for s in range(n)]
     got = {0: pieces[:1]}
     reach = 1 << (n - 1).bit_length() - 1
-    for group in ([k for k in range(reach, n)], [k for k in range(1, reach)]):
+    far = range(reach, n)
+    close = sorted(range(1, reach), key=lambda k: (-k.bit_length(), k & 1, k))
+    for group in ([k for k in far if k % 2 == 0], [k for k in far if k % 2], close):
         sent = [pieces[k : k + 1] for k in group]
         pieces, *sent = lax.optimization_barrier([pieces, *sent])
-        for k, piece in sorted(zip(group, sent), key=lambda pair: (-pair[0].bit_length(), pair[0] & 1, pair[0])):
+        for k, piece in zip(group, sent):
             got[k] = lax.ppermute(piece, "cols", [(i, i ^ k) for i in range(n)])
     return [got[k] for k in range(n)]
 

time: 73.1 us -> 72.3 us (0.989)
  the two profiles are of different devices: /device:TPU:0 before, /device:TPU:25 now
where the time goes in v7:
time: 72.3 us; the launch traced here: 72.1 us
  waiting for transfers between devices  23.8 us (33%)
  starting transfers between devices  23.4 us (32%)
  Pallas kernels  21 us (29%)
  local copies, waits for them, and re-layouts  3.81 us (5%)
    pallas_call x1, Pallas kernels, body(): pl.pallas_call(functools.partial(main_kernel, rounds), out_shape=[f32(col...  12.5 us
    ppermute x4, waiting for transfers between devices, body(): behind = lax.ppermute(behind, 'cols', counter)  11.2 us
    ppermute x7, waiting for transfers between devices, exchange(): got[k] = lax.ppermute(piece, 'cols', [(i, i ^ k) for i in range(n)])  11 us
    ppermute x7, starting transfers between devices, exchange(): got[k] = lax.ppermute(piece, 'cols', [(i, i ^ k) for i in range(n)])  10.3 us
    ppermute x4, starting transfers between devices, body(): ahead = lax.ppermute(ahead, 'cols', clockwise)  6.1 us
    ppermute x1, starting transfers between devices, body(): left = lax.ppermute(last, 'sec', sec_up)  5.05 us
    slice x3, local copies, waits for them, and re-layouts, exchange(): sent = [pieces[k:k + 1] for k in group]  3.12 us
    pallas_call x1, Pallas kernels, body(): pl.pallas_call(prepare_kernel, out_shape=[f32(ny // 2, nz, nx), f32(ny, n...  2.96 us
  transfers between devices with their start and end apart: 19, of which 8 were waited for; matrix products, arithmetic and copies ran while one was open for 3% of the time, Pallas kernels for 11%

profile of v7, /device:TPU:25, one launch (start us, length us, event | category | flops | bytes accessed | tf_op | source)
XLA Modules:
  0.0 72.1 jit_solution(10364675888170818289)
XLA Ops:
  0.0 0.0 copy-start
  0.0 0.0 copy-start.1
  0.0 1.2 %fusion.2 = (f32[1,2,96,128]{3,2,1,0:T(8,128)S(1)}, f32[1,2,96,128]{3,2,1,0:T(8,128)S(1)}, f32[1,2,96,128]{3,2,1,0:T(8,128)S(1)}) fusion(f32[1,16,96,128]{3,2,1,0:T(8,128)} %param.7), kind=kLoop, calls=%fused_computation.2 | loop fusion | bytes 589824 | tf_op jit(solution)/shard_map/slice | solution.py:322
  1.2 0.1 collective-permute-start.3
  1.3 2.2 %collective-permute-start.5 = (f32[1,192,128]{2,1,0:T(8,128)S(1)}, f32[1,192,128]{2,1,0:T(8,128)S(1)}, u32[]{:S(2)}, u32[]{:S(2)}) collective-permute-start(f32[1,192,128]{2,1,0:T(8,128)S(1)} %bitcast.10), channel_id=1, source_target_pairs={{0,24},{4,28},{8,16},{12,20},{16,8},{20,12},{24,0},{28,4},{1,25},{... | collective-permute-start | bytes 294920 | tf_op jit(solution)/shard_map/ppermute | solution.py:325
  3.5 1.0 %fusion.1 = (f32[1,192,128]{2,1,0:T(8,128)S(1)}, f32[1,192,128]{2,1,0:T(8,128)S(1)}) fusion(f32[8,192,128]{2,1,0:T(8,128)} %bitcast.8), kind=kLoop, calls=%fused_computation.1 | loop fusion | bytes 393216 | tf_op jit(solution)/shard_map/slice | solution.py:322
  4.4 1.1 %collective-permute-start.4 = (f32[1,192,128]{2,1,0:T(8,128)S(1)}, f32[1,192,128]{2,1,0:T(8,128)S(1)}, u32[]{:S(2)}, u32[]{:S(2)}) collective-permute-start(f32[1,192,128]{2,1,0:T(8,128)S(1)} %get-tuple-element.38), channel_id=1, source_target_pairs={{0,20},{4,16},{8,28},{12,24},{16,4},{20,0},{24,12},{28,8},{1,21},{... | collective-permute-start | bytes 294920 | tf_op jit(solution)/shard_map/ppermute | solution.py:325
  5.5 2.3 %collective-permute-start.6 = (f32[1,192,128]{2,1,0:T(8,128)S(1)}, f32[1,192,128]{2,1,0:T(8,128)S(1)}, u32[]{:S(2)}, u32[]{:S(2)}) collective-permute-start(f32[1,192,128]{2,1,0:T(8,128)S(1)} %get-tuple-element.40), channel_id=1, source_target_pairs={{0,28},{4,24},{8,20},{12,16},{16,12},{20,8},{24,4},{28,0},{1,29},{... | collective-permute-start | bytes 294920 | tf_op jit(solution)/shard_map/ppermute | solution.py:325
  7.9 1.0 %fusion = (f32[1,192,128]{2,1,0:T(8,128)S(1)}, f32[1,192,128]{2,1,0:T(8,128)S(1)}, f32[1,192,128]{2,1,0:T(8,128)S(1)}) fusion(f32[8,192,128]{2,1,0:T(8,128)} %bitcast.9), kind=kLoop, calls=%fused_computation | loop fusion | bytes 589824 | tf_op jit(solution)/shard_map/slice | solution.py:322
  8.9 1.3 %collective-permute-start = (f32[1,192,128]{2,1,0:T(8,128)S(1)}, f32[1,192,128]{2,1,0:T(8,128)S(1)}, u32[]{:S(2)}, u32[]{:S(2)}) collective-permute-start(f32[1,192,128]{2,1,0:T(8,128)S(1)} %get-tuple-element.34), channel_id=1, source_target_pairs={{0,4},{4,0},{8,12},{12,8},{16,20},{20,16},{24,28},{28,24},{1,5},{5... | collective-permute-start | bytes 294920 | tf_op jit(solution)/shard_map/ppermute | solution.py:325
  10.2 5.0 %collective-permute-done.3.refs_4_ = f32[1,192,128]{2,1,0:T(8,128)S(1)} collective-permute-done((f32[1,192,128]{2,1,0:T(8,128)S(1)}, f32[1,192,128]{2,1,0:T(8,128)S(1)}, u32[]{:S(2)}, u32[]{:S(2)}) %collective-permute-start.3) | collective-permute-done | bytes 98336 | tf_op jit(solution)/shard_map/ppermute | solution.py:325
  15.2 0.0 collective-permute-start.1
  15.2 0.0 collective-permute-done.5.refs_6_
  15.2 3.3 %collective-permute-start.2 = (f32[1,192,128]{2,1,0:T(8,128)S(1)}, f32[1,192,128]{2,1,0:T(8,128)S(1)}, u32[]{:S(2)}, u32[]{:S(2)}) collective-permute-start(f32[1,192,128]{2,1,0:T(8,128)S(1)} %get-tuple-element.36), channel_id=1, source_target_pairs={{0,12},{4,8},{8,4},{12,0},{16,28},{20,24},{24,20},{28,16},{1,13},{... | collective-permute-start | bytes 294920 | tf_op jit(solution)/shard_map/ppermute | solution.py:325
  18.5 1.8 %collective-permute-done.4.refs_5_ = f32[1,192,128]{2,1,0:T(8,128)S(1)} collective-permute-done((f32[1,192,128]{2,1,0:T(8,128)S(1)}, f32[1,192,128]{2,1,0:T(8,128)S(1)}, u32[]{:S(2)}, u32[]{:S(2)}) %collective-permute-start.4) | collective-permute-done | bytes 98336 | tf_op jit(solution)/shard_map/ppermute | solution.py:325
  20.3 0.0 collective-permute-done.6.refs_7_
  20.3 0.0 collective-permute-done.refs_1_
  20.3 1.2 %collective-permute-done.1.refs_2_ = f32[1,192,128]{2,1,0:T(8,128)S(1)} collective-permute-done((f32[1,192,128]{2,1,0:T(8,128)S(1)}, f32[1,192,128]{2,1,0:T(8,128)S(1)}, u32[]{:S(2)}, u32[]{:S(2)}) %collective-permute-start.1) | collective-permute-done | bytes 98336 | tf_op jit(solution)/shard_map/ppermute | solution.py:325
  21.5 3.0 %collective-permute-done.2.refs_3_ = f32[1,192,128]{2,1,0:T(8,128)S(1)} collective-permute-done((f32[1,192,128]{2,1,0:T(8,128)S(1)}, f32[1,192,128]{2,1,0:T(8,128)S(1)}, u32[]{:S(2)}, u32[]{:S(2)}) %collective-permute-start.2) | collective-permute-done | bytes 98336 | tf_op jit(solution)/shard_map/ppermute | solution.py:325
  24.5 0.0 copy-start.4
  24.5 0.7 copy-done.4
  25.2 0.0 copy-start.5
  25.2 0.7 pick.1.refs_0_
  25.9 0.1 collective-permute-start.8
  25.9 1.5 %collective-permute-start.7 = (f32[2,192,128]{2,1,0:T(8,128)S(1)}, f32[2,192,128]{2,1,0:T(8,128)S(1)}, u32[]{:S(2)}, u32[]{:S(2)}) collective-permute-start(f32[2,192,128]{2,1,0:T(8,128)S(1)} %pick.1.refs_0_), channel_id=1, source_target_pairs={{0,8},{8,16},{16,24},{24,28},{28,20},{20,12},{12,4},{4,0},{1,9},{9... | collective-permute-start | bytes 589832 | tf_op jit(solution)/shard_map/ppermute | solution.py:391
  27.4 4.5 %collective-permute-done.8.refs_2_ = f32[2,192,128]{2,1,0:T(8,128)S(1)} collective-permute-done((f32[2,192,128]{2,1,0:T(8,128)S(1)}, f32[2,192,128]{2,1,0:T(8,128)S(1)}, u32[]{:S(2)}, u32[]{:S(2)}) %collective-permute-start.8) | collective-permute-done | bytes 196640 | tf_op jit(solution)/shard_map/ppermute | solution.py:392
  31.9 0.0 collective-permute-start.10
  31.9 0.0 collective-permute-done.7.refs_1_
  31.9 1.5 %collective-permute-start.9 = (f32[2,192,128]{2,1,0:T(8,128)S(1)}, f32[2,192,128]{2,1,0:T(8,128)S(1)}, u32[]{:S(2)}, u32[]{:S(2)}) collective-permute-start(f32[2,192,128]{2,1,0:T(8,128)S(1)} %collective-permute-done.7.refs_1_), channel_id=1, source_target_pairs={{0,8},{8,16},{16,24},{24,28},{28,20},{20,12},{12,4},{4,0},{1,9},{9... | collective-permute-start | bytes 589832 | tf_op jit(solution)/shard_map/ppermute | solution.py:391
  33.4 3.6 %collective-permute-done.10.refs_4_ = f32[2,192,128]{2,1,0:T(8,128)S(1)} collective-permute-done((f32[2,192,128]{2,1,0:T(8,128)S(1)}, f32[2,192,128]{2,1,0:T(8,128)S(1)}, u32[]{:S(2)}, u32[]{:S(2)}) %collective-permute-start.10) | collective-permute-done | bytes 196640 | tf_op jit(solution)/shard_map/ppermute | solution.py:392
  37.0 0.0 collective-permute-start.12
  37.0 0.0 collective-permute-done.9.refs_3_
  37.0 1.5 %collective-permute-start.11 = (f32[2,192,128]{2,1,0:T(8,128)S(1)}, f32[2,192,128]{2,1,0:T(8,128)S(1)}, u32[]{:S(2)}, u32[]{:S(2)}) collective-permute-start(f32[2,192,128]{2,1,0:T(8,128)S(1)} %collective-permute-done.9.refs_3_), channel_id=1, source_target_pairs={{0,8},{8,16},{16,24},{24,28},{28,20},{20,12},{12,4},{4,0},{1,9},{9... | collective-permute-start | bytes 589832 | tf_op jit(solution)/shard_map/ppermute | solution.py:391
  38.5 3.0 %collective-permute-done.12.refs_6_ = f32[2,192,128]{2,1,0:T(8,128)S(1)} collective-permute-done((f32[2,192,128]{2,1,0:T(8,128)S(1)}, f32[2,192,128]{2,1,0:T(8,128)S(1)}, u32[]{:S(2)}, u32[]{:S(2)}) %collective-permute-start.12) | collective-permute-done | bytes 196640 | tf_op jit(solution)/shard_map/ppermute | solution.py:392
  41.5 0.1 collective-permute-start.14
  41.6 0.0 collective-permute-done.11.refs_5_
  41.6 1.7 %collective-permute-start.13 = (f32[2,96,128]{2,1,0:T(8,128)S(1)}, f32[2,96,128]{2,1,0:T(8,128)S(1)}, u32[]{:S(2)}, u32[]{:S(2)}) collective-permute-start(f32[2,96,128]{2,1,0:T(8,128)S(1)} %slice.52), channel_id=1, source_target_pairs={{0,8},{8,16},{16,24},{24,28},{28,20},{20,12},{12,4},{4,0},{1,9},{9... | collective-permute-start | bytes 294920 | tf_op jit(solution)/shard_map/ppermute | solution.py:391
  43.3 0.0 copy-done
  43.3 0.0 copy-done.1
  43.4 1.2 %shard_map.64 = (f32[3,96,128]{2,1,0:T(8,128)S(1)}, f32[3,96,128]{2,1,0:T(8,128)S(1)}) custom-call(f32[2,16,96,128]{3,2,1,0:T(8,128)S(1)} %copy-done, f32[16,96,128]{2,1,0:T(8,128)S(1)} %copy-done.1), custom_call_target="tpu_custom_call" | custom-call | bytes 6291456 | tf_op jit(solution)/shard_map/pallas_call | solution.py:353
  44.6 5.0 %collective-permute-start.17 = (f32[3,96,128]{2,1,0:T(8,128)S(1)}, f32[3,96,128]{2,1,0:T(8,128)S(1)}, u32[]{:S(2)}, u32[]{:S(2)}) collective-permute-start(f32[3,96,128]{2,1,0:T(8,128)S(1)} %get-tuple-element.44), channel_id=1, source_target_pairs={{0,1},{1,2},{2,3},{3,0},{4,5},{5,6},{6,7},{7,4},{8,9},{9,10},{10,1... | collective-permute-start | bytes 442376 | tf_op jit(solution)/shard_map/ppermute | solution.py:361
  49.6 0.0 collective-permute-start.18
  49.7 0.0 collective-permute-done.14.refs_8_
  49.7 0.0 collective-permute-done.13.refs_7_
  49.7 0.0 copy-done.5
  49.7 1.5 %gather.1 = (f32[2,1536,128]{2,1,0:T(8,128)S(1)}, f32[2,96,128]{2,1,0:T(8,128)S(1)}, f32[2,96,128]{2,1,0:T(8,128)S(1)}) custom-call(s32[2]{0:T(128)S(1)} %copy-done.5, f32[2,192,128]{2,1,0:T(8,128)S(1)} %pick.1.refs_0_, f32[2,192,128]{2,1,0:T(8,128)S(1)} %collective-permute-done.7.refs_1_, f32[2,192,128]{2,1,0:T(8,128)S(1)} %collective-permute-done.8.refs_2_, ...), custom_call_target="tpu_custom_call" | custom-call | tf_op jit(solution)/shard_map/gather/pallas_call | solution.py:395
  51.2 1.8 %collective-permute-start.15 = (f32[2,96,128]{2,1,0:T(8,128)S(1)}, f32[2,96,128]{2,1,0:T(8,128)S(1)}, u32[]{:S(2)}, u32[]{:S(2)}) collective-permute-start(f32[2,96,128]{2,1,0:T(8,128)S(1)} %get-tuple-element.42), channel_id=1, source_target_pairs={{0,1},{1,2},{2,3},{3,0},{4,5},{5,6},{6,7},{7,4},{8,9},{9,10},{10,1... | collective-permute-start | bytes 294920 | tf_op jit(solution)/shard_map/ppermute | solution.py:404
  53.0 0.0 copy-start.2
  53.0 0.0 copy-start.3
  53.0 0.0 collective-permute-start.16
  53.0 0.0 collective-permute-done.17.left
  53.0 1.6 %collective-permute-done.18.right = f32[3,96,128]{2,1,0:T(8,128)S(1)} collective-permute-done((f32[3,96,128]{2,1,0:T(8,128)S(1)}, f32[3,96,128]{2,1,0:T(8,128)S(1)}, u32[]{:S(2)}, u32[]{:S(2)}) %collective-permute-start.18) | collective-permute-done | bytes 147488 | tf_op jit(solution)/shard_map/ppermute | solution.py:362
  54.6 3.0 %shard_map.65 = (f32[8,96,128]{2,1,0:T(8,128)S(1)}, f32[16,96,128]{2,1,0:T(8,128)S(1)}, f32[8,96,128]{2,1,0:T(8,128)S(1)}) custom-call(f32[2,16,96,128]{3,2,1,0:T(8,128)S(1)} %copy-done, f32[16,96,128]{2,1,0:T(8,128)S(1)} %copy-done.1, f32[3,96,128]{2,1,0:T(8,128)S(1)} %collective-permute-done.17.left, f32[3,96,128]{2,1,0:T(8,128)S(1)} %collective-permute-done.18.right), custom_call_target="tpu_custom_call" | custom-call | bytes 10485760 | tf_op jit(solution)/shard_map/pallas_call | solution.py:363
  57.5 2.1 %shard_map.66 = (f32[2,8,96,128]{3,2,1,0:T(8,128)S(1)}, f32[2,20,112,128]{3,2,1,0:T(8,128)S(1)}, f32[2,20,112,128]{3,2,1,0:T(8,128)S(1)}, f32[2,20,112,128]{3,2,...) custom-call(f32[2,16,96,128]{3,2,1,0:T(8,128)S(1)} %bitcast.5, ...), custom_call_target="tpu_custom_call" | custom-call | bytes 8388608 | tf_op jit(solution)/shard_map/pallas_call | solution.py:408
  59.6 0.0 collective-permute-done.15.left
  59.7 0.0 collective-permute-done.16.right
  59.7 0.0 copy-done.2
  59.7 0.0 copy-done.3
  59.7 12.5 %main.1 = (f32[2,16,96,128]{3,2,1,0:T(8,128)}, f32[2,20,112,128]{3,2,1,0:T(8,128)S(1)}, f32[2,20,112,128]{3,2,1,0:T(8,128)S(1)}, bf16[1536,768]{1,0:T(8,128)(2,1...) custom-call(f32[2,16,96,128]{3,2,1,0:T(8,128)S(1)} %bitcast.6, ...), custom_call_target="tpu_custom_call", output_to_operand_aliasing={{1}: (10, {}), {2}: (11, {}), {3}: (12, {}), {4}: (14, {}),... | custom-call | tf_op jit(solution)/shard_map/main/pallas_call | solution.py:418
  (2 shorter events, 0.0 us)
Async XLA Ops:
  0.0 43.3 %copy-start = (f32[2,16,96,128]{3,2,1,0:T(8,128)S(1)}, f32[2,16,96,128]{3,2,1,0:T(8,128)}, u32[]{:S(2)}) copy-start(f32[2,16,96,128]{3,2,1,0:T(8,128)} %trial.5) | copy-start | bytes 4718596
  0.0 43.3 %copy-start.1 = (f32[16,96,128]{2,1,0:T(8,128)S(1)}, f32[16,96,128]{2,1,0:T(8,128)}, u32[]{:S(2)}) copy-start(f32[16,96,128]{2,1,0:T(8,128)} %potential.3) | copy-start | bytes 2359300
  1.2 14.0 %collective-permute-start.3 = (f32[1,192,128]{2,1,0:T(8,128)S(1)}, f32[1,192,128]{2,1,0:T(8,128)S(1)}, u32[]{:S(2)}, u32[]{:S(2)}) collective-permute-start(f32[1,192,128]{2,1,0:T(8,128)S(1)} %bitcast.11), channel_id=1, source_target_pairs={{0,16},{4,20},{8,24},{12,28},{16,0},{20,4},{24,8},{28,12},{1,17},{... | collective-permute-start | bytes 294920 | tf_op jit(solution)/shard_map/ppermute | solution.py:325
  1.3 13.9 %collective-permute-start.5 = (f32[1,192,128]{2,1,0:T(8,128)S(1)}, f32[1,192,128]{2,1,0:T(8,128)S(1)}, u32[]{:S(2)}, u32[]{:S(2)}) collective-permute-start(f32[1,192,128]{2,1,0:T(8,128)S(1)} %bitcast.10), channel_id=1, source_target_pairs={{0,24},{4,28},{8,16},{12,20},{16,8},{20,12},{24,0},{28,4},{1,25},{... | collective-permute-start | bytes 294920 | tf_op jit(solution)/shard_map/ppermute | solution.py:325
  4.4 15.9 %collective-permute-start.4 = (f32[1,192,128]{2,1,0:T(8,128)S(1)}, f32[1,192,128]{2,1,0:T(8,128)S(1)}, u32[]{:S(2)}, u32[]{:S(2)}) collective-permute-start(f32[1,192,128]{2,1,0:T(8,128)S(1)} %get-tuple-element.38), channel_id=1, source_target_pairs={{0,20},{4,16},{8,28},{12,24},{16,4},{20,0},{24,12},{28,8},{1,21},{... | collective-permute-start | bytes 294920 | tf_op jit(solution)/shard_map/ppermute | solution.py:325
  5.5 14.8 %collective-permute-start.6 = (f32[1,192,128]{2,1,0:T(8,128)S(1)}, f32[1,192,128]{2,1,0:T(8,128)S(1)}, u32[]{:S(2)}, u32[]{:S(2)}) collective-permute-start(f32[1,192,128]{2,1,0:T(8,128)S(1)} %get-tuple-element.40), channel_id=1, source_target_pairs={{0,28},{4,24},{8,20},{12,16},{16,12},{20,8},{24,4},{28,0},{1,29},{... | collective-permute-start | bytes 294920 | tf_op jit(solution)/shard_map/ppermute | solution.py:325
  8.9 11.4 %collective-permute-start = (f32[1,192,128]{2,1,0:T(8,128)S(1)}, f32[1,192,128]{2,1,0:T(8,128)S(1)}, u32[]{:S(2)}, u32[]{:S(2)}) collective-permute-start(f32[1,192,128]{2,1,0:T(8,128)S(1)} %get-tuple-element.34), channel_id=1, source_target_pairs={{0,4},{4,0},{8,12},{12,8},{16,20},{20,16},{24,28},{28,24},{1,5},{5... | collective-permute-start | bytes 294920 | tf_op jit(solution)/shard_map/ppermute | solution.py:325
  15.2 6.3 %collective-permute-start.1 = (f32[1,192,128]{2,1,0:T(8,128)S(1)}, f32[1,192,128]{2,1,0:T(8,128)S(1)}, u32[]{:S(2)}, u32[]{:S(2)}) collective-permute-start(f32[1,192,128]{2,1,0:T(8,128)S(1)} %get-tuple-element.35), channel_id=1, source_target_pairs={{0,8},{4,12},{8,0},{12,4},{16,24},{20,28},{24,16},{28,20},{1,9},{5... | collective-permute-start | bytes 294920 | tf_op jit(solution)/shard_map/ppermute | solution.py:325
  15.2 9.3 %collective-permute-start.2 = (f32[1,192,128]{2,1,0:T(8,128)S(1)}, f32[1,192,128]{2,1,0:T(8,128)S(1)}, u32[]{:S(2)}, u32[]{:S(2)}) collective-permute-start(f32[1,192,128]{2,1,0:T(8,128)S(1)} %get-tuple-element.36), channel_id=1, source_target_pairs={{0,12},{4,8},{8,4},{12,0},{16,28},{20,24},{24,20},{28,16},{1,13},{... | collective-permute-start | bytes 294920 | tf_op jit(solution)/shard_map/ppermute | solution.py:325
  24.5 0.7 copy-start.4
  25.2 24.5 %copy-start.5 = (s32[2]{0:T(128)S(1)}, s32[2]{0:T(128)}, u32[]{:S(2)}) copy-start(s32[2]{0:T(128)} %owner.3) | copy-start | bytes 28
  25.9 6.0 %collective-permute-start.8 = (f32[2,192,128]{2,1,0:T(8,128)S(1)}, f32[2,192,128]{2,1,0:T(8,128)S(1)}, u32[]{:S(2)}, u32[]{:S(2)}) collective-permute-start(f32[2,192,128]{2,1,0:T(8,128)S(1)} %pick.1.refs_0_), channel_id=1, source_target_pairs={{8,0},{16,8},{24,16},{28,24},{20,28},{12,20},{4,12},{0,4},{9,1},{1... | collective-permute-start | bytes 589832 | tf_op jit(solution)/shard_map/ppermute | solution.py:392
  25.9 6.0 %collective-permute-start.7 = (f32[2,192,128]{2,1,0:T(8,128)S(1)}, f32[2,192,128]{2,1,0:T(8,128)S(1)}, u32[]{:S(2)}, u32[]{:S(2)}) collective-permute-start(f32[2,192,128]{2,1,0:T(8,128)S(1)} %pick.1.refs_0_), channel_id=1, source_target_pairs={{0,8},{8,16},{16,24},{24,28},{28,20},{20,12},{12,4},{4,0},{1,9},{9... | collective-permute-start | bytes 589832 | tf_op jit(solution)/shard_map/ppermute | solution.py:391
  31.9 5.1 %collective-permute-start.10 = (f32[2,192,128]{2,1,0:T(8,128)S(1)}, f32[2,192,128]{2,1,0:T(8,128)S(1)}, u32[]{:S(2)}, u32[]{:S(2)}) collective-permute-start(f32[2,192,128]{2,1,0:T(8,128)S(1)} %collective-permute-done.8.refs_2_), channel_id=1, source_target_pairs={{8,0},{16,8},{24,16},{28,24},{20,28},{12,20},{4,12},{0,4},{9,1},{1... | collective-permute-start | bytes 589832 | tf_op jit(solution)/shard_map/ppermute | solution.py:392
  31.9 5.1 %collective-permute-start.9 = (f32[2,192,128]{2,1,0:T(8,128)S(1)}, f32[2,192,128]{2,1,0:T(8,128)S(1)}, u32[]{:S(2)}, u32[]{:S(2)}) collective-permute-start(f32[2,192,128]{2,1,0:T(8,128)S(1)} %collective-permute-done.7.refs_1_), channel_id=1, source_target_pairs={{0,8},{8,16},{16,24},{24,28},{28,20},{20,12},{12,4},{4,0},{1,9},{9... | collective-permute-start | bytes 589832 | tf_op jit(solution)/shard_map/ppermute | solution.py:391
  37.0 4.5 %collective-permute-start.12 = (f32[2,192,128]{2,1,0:T(8,128)S(1)}, f32[2,192,128]{2,1,0:T(8,128)S(1)}, u32[]{:S(2)}, u32[]{:S(2)}) collective-permute-start(f32[2,192,128]{2,1,0:T(8,128)S(1)} %collective-permute-done.10.refs_4_), channel_id=1, source_target_pairs={{8,0},{16,8},{24,16},{28,24},{20,28},{12,20},{4,12},{0,4},{9,1},{1... | collective-permute-start | bytes 589832 | tf_op jit(solution)/shard_map/ppermute | solution.py:392
  37.0 4.6 %collective-permute-start.11 = (f32[2,192,128]{2,1,0:T(8,128)S(1)}, f32[2,192,128]{2,1,0:T(8,128)S(1)}, u32[]{:S(2)}, u32[]{:S(2)}) collective-permute-start(f32[2,192,128]{2,1,0:T(8,128)S(1)} %collective-permute-done.9.refs_3_), channel_id=1, source_target_pairs={{0,8},{8,16},{16,24},{24,28},{28,20},{20,12},{12,4},{4,0},{1,9},{9... | collective-permute-start | bytes 589832 | tf_op jit(solution)/shard_map/ppermute | solution.py:391
  41.5 8.1 %collective-permute-start.14 = (f32[2,96,128]{2,1,0:T(8,128)S(1)}, f32[2,96,128]{2,1,0:T(8,128)S(1)}, u32[]{:S(2)}, u32[]{:S(2)}) collective-permute-start(f32[2,96,128]{2,1,0:T(8,128)S(1)} %slice.53), channel_id=1, source_target_pairs={{8,0},{16,8},{24,16},{28,24},{20,28},{12,20},{4,12},{0,4},{9,1},{1... | collective-permute-start | bytes 294920 | tf_op jit(solution)/shard_map/ppermute | solution.py:392
  41.6 8.0 %collective-permute-start.13 = (f32[2,96,128]{2,1,0:T(8,128)S(1)}, f32[2,96,128]{2,1,0:T(8,128)S(1)}, u32[]{:S(2)}, u32[]{:S(2)}) collective-permute-start(f32[2,96,128]{2,1,0:T(8,128)S(1)} %slice.52), channel_id=1, source_target_pairs={{0,8},{8,16},{16,24},{24,28},{28,20},{20,12},{12,4},{4,0},{1,9},{9... | collective-permute-start | bytes 294920 | tf_op jit(solution)/shard_map/ppermute | solution.py:391
  44.6 8.4 %collective-permute-start.17 = (f32[3,96,128]{2,1,0:T(8,128)S(1)}, f32[3,96,128]{2,1,0:T(8,128)S(1)}, u32[]{:S(2)}, u32[]{:S(2)}) collective-permute-start(f32[3,96,128]{2,1,0:T(8,128)S(1)} %get-tuple-element.44), channel_id=1, source_target_pairs={{0,1},{1,2},{2,3},{3,0},{4,5},{5,6},{6,7},{7,4},{8,9},{9,10},{10,1... | collective-permute-start | bytes 442376 | tf_op jit(solution)/shard_map/ppermute | solution.py:361
  49.6 4.9 %collective-permute-start.18 = (f32[3,96,128]{2,1,0:T(8,128)S(1)}, f32[3,96,128]{2,1,0:T(8,128)S(1)}, u32[]{:S(2)}, u32[]{:S(2)}) collective-permute-start(f32[3,96,128]{2,1,0:T(8,128)S(1)} %get-tuple-element.45), channel_id=1, source_target_pairs={{1,0},{2,1},{3,2},{0,3},{5,4},{6,5},{7,6},{4,7},{9,8},{10,9},{11,1... | collective-permute-start | bytes 442376 | tf_op jit(solution)/shard_map/ppermute | solution.py:362
  51.2 8.4 %collective-permute-start.15 = (f32[2,96,128]{2,1,0:T(8,128)S(1)}, f32[2,96,128]{2,1,0:T(8,128)S(1)}, u32[]{:S(2)}, u32[]{:S(2)}) collective-permute-start(f32[2,96,128]{2,1,0:T(8,128)S(1)} %get-tuple-element.42), channel_id=1, source_target_pairs={{0,1},{1,2},{2,3},{3,0},{4,5},{5,6},{6,7},{7,4},{8,9},{9,10},{10,1... | collective-permute-start | bytes 294920 | tf_op jit(solution)/shard_map/ppermute | solution.py:404
  53.0 6.7 %copy-start.2 = (bf16[2,768,256]{2,1,0:T(8,128)(2,1)S(1)}, bf16[2,768,256]{2,1,0:T(8,128)(2,1)}, u32[]{:S(2)}) copy-start(bf16[2,768,256]{2,1,0:T(8,128)(2,1)} %constant.4.clone.bands) | copy-start | bytes 2359300
  53.0 6.7 %copy-start.3 = (bf16[256,128]{1,0:T(8,128)(2,1)S(1)}, bf16[256,128]{1,0:T(8,128)(2,1)}, u32[]{:S(2)}) copy-start(bf16[256,128]{1,0:T(8,128)(2,1)} %constant.5.clone.halo_bands) | copy-start | bytes 196612
  53.0 6.7 %collective-permute-start.16 = (f32[2,96,128]{2,1,0:T(8,128)S(1)}, f32[2,96,128]{2,1,0:T(8,128)S(1)}, u32[]{:S(2)}, u32[]{:S(2)}) collective-permute-start(f32[2,96,128]{2,1,0:T(8,128)S(1)} %get-tuple-element.43), channel_id=1, source_target_pairs={{1,0},{2,1},{3,2},{0,3},{5,4},{6,5},{7,6},{4,7},{9,8},{10,9},{11,1... | collective-permute-start | bytes 294920 | tf_op jit(solution)/shard_map/ppermute | solution.py:405
